TPU v7x, 32 devices: a whole 2x2x4 slice. The times are simulated.
32 devices in a mesh: row: 4 (over z), ta: 4 (over y, x), pa: 2 (over core).
Axes of the slice: x: 2, y: 2, z: 4, core: 2. Of those that a mesh axis runs over, the one named last changes fastest.
Arguments:
- density: float32 [16, 256, 512], P('row', 'ta', 'pa'), may hold values from 0.5 to 1.5
- kappa: float32 [16, 256, 512], P('row', 'ta', 'pa'), may hold values from 0.02 to 0.12
Outputs:
- updated: float32 [16, 256, 512], P('row', 'ta', 'pa')
- potential: float32 [16, 256, 512], P('row', 'ta', 'pa')
All inputs are finite; a program needn't handle non-finite values.
Results may differ from a plain program's by a relative error of at most 0.0049.
Values sent between devices are 32-bit elements; how exact they have to be, the bound alone decides.
No kernel may reach another device: no remote copies, remote signals or barrier semaphores. Data moves between devices by JAX's collectives and lax.ppermute only.
A program may use at most 64 MiB of HBM per device.

v0:
```python
import math

import jax
import jax.numpy as jnp
from jax import lax
from jax.sharding import PartitionSpec as P

DEGREES = 128


HIGH = lax.Precision.HIGHEST


def carried_in(value, axis, join, neutral, backward):
    count, mine = (lax.axis_size(axis), lax.axis_index(axis))
    pieces = jax.tree.map(lambda part: lax.all_gather(part, axis), value)
    if backward:
        pieces = jax.tree.map(lambda part: part[::-1], pieces)
        mine = count - 1 - mine
    running = jax.tree.map(
        lambda part, zero: jnp.full_like(part, 0) + jnp.asarray(zero, part.dtype), value, neutral
    )

    def turn(position, running):
        longer = join(running, jax.tree.map(lambda part: part[position], pieces))
        return jax.tree.map(lambda new, old: jnp.where(position < mine, new, old), longer, running)

    return lax.fori_loop(0, count - 1, turn, running)


def padded_2(cells, sides, width):
    for axis, dim in sides:
        count = lax.axis_size(axis)
        ends = count - 1
        head = lax.slice_in_dim(cells, 0, width, axis=dim)
        tail = lax.slice_in_dim(cells, cells.shape[dim] - width, cells.shape[dim], axis=dim)
        cells = jnp.concatenate(
            [
                lax.ppermute(tail, axis, [(i, (i + 1) % count) for i in range(ends)]),
                cells,
                lax.ppermute(head, axis, [((i + 1) % count, i) for i in range(ends)]),
            ],
            axis=dim,
        )
    return cells


def partner(value, axis, bit):
    return lax.ppermute(value, axis, [(i, i ^ 1 << bit) for i in range(lax.axis_size(axis))])


def legendre_table(theta, degrees):
    cos_t = jnp.cos(theta)[:, None]
    sin_t = jnp.sin(theta)[:, None]
    order = jnp.arange(degrees).astype(jnp.float32)[None, :]
    first = jnp.where(order == 0.0, 1.0, 0.0) * jnp.ones_like(theta)[:, None]

    def advance(carry, degree):
        prev, older = carry
        lval = degree.astype(jnp.float32)
        below = order < lval
        denom = jnp.where(below, lval * lval - order * order, 1.0)
        coef_a = jnp.sqrt((4.0 * lval * lval - 1.0) / denom)
        lower = lval - 1.0
        numer_b = jnp.maximum(lower * lower - order * order, 0.0)
        coef_b = jnp.sqrt(numer_b / jnp.maximum(4.0 * lower * lower - 1.0, 1.0))
        general = coef_a * (cos_t * prev - coef_b * older)
        shifted = jnp.concatenate([jnp.zeros_like(prev[:, :1]), prev[:, :-1]], axis=1)
        sect_factor = jnp.where(
            order == 1.0,
            jnp.sqrt(3.0),
            jnp.sqrt((2.0 * order + 1.0) / jnp.maximum(2.0 * order, 1.0)),
        )
        sectoral = sect_factor * sin_t * shifted
        fresh = jnp.where(below, general, jnp.where(order == lval, sectoral, 0.0))
        return ((fresh, prev), fresh)

    _, rest = lax.scan(advance, (first, jnp.zeros_like(first)), jnp.arange(1, degrees))
    return jnp.concatenate([first[None], rest], axis=0)


def forward_join(earlier, later):
    return (earlier[0] * later[0], earlier[1] * later[0][:, None, None] + later[1])


def backward_join(earlier, later):
    return (earlier[0] * later[0], later[1] + later[0][:, None, None] * earlier[1])


def radial_solve(moments, degree, radii, log_step):
    rows = moments.shape[0]
    local = jnp.arange(rows).astype(jnp.float32)
    spacing = local[:, None] - local[None, :]
    inward_weight = jnp.where(
        spacing[:, :, None] >= 0.0,
        jnp.exp(-log_step * jnp.maximum(spacing, 0.0)[:, :, None] * degree[None, None, :]),
        0.0,
    )
    outward_weight = jnp.where(
        spacing[:, :, None] < 0.0,
        jnp.exp(-log_step * jnp.maximum(-spacing, 0.0)[:, :, None] * (degree[None, None, :] + 1.0)),
        0.0,
    )
    inner_local = jnp.einsum("ijl,jlcm->ilcm", inward_weight, moments, precision=HIGH)
    outer_local = jnp.einsum("ijl,jlcm->ilcm", outward_weight, moments, precision=HIGH)
    fwd_value = inner_local[-1]
    fwd_mult = jnp.exp(-log_step * rows * degree)
    bwd_weight = jnp.exp(-log_step * (local[:, None] + 1.0) * (degree[None, :] + 1.0))
    bwd_value = jnp.einsum("jl,jlcm->lcm", bwd_weight, moments, precision=HIGH)
    bwd_mult = jnp.exp(-log_step * rows * (degree + 1.0))
    ident = (jnp.ones_like(fwd_mult), jnp.zeros_like(fwd_value))
    _, carry_in = carried_in((fwd_mult, fwd_value), "row", forward_join, ident, False)
    _, carry_out = carried_in((bwd_mult, bwd_value), "row", backward_join, ident, True)
    lift_in = jnp.exp(-log_step * (local[:, None] + 1.0) * degree[None, :])
    lift_out = jnp.exp(-log_step * (rows - 1.0 - local)[:, None] * (degree[None, :] + 1.0))
    inner = inner_local + lift_in[:, :, None, None] * carry_in[None]
    outer = outer_local + lift_out[:, :, None, None] * carry_out[None]
    scale = 4.0 * math.pi * (2.0 * degree[None, :] + 1.0) * radii[:, None]
    result = -(inner + outer) / scale[:, :, None, None]
    return jnp.where(degree[None, :, None, None] > 0.0, result, 0.0)


def shards(density, kappa):
    rows, polar, azim = density.shape
    row_count = lax.axis_size("row")
    ta_count = lax.axis_size("ta")
    row_index = lax.axis_index("row")
    ta_index = lax.axis_index("ta")
    pa_index = lax.axis_index("pa")
    radial_total = rows * row_count
    polar_total = polar * ta_count
    azim_total = azim * lax.axis_size("pa")
    padded = padded_2(density, (("row", 0), ("ta", 1)), 1)
    caps = jnp.stack([density[:, 0, :], density[:, -1, :]], axis=1)
    sides = jnp.stack([density[:, :, 0], density[:, :, -1]], axis=2)
    far_caps, far_sides = partner((caps, sides), "pa", 0)
    inner_ghost = jnp.where(row_index == 0, density[:1], padded[:1, 1:-1])
    outer_ghost = jnp.where(row_index == row_count - 1, density[-1:], padded[-1:, 1:-1])
    north = jnp.where(ta_index == 0, far_caps[:, 0:1], padded[1:-1, :1])
    south = jnp.where(ta_index == ta_count - 1, far_caps[:, 1:2], padded[1:-1, -1:])
    radial_up = jnp.concatenate([density[1:], outer_ghost], 0)
    radial_down = jnp.concatenate([inner_ghost, density[:-1]], 0)
    polar_up = jnp.concatenate([north, density[:, :-1]], 1)
    polar_down = jnp.concatenate([density[:, 1:], south], 1)
    west = jnp.concatenate([far_sides[:, :, 1:2], density[:, :, :-1]], 2)
    east = jnp.concatenate([density[:, :, 1:], far_sides[:, :, 0:1]], 2)
    lap = radial_up + radial_down + polar_up + polar_down + west + east - 6.0 * density
    updated = density + kappa * lap
    log_eight = math.log(8.0)
    shells = (row_index * rows + jnp.arange(rows)).astype(jnp.float32)
    edges_low = jnp.exp(log_eight * (shells / radial_total - 1.0))
    edges_high = jnp.exp(log_eight * ((shells + 1.0) / radial_total - 1.0))
    volume = (edges_high**3 - edges_low**3) / 3.0
    radii = jnp.exp(log_eight * ((shells + 0.5) / radial_total - 1.0))
    log_step = log_eight / radial_total
    rows_index = (ta_index * polar + jnp.arange(polar)).astype(jnp.float32)
    theta = (rows_index + 0.5) * (math.pi / polar_total)
    band = jnp.cos(rows_index * (math.pi / polar_total)) - jnp.cos(
        (rows_index + 1.0) * (math.pi / polar_total)
    )
    phi = ((pa_index * azim + jnp.arange(azim)).astype(jnp.float32) + 0.5) * (
        2.0 * math.pi / azim_total
    )
    modes = jnp.arange(DEGREES).astype(jnp.float32)
    waves = jnp.concatenate(
        [jnp.cos(phi[:, None] * modes[None, :]), jnp.sin(phi[:, None] * modes[None, :])], axis=1
    )
    weight = updated * volume[:, None, None] * band[None, :, None] * (2.0 * math.pi / azim_total)
    fourier = jnp.dot(weight.reshape(rows * polar, azim), waves, precision=HIGH).reshape(
        rows, polar, 2, DEGREES
    )
    legendre = legendre_table(theta, DEGREES)
    moments = jnp.einsum("rtcm,ltm->rlcm", fourier, legendre, precision=HIGH)
    share = lax.psum_scatter(moments, ("ta", "pa"), scatter_dimension=1, tiled=True)
    block = share.shape[1]
    degree = (lax.axis_index(("ta", "pa")) * block + jnp.arange(block)).astype(jnp.float32)
    part_coeffs = radial_solve(share, degree, radii, log_step)
    coeffs = lax.all_gather(part_coeffs, ("ta", "pa"), axis=1, tiled=True)
    spectral = jnp.einsum("rlcm,ltm->rtcm", coeffs, legendre, precision=HIGH)
    potential = jnp.dot(
        spectral.reshape(rows * polar, 2 * DEGREES), waves.T, precision=HIGH
    ).reshape(rows, polar, azim)
    return (updated, potential)


def solution(mesh):
    placed = (P("row", "ta", "pa"), P("row", "ta", "pa"))
    return jax.shard_map(
        shards,
        mesh=mesh,
        in_specs=placed,
        out_specs=(P("row", "ta", "pa"), P("row", "ta", "pa")),
        check_vma=False,
    )
```

profile of v0, /device:TPU:0, one launch (start us, length us, event | category | flops | bytes accessed | tf_op | source)
XLA Modules:
  0.0 424.1 jit_solution(475359154359853759)
XLA Ops:
  8.1 5.0 %collective-permute-start.1 = (f32[1,64,256]{2,1,0:T(8,128)S(1)}, f32[1,64,256]{2,1,0:T(8,128)S(1)}, u32[]{:S(2)}, u32[]{:S(2)}) collective-permute-start(f32[1,64,256]{2,1,0:T(8,128)S(1)} %get-tuple-element.506), channel_id=1, source_target_pairs={{0,8},{8,16},{16,24},{1,9},{9,17},{17,25},{2,10},{10,18},{18,26},{... | collective-permute-start | bytes 196616 | tf_op jit(solution)/shard_map/ppermute | solution.py:39
  13.1 1.3 collective-permute-start
  15.2 1.1 fusion.87
  17.1 1.2 fusion.86
  18.2 1.1 fusion.88
  21.5 262.3 %while.50 = (s32[]{:T(128)}, f32[64,128]{1,0:T(8,128)S(1)}, f32[64,128]{1,0:T(8,128)S(1)}, f32[127,64,128]{2,1,0:T(8,128)}, s32[127]{0:T(128)S(1)}, /*index=5*/s...) while((s32[]{:T(128)}, f32[64,128]{1,0:T(8,128)S(1)}, ...), condition=%wide.region_1.2_spmd.clone.clone.clone, body=%wide.region_0.1_spmd.clone.clone.clone.sunk | while | flops 68365 | bytes 300045 | solution.py:78
  283.8 5.6 %copy.17 = f32[127,64,128]{0,1,2:T(8,128)} copy(f32[127,64,128]{2,1,0:T(8,128)} %get-tuple-element.334) | data formatting | bytes 8323072 | tf_op jit(solution)/shard_map/while | solution.py:78
  289.6 3.4 collective-permute-start.3
  293.0 1.3 collective-permute-start.4
  294.6 3.9 collective-permute-done.4
  299.8 2.1 copy-done.1
  301.9 1.2 copy-done
  303.2 4.3 %fusion.26 = f32[4,128,2,128]{1,0,2,3:T(4,128)S(1)} fusion(f32[4,64,2,128]{1,0,2,3:T(4,128)S(1)} %copy.19, f32[127,64,128]{0,1,2:T(8,128)S(1)} %copy-done, f32[1,64,128]{0,1,2:T(8,128)S(1)} %broadcast_in_dim.132), kind=kOutput, calls=%fused_computation.39 | convolution fusion | flops 101711872 | bytes 4980736 | tf_op jit(solution)/shard_map/rtcm,ltm->rlcm/dot_general | solution.py:173
  308.6 12.2 %all-gather.2 = f32[4,1,16]{2,1,0:T(1,128)S(1)} all-gather(f32[1,1,16]{2,1,0:T(1,128)S(1)} %exponential_bitcast_fusion), channel_id=1, replica_groups=mesh['row'=4,'ta'=4,'pa'=2] {'row'}, dimensions={0}, use_global_device_ids=true | all-gather | bytes 320 | tf_op jit(solution)/shard_map/all_gather | solution.py:16
  322.0 7.6 %all-gather.1 = f32[4,1,16]{2,1,0:T(1,128)S(1)} all-gather(f32[1,1,16]{2,1,0:T(1,128)S(1)} %exponential_bitcast_fusion.1), channel_id=1, replica_groups=mesh['row'=4,'ta'=4,'pa'=2] {'row'}, dimensions={0}, use_global_device_ids=true | all-gather | bytes 320 | tf_op jit(solution)/shard_map/all_gather | solution.py:16
  329.7 36.2 %all-reduce.4.cloned.1.call-done = f32[4,128,2,128]{3,0,2,1:T(4,128)} async-done(((f32[4,128,2,128]{3,0,2,1:T(4,128)}), f32[4,128,2,128]{3,0,2,1:T(4,128)}) %all-reduce.4.cloned.1.call-update) | async-done | bytes 524304
  365.9 1.1 fusion.51
  367.0 13.2 %all-gather = f32[64,2,128]{2,1,0:T(2,128)S(1)} all-gather(f32[16,2,128]{2,1,0:T(2,128)S(1)} %bitcast.134), channel_id=2, replica_groups=mesh['row'=4,'ta'=4,'pa'=2] {'row'}, dimensions={0}, use_global_device_ids=true | all-gather | bytes 81920 | tf_op jit(solution)/shard_map/all_gather | solution.py:16
  380.6 1.2 convolution_bitcast_fusion.1
  381.8 13.1 %all_gather.21 = f32[4,16,2,128]{3,1,2,0:T(8,128)S(1)} all-gather(f32[1,16,2,128]{3,1,2,0:T(8,128)S(1)} %copy.21), channel_id=1, replica_groups=mesh['row'=4,'ta'=4,'pa'=2] {'row'}, dimensions={0}, use_global_device_ids=true | all-gather | bytes 81920 | tf_op jit(solution)/shard_map/all_gather | solution.py:16
  395.4 1.2 fusion.32
  396.5 9.4 %all_gather.25 = f32[4,128,2,128]{3,0,2,1:T(4,128)S(1)} all-gather(f32[4,16,2,128]{3,0,2,1:T(4,128)S(1)} %fusion.32), channel_id=1, replica_groups=mesh['row'=4,'ta'=4,'pa'=2] {'ta','pa'}, dimensions={1}, use_global_device_ids=true | all-gather | bytes 589824 | tf_op jit(solution)/shard_map/all_gather | solution.py:178
  406.3 9.4 %fusion.27 = f32[4,64,2,128]{1,0,2,3:T(4,128)S(1)} fusion(f32[4,128,2,128]{1,0,2,3:T(4,128)S(1)} %copy.23, f32[127,64,128]{0,1,2:T(8,128)} %copy.17, f32[1,64,128]{0,1,2:T(8,128)} %copy-done.1), kind=kOutput, calls=%fused_computation.40 | convolution fusion | flops 101711872 | bytes 4980736 | tf_op jit(solution)/shard_map/rlcm,ltm->rtcm/dot_general | solution.py:179
  416.2 1.1 fusion.42
  (1107 shorter events, 191.1 us)
Async XLA Ops:
  7.2 358.7 %all-reduce.4.cloned.1.call-start = ((), (), s32[]{:S(2)}) async-start(), calls=%async_computation | async-start | bytes 1048576
  8.1 281.4 %collective-permute-start.1 = (f32[1,64,256]{2,1,0:T(8,128)S(1)}, f32[1,64,256]{2,1,0:T(8,128)S(1)}, u32[]{:S(2)}, u32[]{:S(2)}) collective-permute-start(f32[1,64,256]{2,1,0:T(8,128)S(1)} %get-tuple-element.506), channel_id=1, source_target_pairs={{0,8},{8,16},{16,24},{1,9},{9,17},{17,25},{2,10},{10,18},{18,26},{... | collective-permute-start | bytes 196616 | tf_op jit(solution)/shard_map/ppermute | solution.py:39
  13.1 276.5 %collective-permute-start = (f32[1,64,256]{2,1,0:T(8,128)S(1)}, f32[1,64,256]{2,1,0:T(8,128)S(1)}, u32[]{:S(2)}, u32[]{:S(2)}) collective-permute-start(f32[1,64,256]{2,1,0:T(8,128)S(1)} %get-tuple-element.507), channel_id=1, source_target_pairs={{8,0},{16,8},{24,16},{9,1},{17,9},{25,17},{10,2},{18,10},{26,18},{... | collective-permute-start | bytes 196616 | tf_op jit(solution)/shard_map/ppermute | solution.py:41
  15.2 279.4 %collective-permute-start.2 = (f32[4,2,256]{2,1,0:T(2,128)S(1)}, f32[4,2,256]{2,1,0:T(2,128)S(1)}, u32[]{:S(2)}, u32[]{:S(2)}) collective-permute-start(f32[4,2,256]{2,1,0:T(2,128)S(1)} %pad_maximum_fusion.2), channel_id=1, source_target_pairs={{0,1},{1,0},{2,3},{3,2},{4,5},{5,4},{6,7},{7,6},{8,9},{9,8},{10,11... | collective-permute-start | bytes 24584 | tf_op jit(solution)/shard_map/ppermute | solution.py:49
  16.5 277.8 %collective-permute-start.5 = (f32[4,64,2]{1,0,2:T(4,128)S(1)}, f32[4,64,2]{1,0,2:T(4,128)S(1)}, u32[]{:S(2)}, u32[]{:S(2)}) collective-permute-start(f32[4,64,2]{1,0,2:T(4,128)S(1)} %pad_maximum_fusion.3), channel_id=1, source_target_pairs={{0,1},{1,0},{2,3},{3,2},{4,5},{5,4},{6,7},{7,6},{8,9},{9,8},{10,11... | collective-permute-start | bytes 6152 | tf_op jit(solution)/shard_map/ppermute | solution.py:49
  283.8 5.7 %copy-start.2 = (f32[4,64,256]{2,1,0:T(8,128)S(1)}, f32[4,64,256]{2,1,0:T(8,128)}, u32[]{:S(2)}) copy-start(f32[4,64,256]{2,1,0:T(8,128)} %param.8) | copy-start | bytes 786436
  283.8 14.7 %copy-start.4 = (f32[4,64,256]{2,1,0:T(8,128)S(1)}, f32[4,64,256]{2,1,0:T(8,128)}, u32[]{:S(2)}) copy-start(f32[4,64,256]{2,1,0:T(8,128)} %param.9) | copy-start | bytes 786436
  289.6 5.0 %collective-permute-start.3 = (f32[6,1,256]{2,1,0:T(1,128)S(1)}, f32[6,1,256]{2,1,0:T(1,128)S(1)}, u32[]{:S(2)}, u32[]{:S(2)}) collective-permute-start(f32[6,1,256]{2,1,0:T(1,128)S(1)} %get-tuple-element.495), channel_id=1, source_target_pairs={{0,2},{2,4},{4,6},{1,3},{3,5},{5,7},{8,10},{10,12},{12,14},{9,11},... | collective-permute-start | bytes 18440 | tf_op jit(solution)/shard_map/ppermute | solution.py:39
  293.0 5.5 %collective-permute-start.4 = (f32[6,1,256]{2,1,0:T(1,128)S(1)}, f32[6,1,256]{2,1,0:T(1,128)S(1)}, u32[]{:S(2)}, u32[]{:S(2)}) collective-permute-start(f32[6,1,256]{2,1,0:T(1,128)S(1)} %get-tuple-element.494), channel_id=1, source_target_pairs={{2,0},{4,2},{6,4},{3,1},{5,3},{7,5},{10,8},{12,10},{14,12},{11,9},... | collective-permute-start | bytes 18440 | tf_op jit(solution)/shard_map/ppermute | solution.py:41
  298.7 8.8 %copy-start.3 = (f32[4,64,256]{2,1,0:T(8,128)}, f32[4,64,256]{2,1,0:T(8,128)S(1)}, u32[]{:S(2)}) copy-start(f32[4,64,256]{2,1,0:T(8,128)S(1)} %fusion.39) | copy-start | bytes 786436
  299.5 3.7 copy-start
  299.8 2.1 copy-start.1
  303.2 17.7 %copy-start.5 = (u32[32]{0:T(128)S(1)}, u32[32]{0:T(128)}, u32[]{:S(2)}) copy-start(u32[32]{0:T(128)} %constant.183) | copy-start | bytes 388
Sparse Core Ops, SparseCore 0:
  308.7 57.0 all-reduce.3
where the time goes:
time: 426 us; the launch traced here: 424 us
  other arithmetic  104 us (24%)
  local copies, waits for them, and re-layouts  97.4 us (23%)
  loops' own time  81.7 us (19%)
  blocking collectives  55.6 us (13%)
  waiting for transfers between devices  40.1 us (9%)
  matrix products  18.7 us (4%)
  between operations  15.1 us (4%)
  starting transfers between devices  11.6 us (3%)
    dynamic_update_slice x127, other arithmetic, legendre_table(): lax.scan(advance, (first, jnp.zeros_like(first)), jnp.arange(1, degrees))  90.8 us
    another operation x1, loops' own time, legendre_table(): lax.scan(advance, (first, jnp.zeros_like(first)), jnp.arange(1, degrees))  81.6 us
    dynamic_slice x127, local copies, waits for them, and re-layouts, legendre_table(): lax.scan(advance, (first, jnp.zeros_like(first)), jnp.arange(1, degrees))  77.9 us
    all_gather x4, blocking collectives, carried_in(): pieces = jax.tree.map(lambda part: lax.all_gather(part, axis), value)  46.1 us
    unnamed x2, waiting for transfers between devices  36.2 us
    all_gather x1, blocking collectives, shards(): coeffs = lax.all_gather(part_coeffs, ('ta', 'pa'), axis=1, tiled=True)  9.44 us
    dot_general x1, matrix products, shards(): spectral = jnp.einsum('rlcm,ltm->rtcm', coeffs, legendre, precision=HIGH)  9.37 us
  transfers between devices with their start and end apart: 7, of which 2 were waited for; matrix products, arithmetic and copies ran while one was open for 46% of the time, Pallas kernels for 0%

commit v1 on v0

v1 whole, which is shorter than its diff:
```python
import functools
import math

import jax
import jax.numpy as jnp
import numpy as np
from jax import lax
from jax.experimental import pallas as pl
from jax.experimental.pallas import tpu as pltpu
from jax.sharding import PartitionSpec as P

DEGREES = 128
HIGH = lax.Precision.HIGHEST
AXES = ("row", "ta", "pa")
VMEM = pl.BlockSpec(memory_space=pltpu.VMEM)
SMEM = pl.BlockSpec(memory_space=pltpu.SMEM)


def wave_table(azim_total, parts, owners):
    modes = np.arange(DEGREES).reshape(owners, 1, -1, 1, 1)
    phi = (np.arange(azim_total) + 0.5) * (2.0 * math.pi / azim_total)
    angle = modes * phi.reshape(1, 1, 1, parts, -1)
    both = np.concatenate([np.cos(angle), np.sin(angle)], axis=1)
    rows = 2 * DEGREES
    return both.reshape(rows, parts, -1).transpose(1, 0, 2).astype(np.float32)


def recursion_table(owners):
    l = np.arange(DEGREES, dtype=np.float64)[None, :]
    m = np.arange(DEGREES, dtype=np.float64)[:, None]
    below = m < l
    a = np.sqrt((4 * l * l - 1) / np.where(below, l * l - m * m, 1.0) * below)
    low = l - 1
    b = np.sqrt(np.maximum(low * low - m * m, 0) / np.maximum(4 * low * low - 1, 1.0))
    sect = np.where(l == 1, math.sqrt(3.0), np.sqrt((2 * l + 1) / np.maximum(2 * l, 1.0)))
    first = np.stack([a, a * b]).astype(np.float32)
    per_owner = first.reshape(2, owners, -1).transpose(1, 0, 2)
    return per_owner, sect[0].astype(np.float32)


def legendre_kernel(own, sizes, coef_ref, sect_ref, cos_ref, sin_ref, out_ref):
    owner = own(sizes)
    per, degrees, polar = out_ref.shape
    cos_t = jnp.broadcast_to(cos_ref[...], (8, polar))
    sin_t = jnp.broadcast_to(sin_ref[...], (8, polar))
    sub = lax.broadcasted_iota(jnp.int32, (8, polar), 0)

    def block(step, carry):
        sect, prev, older = carry
        tiles = [jnp.zeros((8, polar), jnp.float32) for _ in range(per)]
        for inner in range(8):
            l = step * 8 + inner
            grown = sect * (sin_t * sect_ref[l])
            sect = jnp.where(l == 0, sect, grown)
            new_prev, new_older = [], []
            for q in range(per):
                a = coef_ref[owner, 0, q * degrees + l]
                b = coef_ref[owner, 1, q * degrees + l]
                fresh = (a * cos_t) * prev[q] - b * older[q]
                fresh = jnp.where(l == owner * per + q, sect, fresh)
                tiles[q] = jnp.where(sub == inner, fresh, tiles[q])
                new_prev.append(fresh)
                new_older.append(prev[q])
            prev, older = new_prev, new_older
        for q in range(per):
            out_ref[q, pl.ds(pl.multiple_of(step * 8, 8), 8), :] = tiles[q]
        return sect, prev, older

    zero = [jnp.zeros((8, polar), jnp.float32) for _ in range(per)]
    lax.fori_loop(0, degrees // 8, block, (jnp.ones((8, polar), jnp.float32), zero, zero))


def stencil_kernel(sizes, rho, kappa, far, below, above, north, south, waves, upd, spec):
    rows, polar, azim = rho.shape
    row, ta, pa = (lax.axis_index(a) for a in AXES)
    lane = lax.broadcasted_iota(jnp.int32, (polar, azim), 1)
    sub = lax.broadcasted_iota(jnp.int32, (polar, azim), 0)
    for r in range(rows):
        c = rho[r]
        p = far[r]
        if r == rows - 1:
            up = jnp.where(row == sizes[0] - 1, c, above[0])
        else:
            up = rho[r + 1]
        if r == 0:
            down = jnp.where(row == 0, c, below[0])
        else:
            down = rho[r - 1]
        first = jnp.where(ta == 0, p[0:1, :], north[r : r + 1, :])
        last = jnp.where(ta == sizes[1] - 1, p[polar - 1 : polar, :], south[r : r + 1, :])
        pol_up = jnp.where(sub == 0, first, pltpu.roll(c, 1, 0))
        pol_down = jnp.where(sub == polar - 1, last, pltpu.roll(c, polar - 1, 0))
        west = pltpu.roll(jnp.where(lane == azim - 1, p, c), 1, 1)
        east = pltpu.roll(jnp.where(lane == 0, p, c), azim - 1, 1)
        lap = up + down + pol_up + pol_down + west + east - 6.0 * c
        upd[r] = c + kappa[r] * lap
    cells = upd[...].reshape(rows * polar, azim)
    spec[...] = lax.dot_general(
        waves[pa], cells, (((1,), (1,)), ((), ())),
        precision=HIGH, preferred_element_type=jnp.float32,
    )


def solve_kernel(own, sizes, rows, polar, spec_ref, leg_ref, band_ref, out_ref, work_ref):
    per, degrees, polar_total = leg_ref.shape
    n_row, n_ta, n_pa = sizes
    shells = rows * n_row
    pair = 2 * per
    owner = own(sizes)
    band = band_ref[...]
    for g in range(n_row):
        parts = []
        for t in range(n_ta):
            base = (g * n_ta + t) * n_pa
            total = spec_ref[base]
            for h in range(1, n_pa):
                total = total + spec_ref[base + h]
            parts.append(total)
        for r in range(rows):
            piece = jnp.concatenate([x[:, r * polar : (r + 1) * polar] for x in parts], axis=1)
            work_ref[g * rows + r] = piece * band
    table = leg_ref[...].reshape(per * degrees, polar_total)
    wide = lax.dot_general(
        work_ref[...].reshape(shells * pair, polar_total), table, (((1,), (1,)), ((), ())),
        precision=HIGH, preferred_element_type=jnp.float32,
    )
    slot = lax.broadcasted_iota(jnp.int32, (shells * pair, degrees), 0) % per
    picked = wide[:, :degrees]
    for q in range(1, per):
        picked = jnp.where(slot == q, wide[:, q * degrees : (q + 1) * degrees], picked)
    log_eight = math.log(8.0)
    step = log_eight / shells
    degree = lax.broadcasted_iota(jnp.int32, (pair, degrees), 1).astype(jnp.float32)
    decay_in = jnp.exp(-step * degree)
    decay_out = jnp.exp(-step * (degree + 1.0))
    scale = jnp.where(degree > 0.0, -1.0 / (4.0 * math.pi * (2.0 * degree + 1.0)), 0.0)
    edges = np.exp(log_eight * (np.arange(shells + 1) / shells - 1.0))
    volume = (edges[1:] ** 3 - edges[:-1] ** 3) / 3.0
    radii = np.exp(log_eight * ((np.arange(shells) + 0.5) / shells - 1.0))
    moments = [picked[i * pair : (i + 1) * pair] * float(volume[i]) for i in range(shells)]
    sums = []
    carry = jnp.zeros((pair, degrees), jnp.float32)
    for i in range(shells):
        carry = carry * decay_in + moments[i]
        sums.append(carry)
    carry = jnp.zeros((pair, degrees), jnp.float32)
    for i in reversed(range(shells)):
        sums[i] = (sums[i] + carry) * (scale * float(1.0 / radii[i]))
        carry = (carry + moments[i]) * decay_out
    coeffs = jnp.concatenate(sums, axis=0)
    spread = jnp.concatenate([jnp.where(slot == q, coeffs, 0.0) for q in range(per)], axis=1)
    field = jnp.dot(spread, table, precision=HIGH, preferred_element_type=jnp.float32)
    for g in range(n_row):
        for t in range(n_ta):
            pieces = [
                field[(g * rows + r) * pair : (g * rows + r + 1) * pair, t * polar : (t + 1) * polar]
                for r in range(rows)
            ]
            block = jnp.concatenate(pieces, axis=1)
            for h in range(n_pa):
                out_ref[(g * n_ta + t) * n_pa + h] = block


def potential_kernel(spec, waves, out):
    rows, polar, azim = out.shape
    pa = lax.axis_index("pa")
    flat = lax.dot_general(
        spec[...], waves[pa], (((0,), (0,)), ((), ())),
        precision=HIGH, preferred_element_type=jnp.float32,
    )
    out[...] = flat.reshape(rows, polar, azim)


def owner_of(sizes):
    row, ta, pa = (lax.axis_index(a) for a in AXES)
    return (row * sizes[1] + ta) * sizes[2] + pa


def shards(sizes, density, kappa):
    rows, polar, azim = density.shape
    n_row, n_ta, n_pa = sizes
    owners = n_row * n_ta * n_pa
    per = DEGREES // owners
    polar_total, azim_total = polar * n_ta, azim * n_pa
    f32 = jnp.float32

    ahead = lambda n: [(i, i + 1) for i in range(n - 1)]
    back = lambda n: [(i + 1, i) for i in range(n - 1)]
    below = lax.ppermute(density[-1:], "row", ahead(n_row))
    above = lax.ppermute(density[:1], "row", back(n_row))
    north = lax.ppermute(density[:, -1, :], "ta", ahead(n_ta))
    south = lax.ppermute(density[:, 0, :], "ta", back(n_ta))
    far = lax.ppermute(density, "pa", [(i, (i + n_pa // 2) % n_pa) for i in range(n_pa)])

    coef, sect = recursion_table(owners)
    edge = np.arange(polar_total + 1) * (math.pi / polar_total)
    theta = (np.arange(polar_total) + 0.5) * (math.pi / polar_total)
    band = (np.cos(edge[:-1]) - np.cos(edge[1:])) * (2.0 * math.pi / azim_total)
    row_of = lambda v: jnp.asarray(v.astype(np.float32)[None, :])
    legendre = pl.pallas_call(
        functools.partial(legendre_kernel, owner_of, sizes),
        out_shape=jax.ShapeDtypeStruct((per, DEGREES, polar_total), f32),
        in_specs=[SMEM, SMEM, VMEM, VMEM],
        out_specs=VMEM,
        cost_estimate=pl.CostEstimate(flops=10**7, bytes_accessed=10**6, transcendentals=0),
        name="legendre",
    )(jnp.asarray(coef), jnp.asarray(sect), row_of(np.cos(theta)), row_of(np.sin(theta)))

    waves = jnp.asarray(wave_table(azim_total, n_pa, owners))
    updated, spec = pl.pallas_call(
        functools.partial(stencil_kernel, sizes),
        out_shape=(
            jax.ShapeDtypeStruct(density.shape, f32),
            jax.ShapeDtypeStruct((2 * DEGREES, rows * polar), f32),
        ),
        in_specs=[VMEM] * 8,
        out_specs=(VMEM, VMEM),
        name="stencil",
    )(density, kappa, far, below, above, north, south, waves)

    spec = lax.all_to_all(
        spec.reshape(owners, 2 * per, rows * polar), AXES, split_axis=0, concat_axis=0, tiled=True
    )
    spec = pl.pallas_call(
        functools.partial(solve_kernel, owner_of, sizes, rows, polar),
        out_shape=jax.ShapeDtypeStruct(spec.shape, f32),
        in_specs=[VMEM] * 3,
        out_specs=VMEM,
        scratch_shapes=[pltpu.VMEM((rows * n_row, 2 * per, polar_total), f32)],
        name="solve",
    )(spec, legendre, row_of(band))
    spec = lax.all_to_all(spec, AXES, split_axis=0, concat_axis=0, tiled=True)

    potential = pl.pallas_call(
        potential_kernel,
        out_shape=jax.ShapeDtypeStruct(density.shape, f32),
        in_specs=[VMEM] * 2,
        out_specs=VMEM,
        name="potential",
    )(spec.reshape(2 * DEGREES, rows * polar), waves)
    return (updated, potential)


def solution(mesh):
    sizes = tuple(mesh.shape[a] for a in AXES)
    placed = (P(*AXES), P(*AXES))
    return jax.shard_map(
        functools.partial(shards, sizes), mesh=mesh, in_specs=placed, out_specs=placed, check_vma=False
    )
```

time: 426 us -> 58.6 us (0.14)
  other arithmetic: 104 us -> 0 us
  local copies, waits for them, and re-layouts: 97.4 us -> 3.69 us
  loops' own time: 81.7 us -> 0 us
  blocking collectives: 55.6 us -> 13.8 us
  waiting for transfers between devices: 40.1 us -> 9.09 us
  matrix products: 18.7 us -> 0 us
  between operations: 15.1 us -> 0.73 us
  Pallas kernels: 0 us -> 13.8 us
  starting transfers between devices: 11.6 us -> 16.9 us
    dynamic_update_slice x127 -> x0, other arithmetic: 90.8 us -> none  [legendre_table(): lax.scan(advance, (first, jnp.zeros_like(first)), jnp.arange(1, degrees))]
    another operation x3 -> x0, loops' own time: 81.7 us -> none  [the longest x1 81.6 us: legendre_table(): lax.scan(advance, (first, jnp.zeros_like(first)), jnp.arange(1, degrees))]
    dynamic_slice x130 -> x0, local copies, waits for them, and re-layouts: 77.9 us -> none  [the longest x127 77.9 us: legendre_table(): lax.scan(advance, (first, jnp.zeros_like(first)), jnp.arange(1, degrees))]
    all_gather x5 -> x0, blocking collectives: 55.6 us -> none  [the longest x4 46.1 us: carried_in(): pieces = jax.tree.map(lambda part: lax.all_gather(part, axis), value)]
    unnamed x2 -> x0, waiting for transfers between devices: 36.2 us -> none
    dot_general x7 -> x0, matrix products: 18.7 us -> none  [the longest x1 9.37 us: shards(): spectral = jnp.einsum('rlcm,ltm->rtcm', coeffs, legendre, precision=HIGH)]
    all_to_all x0 -> x1, blocking collectives: none -> 13.8 us  [shards(): spec = lax.all_to_all(spec, AXES, split_axis=0, concat_axis=0, tiled=True)]
    pallas_call x0 -> x4, Pallas kernels: none -> 13.8 us  [the longest x1 5.67 us: shards(): pl.pallas_call(functools.partial(legendre_kernel, owner_of, sizes), out_s...]
  transfers between devices with their start and end apart: 7 -> 6, of which waited for: 2 -> 2; matrix products, arithmetic and copies ran while one was open for 46% -> 3% of each run, Pallas kernels for 0% -> 10%
where the time goes in v1:
time: 58.6 us; the launch traced here: 58.1 us
  starting transfers between devices  16.9 us (29%)
  Pallas kernels  13.8 us (24%)
  blocking collectives  13.8 us (24%)
  waiting for transfers between devices  9.09 us (16%)
  local copies, waits for them, and re-layouts  3.69 us (6%)
  between operations  0.73 us (1%)
    all_to_all x1, blocking collectives, shards(): spec = lax.all_to_all(spec, AXES, split_axis=0, concat_axis=0, tiled=True)  13.8 us
    pallas_call x1, Pallas kernels, shards(): pl.pallas_call(functools.partial(legendre_kernel, owner_of, sizes), out_s...  5.67 us
    ppermute x1, starting transfers between devices, shards(): below = lax.ppermute(density[-1:], 'row', ahead(n_row))  5.11 us
    all_to_all x1, waiting for transfers between devices, shards(): lax.all_to_all(spec.reshape(owners, 2 * per, rows * polar), AXES, split_a...  4.9 us
    all_to_all x1, starting transfers between devices, shards(): lax.all_to_all(spec.reshape(owners, 2 * per, rows * polar), AXES, split_a...  4.78 us
    ppermute x1, waiting for transfers between devices, shards(): south = lax.ppermute(density[:, 0, :], 'ta', back(n_ta))  4.18 us
    ppermute x1, starting transfers between devices, shards(): north = lax.ppermute(density[:, -1, :], 'ta', ahead(n_ta))  3.83 us
    pallas_call x1, Pallas kernels, shards(): pl.pallas_call(functools.partial(solve_kernel, owner_of, sizes, rows, pol...  3.28 us
  transfers between devices with their start and end apart: 6, of which 2 were waited for; matrix products, arithmetic and copies ran while one was open for 3% of the time, Pallas kernels for 10%

profile of v1, /device:TPU:0, one launch (start us, length us, event | category | flops | bytes accessed | tf_op | source)
XLA Modules:
  0.0 58.1 jit_solution(9584211239563880235)
XLA Ops:
  0.6 0.6 collective-permute-start
  1.2 0.9 %fusion.1 = (f32[1,64,256]{2,1,0:T(8,128)S(1)}, f32[1,64,256]{2,1,0:T(8,128)S(1)}) fusion(f32[4,64,256]{2,1,0:T(8,128)} %rho.1), kind=kLoop, calls=%fused_computation.3 | loop fusion | bytes 262144 | tf_op jit(solution)/shard_map/slice | solution.py:190
  2.1 1.3 %collective-permute-start.2 = (f32[1,64,256]{2,1,0:T(8,128)S(1)}, f32[1,64,256]{2,1,0:T(8,128)S(1)}, u32[]{:S(2)}, u32[]{:S(2)}) collective-permute-start(f32[1,64,256]{2,1,0:T(8,128)S(1)} %get-tuple-element.8), channel_id=1, source_target_pairs={{8,0},{16,8},{24,16},{9,1},{17,9},{25,17},{10,2},{18,10},{26,18},{... | collective-permute-start | bytes 196616 | tf_op jit(solution)/shard_map/ppermute | solution.py:190
  3.4 5.1 %collective-permute-start.1 = (f32[1,64,256]{2,1,0:T(8,128)S(1)}, f32[1,64,256]{2,1,0:T(8,128)S(1)}, u32[]{:S(2)}, u32[]{:S(2)}) collective-permute-start(f32[1,64,256]{2,1,0:T(8,128)S(1)} %get-tuple-element.9), channel_id=1, source_target_pairs={{0,8},{8,16},{16,24},{1,9},{9,17},{17,25},{2,10},{10,18},{18,26},{... | collective-permute-start | bytes 196616 | tf_op jit(solution)/shard_map/ppermute | solution.py:189
  8.5 0.8 %fusion = (f32[4,1,256]{2,1,0:T(1,128)S(1)}, f32[4,1,256]{2,1,0:T(1,128)S(1)}) fusion(f32[4,64,256]{2,1,0:T(8,128)} %rho.1), kind=kLoop, calls=%fused_computation.2 | loop fusion | bytes 16384 | tf_op jit(solution)/shard_map/slice | solution.py:192
  9.3 3.8 %collective-permute-start.3 = (f32[4,256]{1,0:T(4,128)S(1)}, f32[4,256]{1,0:T(4,128)S(1)}, u32[]{:S(2)}, u32[]{:S(2)}) collective-permute-start(f32[4,256]{1,0:T(4,128)S(1)} %bitcast.10), channel_id=1, source_target_pairs={{0,2},{2,4},{4,6},{1,3},{3,5},{5,7},{8,10},{10,12},{12,14},{9,11},... | collective-permute-start | bytes 12296 | tf_op jit(solution)/shard_map/ppermute | solution.py:191
  13.1 1.3 %collective-permute-start.4 = (f32[4,256]{1,0:T(4,128)S(1)}, f32[4,256]{1,0:T(4,128)S(1)}, u32[]{:S(2)}, u32[]{:S(2)}) collective-permute-start(f32[4,256]{1,0:T(4,128)S(1)} %bitcast.11), channel_id=1, source_target_pairs={{2,0},{4,2},{6,4},{3,1},{5,3},{7,5},{10,8},{12,10},{14,12},{11,9},... | collective-permute-start | bytes 12296 | tf_op jit(solution)/shard_map/ppermute | solution.py:192
  14.4 0.0 collective-permute-done.3.north
  14.5 4.2 %collective-permute-done.4.south = f32[4,256]{1,0:T(4,128)S(1)} collective-permute-done((f32[4,256]{1,0:T(4,128)S(1)}, f32[4,256]{1,0:T(4,128)S(1)}, u32[]{:S(2)}, u32[]{:S(2)}) %collective-permute-start.4) | collective-permute-done | bytes 4128 | tf_op jit(solution)/shard_map/ppermute | solution.py:192
  18.6 0.0 collective-permute-done.2.above
  18.6 0.0 collective-permute-done.1.below
  18.7 0.0 collective-permute-done.far
  18.7 0.5 copy-done.5
  19.2 0.0 copy-done.2
  19.3 0.0 copy-done.3
  19.3 0.7 %copy-done.1 = f32[4,64,256]{2,1,0:T(8,128)} copy-done((f32[4,64,256]{2,1,0:T(8,128)}, f32[4,64,256]{2,1,0:T(8,128)S(1)}, u32[]{:S(2)}) %copy-start.1) | copy-done | bytes 262168
  20.0 2.6 %stencil.1 = (f32[4,64,256]{2,1,0:T(8,128)}, f32[256,256]{1,0:T(8,128)}) custom-call(f32[4,64,256]{2,1,0:T(8,128)} %rho.1, f32[4,64,256]{2,1,0:T(8,128)} %kappa.1, f32[4,64,256]{2,1,0:T(8,128)} %copy-done.1, f32[1,64,256]{2,1,0:T(8,128)} %copy-done.3, f32[1,64,256]{2,1,0:T(8,128)} %copy-done.2, f32[4,256]{1,0:T(4,128)} %copy-done.4, f32[4,256]{1,0:T(4,128)} %copy-done.5, ...), custom_call_target="tpu_custom_call" | custom-call | tf_op jit(solution)/shard_map/stencil/pallas_call | solution.py:210
  22.6 4.8 %all-to-all-start = ((f32[32,8,256]{2,1,0:T(8,128)}), f32[32,8,256]{2,1,0:T(8,128)S(1)}, u32[]{:S(2)}, u32[]{:S(2)}) async-start(f32[32,8,256]{2,1,0:T(8,128)} %bitcast.9), calls=%async_computation | async-start | bytes 524288 | tf_op jit(solution)/shard_map/all_to_all | solution.py:221
  27.4 5.7 %legendre.1.leg_ref = f32[4,128,256]{2,1,0:T(8,128)} custom-call(f32[32,2,512]{2,1,0:T(2,128)} %constant.12.clone.coef_ref, f32[128]{0:T(128)} %constant.13.clone.sect_ref, f32[1,256]{1,0:T(1,128)} %constant.14.clone.cos_ref, f32[1,256]{1,0:T(1,128)} %constant.15.clone.sin_ref), custom_call_target="tpu_custom_call" | custom-call | flops 10000000 | bytes 1000000 | tf_op jit(solution)/shard_map/legendre/pallas_call | solution.py:200
  33.1 4.9 %all-to-all-done.spec_ref = f32[32,8,256]{2,1,0:T(8,128)S(1)} async-done(((f32[32,8,256]{2,1,0:T(8,128)}), f32[32,8,256]{2,1,0:T(8,128)S(1)}, u32[]{:S(2)}, u32[]{:S(2)}) %all-to-all-start) | async-done | bytes 262176 | tf_op jit(solution)/shard_map/all_to_all | solution.py:221
  38.0 0.7 %copy-done = f32[32,8,256]{2,1,0:T(8,128)} copy-done((f32[32,8,256]{2,1,0:T(8,128)}, f32[32,8,256]{2,1,0:T(8,128)S(1)}, u32[]{:S(2)}) %copy-start) | copy-done | bytes 262168
  38.7 3.3 %solve.1 = f32[32,8,256]{2,1,0:T(8,128)} custom-call(f32[32,8,256]{2,1,0:T(8,128)} %copy-done, f32[4,128,256]{2,1,0:T(8,128)} %legendre.1.leg_ref, f32[1,256]{1,0:T(1,128)} %constant.17.clone.band_ref), custom_call_target="tpu_custom_call" | custom-call | tf_op jit(solution)/shard_map/solve/pallas_call | solution.py:224
  42.0 13.8 %all_to_all.10 = f32[32,8,256]{2,1,0:T(8,128)} all-to-all(f32[32,8,256]{2,1,0:T(8,128)} %solve.1), channel_id=1, replica_groups=mesh['row'=4,'ta'=4,'pa'=2] {'row','ta','pa'}, dimensions={0} | all-to-all | bytes 524288 | tf_op jit(solution)/shard_map/all_to_all | solution.py:232
  55.8 2.3 %potential.1 = f32[4,64,256]{2,1,0:T(8,128)} custom-call(f32[256,256]{1,0:T(8,128)} %bitcast.8, f32[2,256,256]{2,1,0:T(8,128)} %constant.16.clone.waves), custom_call_target="tpu_custom_call" | custom-call | tf_op jit(solution)/shard_map/potential/pallas_call | solution.py:234
  (9 shorter events, 0.0 us)
Async XLA Ops:
  0.6 18.0 %collective-permute-start = (f32[4,64,256]{2,1,0:T(8,128)}, f32[4,64,256]{2,1,0:T(8,128)S(1)}, u32[]{:S(2)}, u32[]{:S(2)}) collective-permute-start(f32[4,64,256]{2,1,0:T(8,128)} %rho.1), channel_id=1, source_target_pairs={{0,1},{1,0},{2,3},{3,2},{4,5},{5,4},{6,7},{7,6},{8,9},{9,8},{10,11... | collective-permute-start | bytes 786440 | tf_op jit(solution)/shard_map/ppermute | solution.py:193
  2.1 16.6 %collective-permute-start.2 = (f32[1,64,256]{2,1,0:T(8,128)S(1)}, f32[1,64,256]{2,1,0:T(8,128)S(1)}, u32[]{:S(2)}, u32[]{:S(2)}) collective-permute-start(f32[1,64,256]{2,1,0:T(8,128)S(1)} %get-tuple-element.8), channel_id=1, source_target_pairs={{8,0},{16,8},{24,16},{9,1},{17,9},{25,17},{10,2},{18,10},{26,18},{... | collective-permute-start | bytes 196616 | tf_op jit(solution)/shard_map/ppermute | solution.py:190
  3.4 15.3 %collective-permute-start.1 = (f32[1,64,256]{2,1,0:T(8,128)S(1)}, f32[1,64,256]{2,1,0:T(8,128)S(1)}, u32[]{:S(2)}, u32[]{:S(2)}) collective-permute-start(f32[1,64,256]{2,1,0:T(8,128)S(1)} %get-tuple-element.9), channel_id=1, source_target_pairs={{0,8},{8,16},{16,24},{1,9},{9,17},{17,25},{2,10},{10,18},{18,26},{... | collective-permute-start | bytes 196616 | tf_op jit(solution)/shard_map/ppermute | solution.py:189
  9.3 5.2 %collective-permute-start.3 = (f32[4,256]{1,0:T(4,128)S(1)}, f32[4,256]{1,0:T(4,128)S(1)}, u32[]{:S(2)}, u32[]{:S(2)}) collective-permute-start(f32[4,256]{1,0:T(4,128)S(1)} %bitcast.10), channel_id=1, source_target_pairs={{0,2},{2,4},{4,6},{1,3},{3,5},{5,7},{8,10},{10,12},{12,14},{9,11},... | collective-permute-start | bytes 12296 | tf_op jit(solution)/shard_map/ppermute | solution.py:191
  13.1 5.5 %collective-permute-start.4 = (f32[4,256]{1,0:T(4,128)S(1)}, f32[4,256]{1,0:T(4,128)S(1)}, u32[]{:S(2)}, u32[]{:S(2)}) collective-permute-start(f32[4,256]{1,0:T(4,128)S(1)} %bitcast.11), channel_id=1, source_target_pairs={{2,0},{4,2},{6,4},{3,1},{5,3},{7,5},{10,8},{12,10},{14,12},{11,9},... | collective-permute-start | bytes 12296 | tf_op jit(solution)/shard_map/ppermute | solution.py:192
  14.4 4.2 %copy-start.4 = (f32[4,256]{1,0:T(4,128)}, f32[4,256]{1,0:T(4,128)S(1)}, u32[]{:S(2)}) copy-start(f32[4,256]{1,0:T(4,128)S(1)} %collective-permute-done.3.north) | copy-start | bytes 12292
  18.6 0.6 %copy-start.5 = (f32[4,256]{1,0:T(4,128)}, f32[4,256]{1,0:T(4,128)S(1)}, u32[]{:S(2)}) copy-start(f32[4,256]{1,0:T(4,128)S(1)} %collective-permute-done.4.south) | copy-start | bytes 12292
  18.6 0.6 %copy-start.2 = (f32[1,64,256]{2,1,0:T(8,128)}, f32[1,64,256]{2,1,0:T(8,128)S(1)}, u32[]{:S(2)}) copy-start(f32[1,64,256]{2,1,0:T(8,128)S(1)} %collective-permute-done.2.above) | copy-start | bytes 196612
  18.6 0.6 %copy-start.3 = (f32[1,64,256]{2,1,0:T(8,128)}, f32[1,64,256]{2,1,0:T(8,128)S(1)}, u32[]{:S(2)}) copy-start(f32[1,64,256]{2,1,0:T(8,128)S(1)} %collective-permute-done.1.below) | copy-start | bytes 196612
  19.3 0.7 %copy-start.1 = (f32[4,64,256]{2,1,0:T(8,128)}, f32[4,64,256]{2,1,0:T(8,128)S(1)}, u32[]{:S(2)}) copy-start(f32[4,64,256]{2,1,0:T(8,128)S(1)} %collective-permute-done.far) | copy-start | bytes 786436
  22.6 15.4 %all-to-all-start = ((f32[32,8,256]{2,1,0:T(8,128)}), f32[32,8,256]{2,1,0:T(8,128)S(1)}, u32[]{:S(2)}, u32[]{:S(2)}) async-start(f32[32,8,256]{2,1,0:T(8,128)} %bitcast.9), calls=%async_computation | async-start | bytes 524288 | tf_op jit(solution)/shard_map/all_to_all | solution.py:221
  38.0 0.7 %copy-start = (f32[32,8,256]{2,1,0:T(8,128)}, f32[32,8,256]{2,1,0:T(8,128)S(1)}, u32[]{:S(2)}) copy-start(f32[32,8,256]{2,1,0:T(8,128)S(1)} %all-to-all-done.spec_ref) | copy-start | bytes 786436

commit v2 on v1

--- a/solution.py
+++ b/solution.py
@@ -14,15 +14,14 @@
 AXES = ("row", "ta", "pa")
 VMEM = pl.BlockSpec(memory_space=pltpu.VMEM)
 SMEM = pl.BlockSpec(memory_space=pltpu.SMEM)
-
-
-def wave_table(azim_total, parts, owners):
-    modes = np.arange(DEGREES).reshape(owners, 1, -1, 1, 1)
+PARAMS = pltpu.CompilerParams(vmem_limit_bytes=16 * 2**20)
+
+
+def wave_table(azim_total, owners):
+    modes = np.arange(DEGREES).reshape(owners, 1, -1, 1)
     phi = (np.arange(azim_total) + 0.5) * (2.0 * math.pi / azim_total)
-    angle = modes * phi.reshape(1, 1, 1, parts, -1)
-    both = np.concatenate([np.cos(angle), np.sin(angle)], axis=1)
-    rows = 2 * DEGREES
-    return both.reshape(rows, parts, -1).transpose(1, 0, 2).astype(np.float32)
+    both = np.concatenate([np.cos(modes * phi), np.sin(modes * phi)], axis=1)
+    return both.reshape(2 * DEGREES, azim_total).astype(np.float32)
 
 
 def recursion_table(owners):
@@ -70,33 +69,67 @@
     lax.fori_loop(0, degrees // 8, block, (jnp.ones((8, polar), jnp.float32), zero, zero))
 
 
-def stencil_kernel(sizes, rho, kappa, far, below, above, north, south, waves, upd, spec):
+def pair_swap(value, axes, count, first):
+    pairs = []
+    for i in range(first, count - 1, 2):
+        pairs += [(i, i + 1), (i + 1, i)]
+    return lax.ppermute(value, axes, pairs)
+
+
+def joined(pa, own, far):
+    return jnp.concatenate([jnp.where(pa == 0, own, far), jnp.where(pa == 0, far, own)], axis=1)
+
+
+def pack_kernel(rho, far, shell_out, even_out, odd_out):
     rows, polar, azim = rho.shape
+    half = rows // 2
+    ta, pa = lax.axis_index("ta"), lax.axis_index("pa")
+    edge = pa * (rows - 1)
+    shell_out[...] = joined(pa, rho[edge], far[edge])
+    even = ta % 2 == 0
+    for r in range(half):
+        own, other = rho.at[pa * half + r], far.at[pa * half + r]
+        top = joined(pa, own[0:1, :], other[0:1, :])
+        low = joined(pa, own[polar - 1 : polar, :], other[polar - 1 : polar, :])
+        even_out[r : r + 1, :] = jnp.where(even, low, top)
+        odd_out[r : r + 1, :] = jnp.where(even, top, low)
+
+
+def stencil_kernel(sizes, rho, far, kappa, far_kappa, shell, even_in, odd_in, waves, keep, send, spec, cells):
+    rows, polar, azim = rho.shape
+    half = rows // 2
     row, ta, pa = (lax.axis_index(a) for a in AXES)
-    lane = lax.broadcasted_iota(jnp.int32, (polar, azim), 1)
-    sub = lax.broadcasted_iota(jnp.int32, (polar, azim), 0)
-    for r in range(rows):
-        c = rho[r]
-        p = far[r]
-        if r == rows - 1:
-            up = jnp.where(row == sizes[0] - 1, c, above[0])
+    even = ta % 2 == 0
+    sub = lax.broadcasted_iota(jnp.int32, (polar, 2 * azim), 0)
+    at = lambda i: joined(pa, rho[i], far[i])
+    for r in range(half):
+        i = pa * half + r
+        c = at(i)
+        if r == 0:
+            ghost = jnp.where(row == 0, c, shell[...])
+            down = jnp.where(pa == 0, ghost, at(jnp.maximum(i - 1, 0)))
         else:
-            up = rho[r + 1]
-        if r == 0:
-            down = jnp.where(row == 0, c, below[0])
+            down = at(i - 1)
+        if r == half - 1:
+            ghost = jnp.where(row == sizes[0] - 1, c, shell[...])
+            up = jnp.where(pa == 0, at(jnp.minimum(i + 1, rows - 1)), ghost)
         else:
-            down = rho[r - 1]
-        first = jnp.where(ta == 0, p[0:1, :], north[r : r + 1, :])
-        last = jnp.where(ta == sizes[1] - 1, p[polar - 1 : polar, :], south[r : r + 1, :])
-        pol_up = jnp.where(sub == 0, first, pltpu.roll(c, 1, 0))
-        pol_down = jnp.where(sub == polar - 1, last, pltpu.roll(c, polar - 1, 0))
-        west = pltpu.roll(jnp.where(lane == azim - 1, p, c), 1, 1)
-        east = pltpu.roll(jnp.where(lane == 0, p, c), azim - 1, 1)
+            up = at(i + 1)
+        north = jnp.where(even, odd_in[r : r + 1, :], even_in[r : r + 1, :])
+        south = jnp.where(even, even_in[r : r + 1, :], odd_in[r : r + 1, :])
+        north = jnp.where(ta == 0, pltpu.roll(c[0:1, :], azim, 1), north)
+        south = jnp.where(ta == sizes[1] - 1, pltpu.roll(c[polar - 1 :, :], azim, 1), south)
+        pol_up = jnp.where(sub == 0, north, pltpu.roll(c, 1, 0))
+        pol_down = jnp.where(sub == polar - 1, south, pltpu.roll(c, polar - 1, 0))
+        west = pltpu.roll(c, 1, 1)
+        east = pltpu.roll(c, 2 * azim - 1, 1)
         lap = up + down + pol_up + pol_down + west + east - 6.0 * c
-        upd[r] = c + kappa[r] * lap
-    cells = upd[...].reshape(rows * polar, azim)
+        new = c + joined(pa, kappa[i], far_kappa[i]) * lap
+        keep[r] = jnp.where(pa == 0, new[:, :azim], new[:, azim:])
+        send[r] = jnp.where(pa == 0, new[:, azim:], new[:, :azim])
+        cells[r * polar : (r + 1) * polar, :] = new
     spec[...] = lax.dot_general(
-        waves[pa], cells, (((1,), (1,)), ((), ())),
+        waves[...], cells[...], (((1,), (1,)), ((), ())),
         precision=HIGH, preferred_element_type=jnp.float32,
     )
 
@@ -108,17 +141,13 @@
     pair = 2 * per
     owner = own(sizes)
     band = band_ref[...]
+    half = rows // n_pa
     for g in range(n_row):
-        parts = []
-        for t in range(n_ta):
-            base = (g * n_ta + t) * n_pa
-            total = spec_ref[base]
-            for h in range(1, n_pa):
-                total = total + spec_ref[base + h]
-            parts.append(total)
-        for r in range(rows):
-            piece = jnp.concatenate([x[:, r * polar : (r + 1) * polar] for x in parts], axis=1)
-            work_ref[g * rows + r] = piece * band
+        for h in range(n_pa):
+            parts = [spec_ref[(g * n_ta + t) * n_pa + h] for t in range(n_ta)]
+            for r in range(half):
+                piece = jnp.concatenate([x[:, r * polar : (r + 1) * polar] for x in parts], axis=1)
+                work_ref[g * rows + h * half + r] = piece * band
     table = leg_ref[...].reshape(per * degrees, polar_total)
     wide = lax.dot_general(
         work_ref[...].reshape(shells * pair, polar_total), table, (((1,), (1,)), ((), ())),
@@ -151,24 +180,26 @@
     spread = jnp.concatenate([jnp.where(slot == q, coeffs, 0.0) for q in range(per)], axis=1)
     field = jnp.dot(spread, table, precision=HIGH, preferred_element_type=jnp.float32)
     for g in range(n_row):
-        for t in range(n_ta):
-            pieces = [
-                field[(g * rows + r) * pair : (g * rows + r + 1) * pair, t * polar : (t + 1) * polar]
-                for r in range(rows)
-            ]
-            block = jnp.concatenate(pieces, axis=1)
-            for h in range(n_pa):
-                out_ref[(g * n_ta + t) * n_pa + h] = block
-
-
-def potential_kernel(spec, waves, out):
+        for h in range(n_pa):
+            for t in range(n_ta):
+                pieces = []
+                for r in range(half):
+                    i = g * rows + h * half + r
+                    pieces.append(field[i * pair : (i + 1) * pair, t * polar : (t + 1) * polar])
+                out_ref[(g * n_ta + t) * n_pa + h] = jnp.concatenate(pieces, axis=1)
+
+
+def potential_kernel(spec, far, waves, out):
     rows, polar, azim = out.shape
+    half = rows // 2
     pa = lax.axis_index("pa")
-    flat = lax.dot_general(
-        spec[...], waves[pa], (((0,), (0,)), ((), ())),
-        precision=HIGH, preferred_element_type=jnp.float32,
-    )
-    out[...] = flat.reshape(rows, polar, azim)
+    table = waves[:, pl.ds(pl.multiple_of(pa * azim, azim), azim)]
+    for part, place in ((spec, pa), (far, 1 - pa)):
+        flat = lax.dot_general(
+            part[...], table, (((0,), (0,)), ((), ())),
+            precision=HIGH, preferred_element_type=jnp.float32,
+        )
+        out[pl.ds(place * half, half)] = flat.reshape(half, polar, azim)
 
 
 def owner_of(sizes):
@@ -184,13 +215,24 @@
     polar_total, azim_total = polar * n_ta, azim * n_pa
     f32 = jnp.float32
 
-    ahead = lambda n: [(i, i + 1) for i in range(n - 1)]
-    back = lambda n: [(i + 1, i) for i in range(n - 1)]
-    below = lax.ppermute(density[-1:], "row", ahead(n_row))
-    above = lax.ppermute(density[:1], "row", back(n_row))
-    north = lax.ppermute(density[:, -1, :], "ta", ahead(n_ta))
-    south = lax.ppermute(density[:, 0, :], "ta", back(n_ta))
-    far = lax.ppermute(density, "pa", [(i, (i + n_pa // 2) % n_pa) for i in range(n_pa)])
+    half = rows // n_pa
+    swap = functools.partial(pair_swap, axes="pa", count=n_pa, first=0)
+    far, far_kappa = swap(density), swap(kappa)
+    edges = pl.pallas_call(
+        pack_kernel,
+        out_shape=(
+            jax.ShapeDtypeStruct((polar, azim_total), f32),
+            jax.ShapeDtypeStruct((half, azim_total), f32),
+            jax.ShapeDtypeStruct((half, azim_total), f32),
+        ),
+        in_specs=[VMEM] * 2,
+        out_specs=(VMEM,) * 3,
+        compiler_params=PARAMS,
+        name="pack",
+    )(density, far)
+    shell = pair_swap(edges[0], ("row", "pa"), n_row * n_pa, 1)
+    even_in = pair_swap(edges[1], "ta", n_ta, 0)
+    odd_in = pair_swap(edges[2], "ta", n_ta, 1)
 
     coef, sect = recursion_table(owners)
     edge = np.arange(polar_total + 1) * (math.pi / polar_total)
@@ -203,41 +245,51 @@
         in_specs=[SMEM, SMEM, VMEM, VMEM],
         out_specs=VMEM,
         cost_estimate=pl.CostEstimate(flops=10**7, bytes_accessed=10**6, transcendentals=0),
+        compiler_params=PARAMS,
         name="legendre",
     )(jnp.asarray(coef), jnp.asarray(sect), row_of(np.cos(theta)), row_of(np.sin(theta)))
 
-    waves = jnp.asarray(wave_table(azim_total, n_pa, owners))
-    updated, spec = pl.pallas_call(
+    waves = jnp.asarray(wave_table(azim_total, owners))
+    cells = half * polar
+    keep, send, spec = pl.pallas_call(
         functools.partial(stencil_kernel, sizes),
         out_shape=(
-            jax.ShapeDtypeStruct(density.shape, f32),
-            jax.ShapeDtypeStruct((2 * DEGREES, rows * polar), f32),
+            jax.ShapeDtypeStruct((half, polar, azim), f32),
+            jax.ShapeDtypeStruct((half, polar, azim), f32),
+            jax.ShapeDtypeStruct((2 * DEGREES, cells), f32),
         ),
         in_specs=[VMEM] * 8,
-        out_specs=(VMEM, VMEM),
+        out_specs=(VMEM,) * 3,
+        scratch_shapes=[pltpu.VMEM((cells, azim_total), f32)],
+        compiler_params=PARAMS,
         name="stencil",
-    )(density, kappa, far, below, above, north, south, waves)
-
-    spec = lax.all_to_all(
-        spec.reshape(owners, 2 * per, rows * polar), AXES, split_axis=0, concat_axis=0, tiled=True
+    )(density, far, kappa, far_kappa, shell, even_in, odd_in, waves)
+
+    spread = functools.partial(
+        lax.all_to_all, axis_name=AXES, split_axis=0, concat_axis=0, tiled=True
     )
+    spec = spread(spec.reshape(owners, 2 * per, cells))
+    back = swap(send)
+    first = lax.axis_index("pa") == 0
+    updated = jnp.concatenate([jnp.where(first, keep, back), jnp.where(first, back, keep)])
     spec = pl.pallas_call(
         functools.partial(solve_kernel, owner_of, sizes, rows, polar),
         out_shape=jax.ShapeDtypeStruct(spec.shape, f32),
         in_specs=[VMEM] * 3,
         out_specs=VMEM,
         scratch_shapes=[pltpu.VMEM((rows * n_row, 2 * per, polar_total), f32)],
+        compiler_params=PARAMS,
         name="solve",
     )(spec, legendre, row_of(band))
-    spec = lax.all_to_all(spec, AXES, split_axis=0, concat_axis=0, tiled=True)
-
+    spec = spread(spec).reshape(2 * DEGREES, cells)
     potential = pl.pallas_call(
         potential_kernel,
         out_shape=jax.ShapeDtypeStruct(density.shape, f32),
-        in_specs=[VMEM] * 2,
+        in_specs=[VMEM] * 3,
         out_specs=VMEM,
+        compiler_params=PARAMS,
         name="potential",
-    )(spec.reshape(2 * DEGREES, rows * polar), waves)
+    )(spec, swap(spec), waves)
     return (updated, potential)
 
 

time: 58.6 us -> 46.2 us (0.79)
  blocking collectives: 13.8 us -> 0 us
  waiting for transfers between devices: 9.09 us -> 14 us
  Pallas kernels: 13.8 us -> 9.5 us
  starting transfers between devices: 16.9 us -> 19 us
  local copies, waits for them, and re-layouts: 3.69 us -> 1.92 us
  other arithmetic: 0 us -> 0.74 us
    all_to_all x1 -> x0, blocking collectives: 13.8 us -> none  [shards(): spec = lax.all_to_all(spec, AXES, split_axis=0, concat_axis=0, tiled=True)]
    all_to_all x1 -> x2, starting transfers between devices: 4.78 us -> 13.7 us  [the longest x1 11.2 us: shards(): spec = spread(spec.reshape(owners, 2 * per, cells))]
    ppermute x5 -> x7, starting transfers between devices: 12.1 us -> 5.27 us  [pair_swap(): return lax.ppermute(value, axes, pairs)]
    all_to_all x1 -> x2, waiting for transfers between devices: 4.9 us -> 11.4 us  [the longest x1 8.02 us: shards(): spec = spread(spec).reshape(2 * DEGREES, cells)]
    slice x2 -> x0, local copies, waits for them, and re-layouts: 1.66 us -> none  [the longest x1 0.88 us: shards(): above = lax.ppermute(density[:1], 'row', back(n_row))]
    ppermute x5 -> x7, waiting for transfers between devices: 4.19 us -> 2.6 us  [pair_swap(): return lax.ppermute(value, axes, pairs)]
    pallas_call x1, Pallas kernels: 3.28 us -> 2.11 us  [shards(): pl.pallas_call(functools.partial(solve_kernel, owner_of, sizes, rows, pol...]
    pallas_call x1, Pallas kernels: 2.64 us -> 1.49 us  [shards(): pl.pallas_call(functools.partial(stencil_kernel, sizes), out_shape=(jax.S...]
  transfers between devices with their start and end apart: 6 -> 9, of which waited for: 2 -> 5; matrix products, arithmetic and copies ran while one was open for 3% -> 2% of each run, Pallas kernels for 10% -> 10%
where the time goes in v2:
time: 46.2 us; the launch traced here: 45.9 us
  starting transfers between devices  19 us (41%)
  waiting for transfers between devices  14 us (30%)
  Pallas kernels  9.5 us (21%)
  local copies, waits for them, and re-layouts  1.92 us (4%)
  between operations  0.76 us (2%)
  other arithmetic  0.74 us (2%)
    all_to_all x1, starting transfers between devices, shards(): spec = spread(spec.reshape(owners, 2 * per, cells))  11.2 us
    all_to_all x1, waiting for transfers between devices, shards(): spec = spread(spec).reshape(2 * DEGREES, cells)  8.02 us
    ppermute x7, starting transfers between devices, pair_swap(): return lax.ppermute(value, axes, pairs)  5.27 us
    pallas_call x1, Pallas kernels, shards(): pl.pallas_call(functools.partial(legendre_kernel, owner_of, sizes), out_s...  4.73 us
    all_to_all x1, waiting for transfers between devices, shards(): spec = spread(spec.reshape(owners, 2 * per, cells))  3.41 us
    ppermute x7, waiting for transfers between devices, pair_swap(): return lax.ppermute(value, axes, pairs)  2.6 us
    all_to_all x1, starting transfers between devices, shards(): spec = spread(spec).reshape(2 * DEGREES, cells)  2.58 us
    pallas_call x1, Pallas kernels, shards(): pl.pallas_call(functools.partial(solve_kernel, owner_of, sizes, rows, pol...  2.11 us
  transfers between devices with their start and end apart: 9, of which 5 were waited for; matrix products, arithmetic and copies ran while one was open for 2% of the time, Pallas kernels for 10%

profile of v2, /device:TPU:0, one launch (start us, length us, event | category | flops | bytes accessed | tf_op | source)
XLA Modules:
  0.0 45.9 jit_solution(5015408614394310801)
XLA Ops:
  0.6 0.0 copy-start
  0.6 0.6 %collective-permute-start = (f32[4,64,256]{2,1,0:T(8,128)}, f32[4,64,256]{2,1,0:T(8,128)S(1)}, u32[]{:S(2)}, u32[]{:S(2)}) collective-permute-start(f32[4,64,256]{2,1,0:T(8,128)} %rho.3), channel_id=1, source_target_pairs={{0,1},{1,0},{2,3},{3,2},{4,5},{5,4},{6,7},{7,6},{8,9},{9,8},{10,11... | collective-permute-start | bytes 786440 | tf_op jit(solution)/shard_map/ppermute | solution.py:76
  1.2 0.1 collective-permute-start.1
  1.3 1.3 %collective-permute-done.far = f32[4,64,256]{2,1,0:T(8,128)S(1)} collective-permute-done((f32[4,64,256]{2,1,0:T(8,128)}, f32[4,64,256]{2,1,0:T(8,128)S(1)}, u32[]{:S(2)}, u32[]{:S(2)}) %collective-permute-start) | collective-permute-done | bytes 262176 | tf_op jit(solution)/shard_map/ppermute | solution.py:76
  2.6 0.9 %copy-done.1 = f32[4,64,256]{2,1,0:T(8,128)S(1)} copy-done((f32[4,64,256]{2,1,0:T(8,128)S(1)}, f32[4,64,256]{2,1,0:T(8,128)}, u32[]{:S(2)}) %copy-start.1) | copy-done | bytes 262168
  3.6 0.7 %collective-permute-start.2 = (f32[64,512]{1,0:T(8,128)S(1)}, f32[64,512]{1,0:T(8,128)S(1)}, u32[]{:S(2)}, u32[]{:S(2)}) collective-permute-start(f32[64,512]{1,0:T(8,128)S(1)} %get-tuple-element.8), channel_id=1, source_target_pairs={{1,8},{8,1},{9,16},{16,9},{17,24},{24,17},{3,10},{10,3},{11,18},{1... | collective-permute-start | bytes 393224 | tf_op jit(solution)/shard_map/ppermute | solution.py:76
  4.2 2.9 %collective-permute-start.3 = (f32[2,512]{1,0:T(2,128)S(1)}, f32[2,512]{1,0:T(2,128)S(1)}, u32[]{:S(2)}, u32[]{:S(2)}) collective-permute-start(f32[2,512]{1,0:T(2,128)S(1)} %get-tuple-element.9), channel_id=1, source_target_pairs={{0,2},{2,0},{4,6},{6,4},{1,3},{3,1},{5,7},{7,5},{8,10},{10,8},{12,... | collective-permute-start | bytes 12296 | tf_op jit(solution)/shard_map/ppermute | solution.py:76
  7.1 0.6 %collective-permute-start.4 = (f32[2,512]{1,0:T(2,128)S(1)}, f32[2,512]{1,0:T(2,128)S(1)}, u32[]{:S(2)}, u32[]{:S(2)}) collective-permute-start(f32[2,512]{1,0:T(2,128)S(1)} %get-tuple-element.10), channel_id=1, source_target_pairs={{2,4},{4,2},{3,5},{5,3},{10,12},{12,10},{11,13},{13,11},{18,20},{2... | collective-permute-start | bytes 12296 | tf_op jit(solution)/shard_map/ppermute | solution.py:76
  7.8 0.9 %collective-permute-done.3.even_in = f32[2,512]{1,0:T(2,128)S(1)} collective-permute-done((f32[2,512]{1,0:T(2,128)S(1)}, f32[2,512]{1,0:T(2,128)S(1)}, u32[]{:S(2)}, u32[]{:S(2)}) %collective-permute-start.3) | collective-permute-done | bytes 4128 | tf_op jit(solution)/shard_map/ppermute | solution.py:76
  8.7 0.0 copy-start.2
  8.8 0.9 %copy-done.2 = f32[4,64,256]{2,1,0:T(8,128)S(1)} copy-done((f32[4,64,256]{2,1,0:T(8,128)S(1)}, f32[4,64,256]{2,1,0:T(8,128)}, u32[]{:S(2)}) %copy-start.2) | copy-done | bytes 262168
  9.7 1.5 %stencil.1 = (f32[2,64,256]{2,1,0:T(8,128)S(1)}, f32[2,64,256]{2,1,0:T(8,128)S(1)}, f32[256,128]{1,0:T(8,128)}) custom-call(f32[4,64,256]{2,1,0:T(8,128)S(1)} %copy-done.1, f32[4,64,256]{2,1,0:T(8,128)S(1)} %collective-permute-done.far, f32[4,64,256]{2,1,0:T(8,128)S(1)} %copy-done.2, f32[4,64,256]{2,1,0:T(8,128)S(1)} %collective-permute-done.1.far_kappa, ...), custom_call_target="tpu_custom_call" | custom-call | tf_op jit(solution)/shard_map/stencil/pallas_call | solution.py:254
  11.2 11.2 %all-to-all-start = ((f32[32,8,128]{2,1,0:T(8,128)}), f32[32,8,128]{2,1,0:T(8,128)S(1)}, u32[]{:S(2)}, u32[]{:S(2)}) async-start(f32[32,8,128]{2,1,0:T(8,128)} %bitcast), calls=%async_computation | async-start | bytes 262144 | tf_op jit(solution)/shard_map/all_to_all | solution.py:271
  22.4 0.0 copy-start.4
  22.4 4.7 %legendre.1.leg_ref = f32[4,128,256]{2,1,0:T(8,128)S(1)} custom-call(f32[32,2,512]{2,1,0:T(2,128)S(1)} %copy-done.3, f32[128]{0:T(128)S(1)} %copy-done.7, f32[1,256]{1,0:T(1,128)S(1)} %copy-done.5, f32[1,256]{1,0:T(1,128)S(1)} %copy-done.6), custom_call_target="tpu_custom_call" | custom-call | flops 10000000 | bytes 1000000 | tf_op jit(solution)/shard_map/legendre/pallas_call | solution.py:242
  27.2 3.4 %all-to-all-done.spec_ref = f32[32,8,128]{2,1,0:T(8,128)S(1)} async-done(((f32[32,8,128]{2,1,0:T(8,128)}), f32[32,8,128]{2,1,0:T(8,128)S(1)}, u32[]{:S(2)}, u32[]{:S(2)}) %all-to-all-start) | async-done | bytes 131104 | tf_op jit(solution)/shard_map/all_to_all | solution.py:271
  30.6 2.1 %solve.1 = f32[32,8,128]{2,1,0:T(8,128)} custom-call(f32[32,8,128]{2,1,0:T(8,128)S(1)} %all-to-all-done.spec_ref, f32[4,128,256]{2,1,0:T(8,128)S(1)} %legendre.1.leg_ref, f32[1,256]{1,0:T(1,128)S(1)} %copy-done.4), custom_call_target="tpu_custom_call" | custom-call | tf_op jit(solution)/shard_map/solve/pallas_call | solution.py:275
  32.7 2.6 %all-to-all-start.1 = ((f32[32,8,128]{2,1,0:T(8,128)}), f32[32,8,128]{2,1,0:T(8,128)S(1)}, u32[]{:S(2)}, u32[]{:S(2)}) async-start(f32[32,8,128]{2,1,0:T(8,128)} %solve.1), calls=%async_computation.1 | async-start | bytes 262144 | tf_op jit(solution)/shard_map/all_to_all | solution.py:284
  35.3 0.2 collective-permute-start.5
  35.4 8.0 %all-to-all-done.1 = f32[32,8,128]{2,1,0:T(8,128)S(1)} async-done(((f32[32,8,128]{2,1,0:T(8,128)}), f32[32,8,128]{2,1,0:T(8,128)S(1)}, u32[]{:S(2)}, u32[]{:S(2)}) %all-to-all-start.1) | async-done | bytes 131104 | tf_op jit(solution)/shard_map/all_to_all | solution.py:284
  43.5 0.2 collective-permute-start.6
  43.7 0.7 %pad_maximum_fusion = f32[4,64,256]{2,1,0:T(8,128)} fusion(f32[2,64,256]{2,1,0:T(8,128)S(1)} %get-tuple-element.15, f32[2,64,256]{2,1,0:T(8,128)S(1)} %get-tuple-element.14), kind=kLoop, calls=%fused_computation | loop fusion | flops 65536 | bytes 524288 | tf_op jit(solution)/shard_map/concatenate | solution.py:274
  44.4 0.4 collective-permute-done.6.far
  44.8 1.1 %potential.1 = f32[4,64,256]{2,1,0:T(8,128)} custom-call(f32[256,128]{1,0:T(8,128)S(1)} %bitcast.3, f32[256,128]{1,0:T(8,128)S(1)} %collective-permute-done.6.far, f32[256,512]{1,0:T(8,128)S(1)} %copy-done), custom_call_target="tpu_custom_call" | custom-call | tf_op jit(solution)/shard_map/potential/pallas_call | solution.py:285
  (17 shorter events, 0.1 us)
Async XLA Ops:
  0.6 8.1 %copy-start = (f32[256,512]{1,0:T(8,128)S(1)}, f32[256,512]{1,0:T(8,128)}, u32[]{:S(2)}) copy-start(f32[256,512]{1,0:T(8,128)} %constant.22.clone.waves) | copy-start | bytes 1572868
  0.6 1.9 %collective-permute-start = (f32[4,64,256]{2,1,0:T(8,128)}, f32[4,64,256]{2,1,0:T(8,128)S(1)}, u32[]{:S(2)}, u32[]{:S(2)}) collective-permute-start(f32[4,64,256]{2,1,0:T(8,128)} %rho.3), channel_id=1, source_target_pairs={{0,1},{1,0},{2,3},{3,2},{4,5},{5,4},{6,7},{7,6},{8,9},{9,8},{10,11... | collective-permute-start | bytes 786440 | tf_op jit(solution)/shard_map/ppermute | solution.py:76
  1.2 6.6 %collective-permute-start.1 = (f32[4,64,256]{2,1,0:T(8,128)}, f32[4,64,256]{2,1,0:T(8,128)S(1)}, u32[]{:S(2)}, u32[]{:S(2)}) collective-permute-start(f32[4,64,256]{2,1,0:T(8,128)} %kappa.1), channel_id=1, source_target_pairs={{0,1},{1,0},{2,3},{3,2},{4,5},{5,4},{6,7},{7,6},{8,9},{9,8},{10,11... | collective-permute-start | bytes 786440 | tf_op jit(solution)/shard_map/ppermute | solution.py:76
  2.6 0.9 %copy-start.1 = (f32[4,64,256]{2,1,0:T(8,128)S(1)}, f32[4,64,256]{2,1,0:T(8,128)}, u32[]{:S(2)}) copy-start(f32[4,64,256]{2,1,0:T(8,128)} %rho.3) | copy-start | bytes 786436
  3.6 5.2 %collective-permute-start.2 = (f32[64,512]{1,0:T(8,128)S(1)}, f32[64,512]{1,0:T(8,128)S(1)}, u32[]{:S(2)}, u32[]{:S(2)}) collective-permute-start(f32[64,512]{1,0:T(8,128)S(1)} %get-tuple-element.8), channel_id=1, source_target_pairs={{1,8},{8,1},{9,16},{16,9},{17,24},{24,17},{3,10},{10,3},{11,18},{1... | collective-permute-start | bytes 393224 | tf_op jit(solution)/shard_map/ppermute | solution.py:76
  4.2 4.5 %collective-permute-start.3 = (f32[2,512]{1,0:T(2,128)S(1)}, f32[2,512]{1,0:T(2,128)S(1)}, u32[]{:S(2)}, u32[]{:S(2)}) collective-permute-start(f32[2,512]{1,0:T(2,128)S(1)} %get-tuple-element.9), channel_id=1, source_target_pairs={{0,2},{2,0},{4,6},{6,4},{1,3},{3,1},{5,7},{7,5},{8,10},{10,8},{12,... | collective-permute-start | bytes 12296 | tf_op jit(solution)/shard_map/ppermute | solution.py:76
  7.1 1.6 %collective-permute-start.4 = (f32[2,512]{1,0:T(2,128)S(1)}, f32[2,512]{1,0:T(2,128)S(1)}, u32[]{:S(2)}, u32[]{:S(2)}) collective-permute-start(f32[2,512]{1,0:T(2,128)S(1)} %get-tuple-element.10), channel_id=1, source_target_pairs={{2,4},{4,2},{3,5},{5,3},{10,12},{12,10},{11,13},{13,11},{18,20},{2... | collective-permute-start | bytes 12296 | tf_op jit(solution)/shard_map/ppermute | solution.py:76
  8.7 1.0 %copy-start.2 = (f32[4,64,256]{2,1,0:T(8,128)S(1)}, f32[4,64,256]{2,1,0:T(8,128)}, u32[]{:S(2)}) copy-start(f32[4,64,256]{2,1,0:T(8,128)} %kappa.1) | copy-start | bytes 786436
  11.2 11.2 %copy-start.3 = (f32[32,2,512]{2,1,0:T(2,128)S(1)}, f32[32,2,512]{2,1,0:T(2,128)}, u32[]{:S(2)}) copy-start(f32[32,2,512]{2,1,0:T(2,128)} %constant.18.clone.coef_ref) | copy-start | bytes 393220
  11.2 11.2 %copy-start.5 = (f32[1,256]{1,0:T(1,128)S(1)}, f32[1,256]{1,0:T(1,128)}, u32[]{:S(2)}) copy-start(f32[1,256]{1,0:T(1,128)} %constant.20.clone.cos_ref) | copy-start | bytes 3076
  11.2 11.2 %copy-start.6 = (f32[1,256]{1,0:T(1,128)S(1)}, f32[1,256]{1,0:T(1,128)}, u32[]{:S(2)}) copy-start(f32[1,256]{1,0:T(1,128)} %constant.21.clone.sin_ref) | copy-start | bytes 3076
  11.2 11.2 %copy-start.7 = (f32[128]{0:T(128)S(1)}, f32[128]{0:T(128)}, u32[]{:S(2)}) copy-start(f32[128]{0:T(128)} %constant.19.clone.sect_ref) | copy-start | bytes 1540
  11.2 19.4 %all-to-all-start = ((f32[32,8,128]{2,1,0:T(8,128)}), f32[32,8,128]{2,1,0:T(8,128)S(1)}, u32[]{:S(2)}, u32[]{:S(2)}) async-start(f32[32,8,128]{2,1,0:T(8,128)} %bitcast), calls=%async_computation | async-start | bytes 262144 | tf_op jit(solution)/shard_map/all_to_all | solution.py:271
  22.4 8.2 %copy-start.4 = (f32[1,256]{1,0:T(1,128)S(1)}, f32[1,256]{1,0:T(1,128)}, u32[]{:S(2)}) copy-start(f32[1,256]{1,0:T(1,128)} %constant.23.clone.band_ref) | copy-start | bytes 3076
  32.7 10.8 %all-to-all-start.1 = ((f32[32,8,128]{2,1,0:T(8,128)}), f32[32,8,128]{2,1,0:T(8,128)S(1)}, u32[]{:S(2)}, u32[]{:S(2)}) async-start(f32[32,8,128]{2,1,0:T(8,128)} %solve.1), calls=%async_computation.1 | async-start | bytes 262144 | tf_op jit(solution)/shard_map/all_to_all | solution.py:284
  35.3 8.4 %collective-permute-start.5 = (f32[2,64,256]{2,1,0:T(8,128)S(1)}, f32[2,64,256]{2,1,0:T(8,128)S(1)}, u32[]{:S(2)}, u32[]{:S(2)}) collective-permute-start(f32[2,64,256]{2,1,0:T(8,128)S(1)} %get-tuple-element.12), channel_id=1, source_target_pairs={{0,1},{1,0},{2,3},{3,2},{4,5},{5,4},{6,7},{7,6},{8,9},{9,8},{10,11... | collective-permute-start | bytes 393224 | tf_op jit(solution)/shard_map/ppermute | solution.py:76
  43.5 1.3 %collective-permute-start.6 = (f32[256,128]{1,0:T(8,128)S(1)}, f32[256,128]{1,0:T(8,128)S(1)}, u32[]{:S(2)}, u32[]{:S(2)}) collective-permute-start(f32[256,128]{1,0:T(8,128)S(1)} %bitcast.2), channel_id=1, source_target_pairs={{0,1},{1,0},{2,3},{3,2},{4,5},{5,4},{6,7},{7,6},{8,9},{9,8},{10,11... | collective-permute-start | bytes 393224 | tf_op jit(solution)/shard_map/ppermute | solution.py:76

commit v3 on v2

--- a/solution.py
+++ b/solution.py
@@ -76,30 +76,41 @@
     return lax.ppermute(value, axes, pairs)
 
 
+def polar_pairs(n_ta, n_pa):
+    pairs = []
+    for core in range(2):
+        for t in range(core, n_ta - 1, 2):
+            here, there = t * n_pa + core, (t + 1) * n_pa + core
+            pairs += [(here, there), (there, here)]
+    return pairs
+
+
 def joined(pa, own, far):
     return jnp.concatenate([jnp.where(pa == 0, own, far), jnp.where(pa == 0, far, own)], axis=1)
 
 
-def pack_kernel(rho, far, shell_out, even_out, odd_out):
+def stage_kernel(rho, kappa, rho_out, kappa_out):
+    rho_out[...] = rho[...]
+    kappa_out[...] = kappa[...]
+
+
+def pack_kernel(rho, far, shell_out, ends_out):
     rows, polar, azim = rho.shape
-    half = rows // 2
     ta, pa = lax.axis_index("ta"), lax.axis_index("pa")
     edge = pa * (rows - 1)
     shell_out[...] = joined(pa, rho[edge], far[edge])
-    even = ta % 2 == 0
-    for r in range(half):
-        own, other = rho.at[pa * half + r], far.at[pa * half + r]
-        top = joined(pa, own[0:1, :], other[0:1, :])
-        low = joined(pa, own[polar - 1 : polar, :], other[polar - 1 : polar, :])
-        even_out[r : r + 1, :] = jnp.where(even, low, top)
-        odd_out[r : r + 1, :] = jnp.where(even, top, low)
-
-
-def stencil_kernel(sizes, rho, far, kappa, far_kappa, shell, even_in, odd_in, waves, keep, send, spec, cells):
+    low = ta % 2 == pa
+    for r in range(rows):
+        first = joined(pa, rho[r, 0:1, :], far[r, 0:1, :])
+        last = joined(pa, rho[r, polar - 1 : polar, :], far[r, polar - 1 : polar, :])
+        ends_out[r : r + 1, :] = jnp.where(low, last, first)
+
+
+def stencil_kernel(sizes, rho, far, kappa, far_kappa, shell, mine, theirs, waves, keep, send, spec, cells):
     rows, polar, azim = rho.shape
     half = rows // 2
     row, ta, pa = (lax.axis_index(a) for a in AXES)
-    even = ta % 2 == 0
+    low = ta % 2 == pa
     sub = lax.broadcasted_iota(jnp.int32, (polar, 2 * azim), 0)
     at = lambda i: joined(pa, rho[i], far[i])
     for r in range(half):
@@ -115,8 +126,8 @@
             up = jnp.where(pa == 0, at(jnp.minimum(i + 1, rows - 1)), ghost)
         else:
             up = at(i + 1)
-        north = jnp.where(even, odd_in[r : r + 1, :], even_in[r : r + 1, :])
-        south = jnp.where(even, even_in[r : r + 1, :], odd_in[r : r + 1, :])
+        north = jnp.where(low, theirs[pl.ds(i, 1), :], mine[pl.ds(i, 1), :])
+        south = jnp.where(low, mine[pl.ds(i, 1), :], theirs[pl.ds(i, 1), :])
         north = jnp.where(ta == 0, pltpu.roll(c[0:1, :], azim, 1), north)
         south = jnp.where(ta == sizes[1] - 1, pltpu.roll(c[polar - 1 :, :], azim, 1), south)
         pol_up = jnp.where(sub == 0, north, pltpu.roll(c, 1, 0))
@@ -218,21 +229,29 @@
     half = rows // n_pa
     swap = functools.partial(pair_swap, axes="pa", count=n_pa, first=0)
     far, far_kappa = swap(density), swap(kappa)
-    edges = pl.pallas_call(
+    density, kappa = pl.pallas_call(
+        stage_kernel,
+        out_shape=(jax.ShapeDtypeStruct(density.shape, f32),) * 2,
+        in_specs=[VMEM] * 2,
+        out_specs=(VMEM,) * 2,
+        compiler_params=PARAMS,
+        cost_estimate=pl.CostEstimate(flops=0, bytes_accessed=2**20, transcendentals=0),
+        name="stage",
+    )(density, kappa)
+    shell, ends = pl.pallas_call(
         pack_kernel,
         out_shape=(
             jax.ShapeDtypeStruct((polar, azim_total), f32),
-            jax.ShapeDtypeStruct((half, azim_total), f32),
-            jax.ShapeDtypeStruct((half, azim_total), f32),
+            jax.ShapeDtypeStruct((rows, azim_total), f32),
         ),
         in_specs=[VMEM] * 2,
-        out_specs=(VMEM,) * 3,
+        out_specs=(VMEM,) * 2,
         compiler_params=PARAMS,
         name="pack",
     )(density, far)
-    shell = pair_swap(edges[0], ("row", "pa"), n_row * n_pa, 1)
-    even_in = pair_swap(edges[1], "ta", n_ta, 0)
-    odd_in = pair_swap(edges[2], "ta", n_ta, 1)
+    mine = lax.ppermute(ends, ("ta", "pa"), polar_pairs(n_ta, n_pa))
+    shell = pair_swap(shell, ("row", "pa"), n_row * n_pa, 1)
+    theirs = swap(mine)
 
     coef, sect = recursion_table(owners)
     edge = np.arange(polar_total + 1) * (math.pi / polar_total)
@@ -263,7 +282,7 @@
         scratch_shapes=[pltpu.VMEM((cells, azim_total), f32)],
         compiler_params=PARAMS,
         name="stencil",
-    )(density, far, kappa, far_kappa, shell, even_in, odd_in, waves)
+    )(density, far, kappa, far_kappa, shell, mine, theirs, waves)
 
     spread = functools.partial(
         lax.all_to_all, axis_name=AXES, split_axis=0, concat_axis=0, tiled=True

time: 46.2 us -> 44.7 us (0.968)
  starting transfers between devices: 19 us -> 16.8 us
  waiting for transfers between devices: 14 us -> 14.6 us
    ppermute x0 -> x1, starting transfers between devices: none -> 4.81 us  [shards(): mine = lax.ppermute(ends, ('ta', 'pa'), polar_pairs(n_ta, n_pa))]
    ppermute x7 -> x6, starting transfers between devices: 5.27 us -> 1.71 us  [pair_swap(): return lax.ppermute(value, axes, pairs)]
    all_to_all x1, starting transfers between devices: 11.2 us -> 7.75 us  [shards(): spec = spread(spec.reshape(owners, 2 * per, cells))]
    ppermute x0 -> x1, waiting for transfers between devices: none -> 1.61 us  [shards(): mine = lax.ppermute(ends, ('ta', 'pa'), polar_pairs(n_ta, n_pa))]
    ppermute x7 -> x6, waiting for transfers between devices: 2.6 us -> 1.56 us  [pair_swap(): return lax.ppermute(value, axes, pairs)]
  transfers between devices with their start and end apart: 9 -> 9, of which waited for: 5 -> 5; matrix products, arithmetic and copies ran while one was open for 2% -> 2% of each run, Pallas kernels for 10% -> 11%
where the time goes in v3:
time: 44.7 us; the launch traced here: 44.4 us
  starting transfers between devices  16.8 us (38%)
  waiting for transfers between devices  14.6 us (33%)
  Pallas kernels  9.53 us (21%)
  local copies, waits for them, and re-layouts  1.93 us (4%)
  between operations  0.76 us (2%)
  other arithmetic  0.74 us (2%)
    all_to_all x1, waiting for transfers between devices, shards(): spec = spread(spec).reshape(2 * DEGREES, cells)  8.02 us
    all_to_all x1, starting transfers between devices, shards(): spec = spread(spec.reshape(owners, 2 * per, cells))  7.75 us
    ppermute x1, starting transfers between devices, shards(): mine = lax.ppermute(ends, ('ta', 'pa'), polar_pairs(n_ta, n_pa))  4.81 us
    pallas_call x1, Pallas kernels, shards(): pl.pallas_call(functools.partial(legendre_kernel, owner_of, sizes), out_s...  4.73 us
    all_to_all x1, waiting for transfers between devices, shards(): spec = spread(spec.reshape(owners, 2 * per, cells))  3.41 us
    all_to_all x1, starting transfers between devices, shards(): spec = spread(spec).reshape(2 * DEGREES, cells)  2.58 us
    pallas_call x1, Pallas kernels, shards(): pl.pallas_call(functools.partial(solve_kernel, owner_of, sizes, rows, pol...  2.11 us
    unnamed x16, local copies, waits for them, and re-layouts  1.93 us
  transfers between devices with their start and end apart: 9, of which 5 were waited for; matrix products, arithmetic and copies ran while one was open for 2% of the time, Pallas kernels for 11%

profile of v3, /device:TPU:0, one launch (start us, length us, event | category | flops | bytes accessed | tf_op | source)
XLA Modules:
  0.0 44.4 jit_solution(6341188638165480792)
XLA Ops:
  0.6 0.0 copy-start
  0.6 0.6 %collective-permute-start = (f32[4,64,256]{2,1,0:T(8,128)}, f32[4,64,256]{2,1,0:T(8,128)S(1)}, u32[]{:S(2)}, u32[]{:S(2)}) collective-permute-start(f32[4,64,256]{2,1,0:T(8,128)} %rho.1), channel_id=1, source_target_pairs={{0,1},{1,0},{2,3},{3,2},{4,5},{5,4},{6,7},{7,6},{8,9},{9,8},{10,11... | collective-permute-start | bytes 786440 | tf_op jit(solution)/shard_map/ppermute | solution.py:76
  1.2 0.1 collective-permute-start.1
  1.3 0.9 %copy-done.1 = f32[4,64,256]{2,1,0:T(8,128)S(1)} copy-done((f32[4,64,256]{2,1,0:T(8,128)S(1)}, f32[4,64,256]{2,1,0:T(8,128)}, u32[]{:S(2)}) %copy-start.1) | copy-done | bytes 262168
  2.2 0.9 %copy-done.2 = f32[4,64,256]{2,1,0:T(8,128)S(1)} copy-done((f32[4,64,256]{2,1,0:T(8,128)S(1)}, f32[4,64,256]{2,1,0:T(8,128)}, u32[]{:S(2)}) %copy-start.2) | copy-done | bytes 262168
  3.3 0.7 %collective-permute-start.2 = (f32[64,512]{1,0:T(8,128)S(1)}, f32[64,512]{1,0:T(8,128)S(1)}, u32[]{:S(2)}, u32[]{:S(2)}) collective-permute-start(f32[64,512]{1,0:T(8,128)S(1)} %get-tuple-element.11), channel_id=1, source_target_pairs={{1,8},{8,1},{9,16},{16,9},{17,24},{24,17},{3,10},{10,3},{11,18},{1... | collective-permute-start | bytes 393224 | tf_op jit(solution)/shard_map/ppermute | solution.py:76
  3.9 4.8 %collective-permute-start.3 = (f32[4,512]{1,0:T(4,128)S(1)}, f32[4,512]{1,0:T(4,128)S(1)}, u32[]{:S(2)}, u32[]{:S(2)}) collective-permute-start(f32[4,512]{1,0:T(4,128)S(1)} %get-tuple-element.12), channel_id=1, source_target_pairs={{0,2},{2,0},{4,6},{6,4},{3,5},{5,3},{8,10},{10,8},{12,14},{14,12},... | collective-permute-start | bytes 24584 | tf_op jit(solution)/shard_map/ppermute | solution.py:252
  8.8 1.6 %collective-permute-done.3.mine = f32[4,512]{1,0:T(4,128)S(1)} collective-permute-done((f32[4,512]{1,0:T(4,128)S(1)}, f32[4,512]{1,0:T(4,128)S(1)}, u32[]{:S(2)}, u32[]{:S(2)}) %collective-permute-start.3) | collective-permute-done | bytes 8224 | tf_op jit(solution)/shard_map/ppermute | solution.py:252
  10.4 0.0 collective-permute-start.4
  10.4 0.0 collective-permute-done.1.far_kappa
  10.4 1.2 %collective-permute-done.4.theirs = f32[4,512]{1,0:T(4,128)S(1)} collective-permute-done((f32[4,512]{1,0:T(4,128)S(1)}, f32[4,512]{1,0:T(4,128)S(1)}, u32[]{:S(2)}, u32[]{:S(2)}) %collective-permute-start.4) | collective-permute-done | bytes 8224 | tf_op jit(solution)/shard_map/ppermute | solution.py:76
  11.6 1.5 %stencil.1 = (f32[2,64,256]{2,1,0:T(8,128)S(1)}, f32[2,64,256]{2,1,0:T(8,128)S(1)}, f32[256,128]{1,0:T(8,128)}) custom-call(f32[4,64,256]{2,1,0:T(8,128)S(1)} %get-tuple-element.9.rho, f32[4,64,256]{2,1,0:T(8,128)S(1)} %collective-permute-done.far, f32[4,64,256]{2,1,0:T(8,128)S(1)} %get-tuple-element.10.kappa, ...), custom_call_target="tpu_custom_call" | custom-call | tf_op jit(solution)/shard_map/stencil/pallas_call | solution.py:273
  13.1 7.8 %all-to-all-start = ((f32[32,8,128]{2,1,0:T(8,128)}), f32[32,8,128]{2,1,0:T(8,128)S(1)}, u32[]{:S(2)}, u32[]{:S(2)}) async-start(f32[32,8,128]{2,1,0:T(8,128)} %bitcast), calls=%async_computation | async-start | bytes 262144 | tf_op jit(solution)/shard_map/all_to_all | solution.py:290
  20.8 0.0 copy-start.4
  20.9 4.7 %legendre.1.leg_ref = f32[4,128,256]{2,1,0:T(8,128)S(1)} custom-call(f32[32,2,512]{2,1,0:T(2,128)S(1)} %copy-done.3, f32[128]{0:T(128)S(1)} %copy-done.7, f32[1,256]{1,0:T(1,128)S(1)} %copy-done.5, f32[1,256]{1,0:T(1,128)S(1)} %copy-done.6), custom_call_target="tpu_custom_call" | custom-call | flops 10000000 | bytes 1000000 | tf_op jit(solution)/shard_map/legendre/pallas_call | solution.py:261
  25.6 3.4 %all-to-all-done.spec_ref = f32[32,8,128]{2,1,0:T(8,128)S(1)} async-done(((f32[32,8,128]{2,1,0:T(8,128)}), f32[32,8,128]{2,1,0:T(8,128)S(1)}, u32[]{:S(2)}, u32[]{:S(2)}) %all-to-all-start) | async-done | bytes 131104 | tf_op jit(solution)/shard_map/all_to_all | solution.py:290
  29.0 2.1 %solve.1 = f32[32,8,128]{2,1,0:T(8,128)} custom-call(f32[32,8,128]{2,1,0:T(8,128)S(1)} %all-to-all-done.spec_ref, f32[4,128,256]{2,1,0:T(8,128)S(1)} %legendre.1.leg_ref, f32[1,256]{1,0:T(1,128)S(1)} %copy-done.4), custom_call_target="tpu_custom_call" | custom-call | tf_op jit(solution)/shard_map/solve/pallas_call | solution.py:294
  31.1 2.6 %all-to-all-start.1 = ((f32[32,8,128]{2,1,0:T(8,128)}), f32[32,8,128]{2,1,0:T(8,128)S(1)}, u32[]{:S(2)}, u32[]{:S(2)}) async-start(f32[32,8,128]{2,1,0:T(8,128)} %solve.1), calls=%async_computation.1 | async-start | bytes 262144 | tf_op jit(solution)/shard_map/all_to_all | solution.py:303
  33.7 0.2 collective-permute-start.5
  33.9 8.0 %all-to-all-done.1 = f32[32,8,128]{2,1,0:T(8,128)S(1)} async-done(((f32[32,8,128]{2,1,0:T(8,128)}), f32[32,8,128]{2,1,0:T(8,128)S(1)}, u32[]{:S(2)}, u32[]{:S(2)}) %all-to-all-start.1) | async-done | bytes 131104 | tf_op jit(solution)/shard_map/all_to_all | solution.py:303
  41.9 0.2 collective-permute-start.6
  42.2 0.7 %pad_maximum_fusion = f32[4,64,256]{2,1,0:T(8,128)} fusion(f32[2,64,256]{2,1,0:T(8,128)S(1)} %get-tuple-element.17, f32[2,64,256]{2,1,0:T(8,128)S(1)} %get-tuple-element.16), kind=kLoop, calls=%fused_computation | loop fusion | flops 65536 | bytes 524288 | tf_op jit(solution)/shard_map/concatenate | solution.py:293
  42.9 0.4 collective-permute-done.6.far
  43.3 1.1 %potential.1 = f32[4,64,256]{2,1,0:T(8,128)} custom-call(f32[256,128]{1,0:T(8,128)S(1)} %bitcast.3, f32[256,128]{1,0:T(8,128)S(1)} %collective-permute-done.6.far, f32[256,512]{1,0:T(8,128)S(1)} %copy-done), custom_call_target="tpu_custom_call" | custom-call | tf_op jit(solution)/shard_map/potential/pallas_call | solution.py:304
  (18 shorter events, 0.1 us)
Async XLA Ops:
  0.6 10.9 %copy-start = (f32[256,512]{1,0:T(8,128)S(1)}, f32[256,512]{1,0:T(8,128)}, u32[]{:S(2)}) copy-start(f32[256,512]{1,0:T(8,128)} %constant.22.clone.waves) | copy-start | bytes 1572868
  0.6 2.6 %collective-permute-start = (f32[4,64,256]{2,1,0:T(8,128)}, f32[4,64,256]{2,1,0:T(8,128)S(1)}, u32[]{:S(2)}, u32[]{:S(2)}) collective-permute-start(f32[4,64,256]{2,1,0:T(8,128)} %rho.1), channel_id=1, source_target_pairs={{0,1},{1,0},{2,3},{3,2},{4,5},{5,4},{6,7},{7,6},{8,9},{9,8},{10,11... | collective-permute-start | bytes 786440 | tf_op jit(solution)/shard_map/ppermute | solution.py:76
  1.2 9.2 %collective-permute-start.1 = (f32[4,64,256]{2,1,0:T(8,128)}, f32[4,64,256]{2,1,0:T(8,128)S(1)}, u32[]{:S(2)}, u32[]{:S(2)}) collective-permute-start(f32[4,64,256]{2,1,0:T(8,128)} %kappa.1), channel_id=1, source_target_pairs={{0,1},{1,0},{2,3},{3,2},{4,5},{5,4},{6,7},{7,6},{8,9},{9,8},{10,11... | collective-permute-start | bytes 786440 | tf_op jit(solution)/shard_map/ppermute | solution.py:76
  1.3 0.9 %copy-start.1 = (f32[4,64,256]{2,1,0:T(8,128)S(1)}, f32[4,64,256]{2,1,0:T(8,128)}, u32[]{:S(2)}) copy-start(f32[4,64,256]{2,1,0:T(8,128)} %rho.1) | copy-start | bytes 786436
  2.2 0.9 %copy-start.2 = (f32[4,64,256]{2,1,0:T(8,128)S(1)}, f32[4,64,256]{2,1,0:T(8,128)}, u32[]{:S(2)}) copy-start(f32[4,64,256]{2,1,0:T(8,128)} %kappa.1) | copy-start | bytes 786436
  3.3 8.3 %collective-permute-start.2 = (f32[64,512]{1,0:T(8,128)S(1)}, f32[64,512]{1,0:T(8,128)S(1)}, u32[]{:S(2)}, u32[]{:S(2)}) collective-permute-start(f32[64,512]{1,0:T(8,128)S(1)} %get-tuple-element.11), channel_id=1, source_target_pairs={{1,8},{8,1},{9,16},{16,9},{17,24},{24,17},{3,10},{10,3},{11,18},{1... | collective-permute-start | bytes 393224 | tf_op jit(solution)/shard_map/ppermute | solution.py:76
  3.9 6.4 %collective-permute-start.3 = (f32[4,512]{1,0:T(4,128)S(1)}, f32[4,512]{1,0:T(4,128)S(1)}, u32[]{:S(2)}, u32[]{:S(2)}) collective-permute-start(f32[4,512]{1,0:T(4,128)S(1)} %get-tuple-element.12), channel_id=1, source_target_pairs={{0,2},{2,0},{4,6},{6,4},{3,5},{5,3},{8,10},{10,8},{12,14},{14,12},... | collective-permute-start | bytes 24584 | tf_op jit(solution)/shard_map/ppermute | solution.py:252
  10.4 1.2 %collective-permute-start.4 = (f32[4,512]{1,0:T(4,128)S(1)}, f32[4,512]{1,0:T(4,128)S(1)}, u32[]{:S(2)}, u32[]{:S(2)}) collective-permute-start(f32[4,512]{1,0:T(4,128)S(1)} %collective-permute-done.3.mine), channel_id=1, source_target_pairs={{0,1},{1,0},{2,3},{3,2},{4,5},{5,4},{6,7},{7,6},{8,9},{9,8},{10,11... | collective-permute-start | bytes 24584 | tf_op jit(solution)/shard_map/ppermute | solution.py:76
  13.0 7.8 %copy-start.3 = (f32[32,2,512]{2,1,0:T(2,128)S(1)}, f32[32,2,512]{2,1,0:T(2,128)}, u32[]{:S(2)}) copy-start(f32[32,2,512]{2,1,0:T(2,128)} %constant.18.clone.coef_ref) | copy-start | bytes 393220
  13.0 7.8 %copy-start.5 = (f32[1,256]{1,0:T(1,128)S(1)}, f32[1,256]{1,0:T(1,128)}, u32[]{:S(2)}) copy-start(f32[1,256]{1,0:T(1,128)} %constant.20.clone.cos_ref) | copy-start | bytes 3076
  13.0 7.8 %copy-start.6 = (f32[1,256]{1,0:T(1,128)S(1)}, f32[1,256]{1,0:T(1,128)}, u32[]{:S(2)}) copy-start(f32[1,256]{1,0:T(1,128)} %constant.21.clone.sin_ref) | copy-start | bytes 3076
  13.0 7.8 %copy-start.7 = (f32[128]{0:T(128)S(1)}, f32[128]{0:T(128)}, u32[]{:S(2)}) copy-start(f32[128]{0:T(128)} %constant.19.clone.sect_ref) | copy-start | bytes 1540
  13.1 16.0 %all-to-all-start = ((f32[32,8,128]{2,1,0:T(8,128)}), f32[32,8,128]{2,1,0:T(8,128)S(1)}, u32[]{:S(2)}, u32[]{:S(2)}) async-start(f32[32,8,128]{2,1,0:T(8,128)} %bitcast), calls=%async_computation | async-start | bytes 262144 | tf_op jit(solution)/shard_map/all_to_all | solution.py:290
  20.8 8.2 %copy-start.4 = (f32[1,256]{1,0:T(1,128)S(1)}, f32[1,256]{1,0:T(1,128)}, u32[]{:S(2)}) copy-start(f32[1,256]{1,0:T(1,128)} %constant.23.clone.band_ref) | copy-start | bytes 3076
  31.1 10.8 %all-to-all-start.1 = ((f32[32,8,128]{2,1,0:T(8,128)}), f32[32,8,128]{2,1,0:T(8,128)S(1)}, u32[]{:S(2)}, u32[]{:S(2)}) async-start(f32[32,8,128]{2,1,0:T(8,128)} %solve.1), calls=%async_computation.1 | async-start | bytes 262144 | tf_op jit(solution)/shard_map/all_to_all | solution.py:303
  33.7 8.4 %collective-permute-start.5 = (f32[2,64,256]{2,1,0:T(8,128)S(1)}, f32[2,64,256]{2,1,0:T(8,128)S(1)}, u32[]{:S(2)}, u32[]{:S(2)}) collective-permute-start(f32[2,64,256]{2,1,0:T(8,128)S(1)} %get-tuple-element.14), channel_id=1, source_target_pairs={{0,1},{1,0},{2,3},{3,2},{4,5},{5,4},{6,7},{7,6},{8,9},{9,8},{10,11... | collective-permute-start | bytes 393224 | tf_op jit(solution)/shard_map/ppermute | solution.py:76
  41.9 1.3 %collective-permute-start.6 = (f32[256,128]{1,0:T(8,128)S(1)}, f32[256,128]{1,0:T(8,128)S(1)}, u32[]{:S(2)}, u32[]{:S(2)}) collective-permute-start(f32[256,128]{1,0:T(8,128)S(1)} %bitcast.2), channel_id=1, source_target_pairs={{0,1},{1,0},{2,3},{3,2},{4,5},{5,4},{6,7},{7,6},{8,9},{9,8},{10,11... | collective-permute-start | bytes 393224 | tf_op jit(solution)/shard_map/ppermute | solution.py:76

commit v4 on v2

v4 whole, which is shorter than its diff:
```python
import functools
import math

import jax
import jax.numpy as jnp
import numpy as np
from jax import lax
from jax.experimental import pallas as pl
from jax.experimental.pallas import tpu as pltpu
from jax.sharding import PartitionSpec as P


DEGREES = 128
AXES = ("row", "ta", "pa")
VMEM = pl.BlockSpec(memory_space=pltpu.VMEM)
PARAMS = pltpu.CompilerParams(vmem_limit_bytes=16 * 2**20)
F32 = jnp.float32
BF16 = jnp.bfloat16
NT = (((1,), (1,)), ((), ()))
NN = (((1,), (0,)), ((), ()))
TN = (((0,), (0,)), ((), ()))


def split(x):
    high = x.astype(BF16)
    return high, (x - high.astype(F32)).astype(BF16)


def dot3(a, b, dims):
    one = functools.partial(lax.dot_general, dimension_numbers=dims, preferred_element_type=F32)
    return one(a[0], b[0]) + (one(a[0], b[1]) + one(a[1], b[0]))


def wave_table(azim_total, owners):
    modes = np.arange(DEGREES).reshape(owners, 1, -1, 1)
    phi = (np.arange(azim_total) + 0.5) * (2.0 * math.pi / azim_total)
    both = np.concatenate([np.cos(modes * phi), np.sin(modes * phi)], axis=1)
    table = both.reshape(2 * DEGREES, azim_total)
    high = table.astype(BF16)
    low = (table - high.astype(np.float64)).astype(BF16)
    return jnp.asarray(high), jnp.asarray(low)


def recursion_table():
    l = np.arange(DEGREES, dtype=np.float64)[:, None]
    m = np.arange(DEGREES, dtype=np.float64)[None, :]
    below = m < l
    a = np.sqrt((4 * l * l - 1) / np.where(below, l * l - m * m, 1.0) * below)
    low = l - 1
    b = np.sqrt(np.maximum(low * low - m * m, 0) / np.maximum(4 * low * low - 1, 1.0))
    sect = np.where(l == 1, math.sqrt(3.0), np.sqrt((2 * l + 1) / np.maximum(2 * l, 1.0)))
    wide = np.broadcast_to(sect, (DEGREES, 128))
    return jnp.asarray(np.concatenate([a, a * b, wide]).astype(np.float32))


def small_table(polar_total, azim_total):
    edge = np.arange(polar_total + 1) * (math.pi / polar_total)
    theta = (np.arange(polar_total) + 0.5) * (math.pi / polar_total)
    band = (np.cos(edge[:-1]) - np.cos(edge[1:])) * (2.0 * math.pi / azim_total)
    x = np.cos(theta)
    mean = np.zeros(polar_total)
    prev, older = np.ones_like(x), np.zeros_like(x)
    for l in range(DEGREES):
        mean[l] = azim_total * np.sum(band * prev)
        n = l + 1
        a = math.sqrt((4 * n * n - 1) / (n * n))
        b = math.sqrt(l * l / max(4 * l * l - 1, 1))
        prev, older = a * (x * prev - b * older), prev
    return jnp.asarray(np.stack([x, np.sin(theta), band, mean]).astype(np.float32))


def owner_of(sizes):
    row, ta, pa = (lax.axis_index(a) for a in AXES)
    return (row * sizes[1] + ta) * sizes[2] + pa


def stage_kernel(source, target):
    target[...] = source[...]


def pack_kernel(rho, far, shell_out, ends_out):
    rows, polar, azim = rho.shape
    ta, pa = lax.axis_index("ta"), lax.axis_index("pa")
    edge = pa * (rows - 1)
    low = ta % 2 == pa
    for k, half in enumerate((rho, far)):
        at = pl.ds(k * azim, azim)
        shell_out[:, at] = half[edge]
        for r in range(rows):
            ends_out[r : r + 1, at] = jnp.where(low, half[r, polar - 1 : polar, :], half[r, 0:1, :])


def stencil_kernel(
    sizes, rho, far, kappa, far_kappa, shell, mine, theirs, w_high, w_low, keep, send, spec, cells
):
    rows, polar, azim = rho.shape
    half = rows // 2
    row, ta, pa = (lax.axis_index(a) for a in AXES)
    low = ta % 2 == pa
    sub = lax.broadcasted_iota(jnp.int32, (polar, 2 * azim), 0)
    both = lambda a, b: jnp.concatenate([a, b], axis=1)
    at = lambda i: both(rho[i], far[i])
    turned = lambda x: both(x[:, azim:], x[:, :azim])
    outer = turned(shell[...])
    for r in range(half):
        i = pa * half + r
        c = at(i)
        if r == 0:
            ghost = jnp.where(row == 0, c, outer)
            down = jnp.where(pa == 0, ghost, at(jnp.maximum(i - 1, 0)))
        else:
            down = at(i - 1)
        if r == half - 1:
            ghost = jnp.where(row == sizes[0] - 1, c, outer)
            up = jnp.where(pa == 0, at(jnp.minimum(i + 1, rows - 1)), ghost)
        else:
            up = at(i + 1)
        near, other = mine[pl.ds(i, 1), :], turned(theirs[pl.ds(i, 1), :])
        north = jnp.where(ta == 0, turned(c[0:1, :]), jnp.where(low, other, near))
        south = jnp.where(low, near, other)
        south = jnp.where(ta == sizes[1] - 1, turned(c[polar - 1 :, :]), south)
        pol_up = jnp.where(sub == 0, north, pltpu.roll(c, 1, 0))
        pol_down = jnp.where(sub == polar - 1, south, pltpu.roll(c, polar - 1, 0))
        west = pltpu.roll(c, 1, 1)
        east = pltpu.roll(c, 2 * azim - 1, 1)
        lap = up + down + pol_up + pol_down + west + east - 6.0 * c
        new = c + both(kappa[i], far_kappa[i]) * lap
        keep[r] = new[:, :azim]
        send[r] = new[:, azim:]
        cells[r * polar : (r + 1) * polar, :] = new - 1.0
    total = None
    for k, place in enumerate((pa, 1 - pa)):
        at = pl.ds(pl.multiple_of(place * azim, azim), azim)
        term = dot3((w_high[:, at], w_low[:, at]), split(cells[:, k * azim : (k + 1) * azim]), NT)
        total = term if total is None else total + term
    spec[...] = total


def join_kernel(keep, back, out):
    half = keep.shape[0]
    pa = lax.axis_index("pa")
    out[pl.ds(pa * half, half)] = keep[...]
    out[pl.ds((1 - pa) * half, half)] = back[...]


def table_kernel(sizes, coef_ref, trig_ref, high_ref, low_ref, extra_ref, spread_ref, work):
    per, degrees, polar = work.shape
    extra_ref[...] = trig_ref[2:4, :]
    start = owner_of(sizes) * per
    lanes = 128
    order = lax.broadcasted_iota(jnp.int32, (degrees, per * lanes), 0)
    slot = lax.broadcasted_iota(jnp.int32, (degrees, per * lanes), 1) // lanes
    pick = jnp.where(order == slot + start, 1.0, 0.0).astype(F32)
    wide = lax.dot_general(
        coef_ref[: 2 * degrees, :], pick, NN,
        precision=lax.Precision.HIGHEST, preferred_element_type=F32,
    )
    for q in range(per):
        spread_ref[q] = wide[:, q * lanes : (q + 1) * lanes]
    parts = polar // lanes
    cut = lambda row, k: jnp.broadcast_to(trig_ref[row : row + 1, k * lanes : (k + 1) * lanes], (8, lanes))
    cos_t = [cut(0, k) for k in range(parts)]
    sin_t = [cut(1, k) for k in range(parts)]
    sub = lax.broadcasted_iota(jnp.int32, (8, lanes), 0)

    def block(step, carry):
        sect, prev, older = carry
        base = pl.multiple_of(step * 8, 8)
        tiles = [[jnp.zeros((8, lanes), F32)] * parts for _ in range(per)]
        for inner in range(8):
            l = base + inner
            factor = coef_ref[pl.ds(2 * degrees + l, 8, stride=0), :]
            grown = [s * (factor * sin_t[k]) for k, s in enumerate(sect)]
            if inner == 0:
                grown = [jnp.where(step == 0, s, g) for s, g in zip(sect, grown)]
            sect = grown
            fresh = []
            for q in range(per):
                a = spread_ref[q, pl.ds(l, 8, stride=0), :]
                ab = spread_ref[q, pl.ds(degrees + l, 8, stride=0), :]
                seed = l == start + q
                line = []
                for k in range(parts):
                    new = (a * cos_t[k]) * prev[q][k] - ab * older[q][k]
                    new = jnp.where(seed, sect[k], new)
                    tiles[q][k] = jnp.where(sub == inner, new, tiles[q][k])
                    line.append(new)
                fresh.append(line)
            prev, older = fresh, prev
        for q in range(per):
            for k in range(parts):
                work[q, pl.ds(base, 8), k * lanes : (k + 1) * lanes] = tiles[q][k]
        return sect, prev, older

    zero = [[jnp.zeros((8, lanes), F32)] * parts for _ in range(per)]
    lax.fori_loop(0, degrees // 8, block, ([jnp.ones((8, lanes), F32)] * parts, zero, zero))
    for q in range(per):
        at = pl.ds(q * degrees, degrees)
        high_ref[at, :], low_ref[at, :] = split(work[q])


def solve_kernel(sizes, rows, polar, spec_ref, high_ref, low_ref, extra_ref, out_ref, work_ref):
    n_row, n_ta, n_pa = sizes
    shells = rows * n_row
    pair = spec_ref.shape[1]
    per = pair // 2
    degrees = high_ref.shape[0] // per
    half = rows // n_pa
    band = extra_ref[0:1, :]
    for g in range(n_row):
        for h in range(n_pa):
            parts = [spec_ref[(g * n_ta + t) * n_pa + h] for t in range(n_ta)]
            for r in range(half):
                piece = jnp.concatenate([x[:, r * polar : (r + 1) * polar] for x in parts], axis=1)
                work_ref[pl.ds((g * rows + h * half + r) * pair, pair), :] = piece * band
    table = high_ref[...], low_ref[...]
    wide = dot3(split(work_ref[...]), table, NT)
    slot = lax.broadcasted_iota(jnp.int32, (shells * pair, degrees), 0) % per
    picked = wide[:, :degrees]
    for q in range(1, per):
        picked = jnp.where(slot == q, wide[:, q * degrees : (q + 1) * degrees], picked)
    log_eight = math.log(8.0)
    step = log_eight / shells
    degree = lax.broadcasted_iota(jnp.int32, (pair, degrees), 1).astype(F32)
    decay_in = jnp.exp(-step * degree)
    decay_out = jnp.exp(-step * (degree + 1.0))
    scale = jnp.where(degree > 0.0, -1.0 / (4.0 * math.pi * (2.0 * degree + 1.0)), 0.0)
    edges = np.exp(log_eight * (np.arange(shells + 1) / shells - 1.0))
    volume = (edges[1:] ** 3 - edges[:-1] ** 3) / 3.0
    radii = np.exp(log_eight * ((np.arange(shells) + 0.5) / shells - 1.0))
    sub = lax.broadcasted_iota(jnp.int32, (pair, degrees), 0)
    mean = jnp.where((sub == 0) & (owner_of(sizes) == 0), extra_ref[1:2, :degrees], 0.0)
    picked = [picked[i * pair : (i + 1) * pair] + mean for i in range(shells)]
    moments = [picked[i] * float(volume[i]) for i in range(shells)]
    sums = []
    carry = jnp.zeros((pair, degrees), F32)
    for i in range(shells):
        carry = carry * decay_in + moments[i]
        sums.append(carry)
    carry = jnp.zeros((pair, degrees), F32)
    for i in reversed(range(shells)):
        sums[i] = (sums[i] + carry) * (scale * float(1.0 / radii[i]))
        carry = (carry + moments[i]) * decay_out
    coeffs = jnp.concatenate(sums, axis=0)
    spread = jnp.concatenate([jnp.where(slot == q, coeffs, 0.0) for q in range(per)], axis=1)
    field = dot3(split(spread), table, NN)
    for g in range(n_row):
        for h in range(n_pa):
            for t in range(n_ta):
                pieces = []
                for r in range(half):
                    i = g * rows + h * half + r
                    pieces.append(field[i * pair : (i + 1) * pair, t * polar : (t + 1) * polar])
                out_ref[(g * n_ta + t) * n_pa + h] = jnp.concatenate(pieces, axis=1)


def potential_kernel(spec, far, w_high, w_low, out):
    rows, polar, azim = out.shape
    half = rows // 2
    pa = lax.axis_index("pa")
    at = pl.ds(pl.multiple_of(pa * azim, azim), azim)
    table = w_high[:, at], w_low[:, at]
    for part, place in ((spec, pa), (far, 1 - pa)):
        flat = dot3(split(part[...]), table, TN)
        out[pl.ds(place * half, half)] = flat.reshape(half, polar, azim)


def call(kernel, outs, specs, scratch=(), flops=0):
    shapes = tuple(jax.ShapeDtypeStruct(s, d) for s, d in outs)
    return pl.pallas_call(
        kernel,
        out_shape=shapes,
        in_specs=specs,
        out_specs=(VMEM,) * len(outs),
        scratch_shapes=list(scratch),
        compiler_params=PARAMS,
        cost_estimate=pl.CostEstimate(flops=flops, bytes_accessed=2**20, transcendentals=0),
    )


def pair_swap(value, axes, count, first):
    pairs = []
    for i in range(first, count - 1, 2):
        pairs += [(i, i + 1), (i + 1, i)]
    return lax.ppermute(value, axes, pairs)


def polar_pairs(n_ta, n_pa):
    pairs = []
    for core in range(2):
        for t in range(core, n_ta - 1, 2):
            here, there = t * n_pa + core, (t + 1) * n_pa + core
            pairs += [(here, there), (there, here)]
    return pairs


def shards(sizes, density, kappa):
    n_row, n_ta, n_pa = sizes
    rows, polar, azim = density.shape
    owners = n_row * n_ta * n_pa
    per = DEGREES // owners
    polar_total, azim_total = polar * n_ta, azim * n_pa
    half = rows // n_pa
    cells = half * polar
    swap = functools.partial(pair_swap, axes="pa", count=n_pa, first=0)

    far, far_kappa = swap(density), swap(kappa)
    (density,) = call(stage_kernel, ((density.shape, F32),), [VMEM])(density)
    (kappa,) = call(stage_kernel, ((kappa.shape, F32),), [VMEM])(kappa)
    shell, ends = call(
        pack_kernel, (((polar, azim_total), F32), ((rows, azim_total), F32)), [VMEM] * 2
    )(density, far)
    mine = lax.ppermute(ends, ("ta", "pa"), polar_pairs(n_ta, n_pa))
    shell = pair_swap(shell, ("row", "pa"), n_row * n_pa, 1)
    theirs = swap(mine)

    small = small_table(polar_total, azim_total)
    high, low, extra = call(
        functools.partial(table_kernel, sizes),
        (((per * DEGREES, polar_total), BF16),) * 2 + (((2, polar_total), F32),),
        [VMEM] * 2,
        [pltpu.VMEM((per, 2 * DEGREES, 128), F32), pltpu.VMEM((per, DEGREES, polar_total), F32)],
        flops=10**7,
    )(recursion_table(), small)

    waves = wave_table(azim_total, owners)
    keep, send, spec = call(
        functools.partial(stencil_kernel, sizes),
        (((half, polar, azim), F32), ((half, polar, azim), F32), ((2 * DEGREES, cells), F32)),
        [VMEM] * 9,
        [pltpu.VMEM((cells, azim_total), F32)],
    )(density, far, kappa, far_kappa, shell, mine, theirs, *waves)

    back = swap(send)
    spread = functools.partial(
        lax.all_to_all, axis_name=AXES, split_axis=0, concat_axis=0, tiled=True
    )
    spec = spread(spec.reshape(owners, 2 * per, cells))

    (spec,) = call(
        functools.partial(solve_kernel, sizes, rows, polar),
        ((spec.shape, F32),),
        [VMEM] * 4,
        [pltpu.VMEM((rows * n_row * 2 * per, polar_total), F32)],
    )(spec, high, low, extra)
    spec = spread(spec).reshape(2 * DEGREES, cells)
    far = swap(spec)
    (updated,) = call(join_kernel, ((density.shape, F32),), [VMEM] * 2)(keep, back)
    (potential,) = call(potential_kernel, ((density.shape, F32),), [VMEM] * 4)(spec, far, *waves)
    return (updated, potential)


def solution(mesh):
    sizes = tuple(mesh.shape[a] for a in AXES)
    placed = (P(*AXES), P(*AXES))

    def body(density, kappa):
        return shards(sizes, density, kappa)

    return jax.shard_map(body, mesh=mesh, in_specs=placed, out_specs=placed, check_vma=False)
```

time: 46.2 us -> 43.2 us (0.935)
  waiting for transfers between devices: 14 us -> 17.7 us
  Pallas kernels: 9.5 us -> 6.51 us
  starting transfers between devices: 19 us -> 17 us
  local copies, waits for them, and re-layouts: 1.92 us -> 0.98 us
  other arithmetic: 0.74 us -> 0 us
    ppermute x0 -> x1, starting transfers between devices: none -> 4.89 us  [shards(): mine = lax.ppermute(ends, ('ta', 'pa'), polar_pairs(n_ta, n_pa))]
    ppermute x7 -> x6, starting transfers between devices: 5.27 us -> 1.7 us  [pair_swap(): return lax.ppermute(value, axes, pairs)]
    all_to_all x1, starting transfers between devices: 11.2 us -> 7.8 us  [shards(): spec = spread(spec.reshape(owners, 2 * per, cells))]
    pallas_call x5 -> x8, Pallas kernels: 9.5 us -> 6.51 us  [the longest x1 1.95 us: shards(): call(functools.partial(table_kernel, sizes), (((per * DEGREES, polar_tota...]
    all_to_all x1, waiting for transfers between devices: 3.41 us -> 6.23 us  [shards(): spec = spread(spec.reshape(owners, 2 * per, cells))]
    ppermute x0 -> x1, waiting for transfers between devices: none -> 1.61 us  [shards(): mine = lax.ppermute(ends, ('ta', 'pa'), polar_pairs(n_ta, n_pa))]
    unnamed x16 -> x12, local copies, waits for them, and re-layouts: 1.92 us -> 0.98 us
    ppermute x7 -> x6, waiting for transfers between devices: 2.6 us -> 1.85 us  [pair_swap(): return lax.ppermute(value, axes, pairs)]
  transfers between devices with their start and end apart: 9 -> 9, of which waited for: 5 -> 6; matrix products, arithmetic and copies ran while one was open for 2% -> 0% of each run, Pallas kernels for 10% -> 6%
where the time goes in v4:
time: 43.2 us; the launch traced here: 42.9 us
  waiting for transfers between devices  17.7 us (41%)
  starting transfers between devices  17 us (39%)
  Pallas kernels  6.51 us (15%)
  local copies, waits for them, and re-layouts  0.98 us (2%)
  between operations  0.74 us (2%)
    all_to_all x1, waiting for transfers between devices, shards(): spec = spread(spec).reshape(2 * DEGREES, cells)  8.03 us
    all_to_all x1, starting transfers between devices, shards(): spec = spread(spec.reshape(owners, 2 * per, cells))  7.8 us
    all_to_all x1, waiting for transfers between devices, shards(): spec = spread(spec.reshape(owners, 2 * per, cells))  6.23 us
    ppermute x1, starting transfers between devices, shards(): mine = lax.ppermute(ends, ('ta', 'pa'), polar_pairs(n_ta, n_pa))  4.89 us
    all_to_all x1, starting transfers between devices, shards(): spec = spread(spec).reshape(2 * DEGREES, cells)  2.58 us
    pallas_call x1, Pallas kernels, shards(): call(functools.partial(table_kernel, sizes), (((per * DEGREES, polar_tota...  1.95 us
    ppermute x6, waiting for transfers between devices, pair_swap(): return lax.ppermute(value, axes, pairs)  1.85 us
    ppermute x6, starting transfers between devices, pair_swap(): return lax.ppermute(value, axes, pairs)  1.7 us
  transfers between devices with their start and end apart: 9, of which 6 were waited for; matrix products, arithmetic and copies ran while one was open for 0% of the time, Pallas kernels for 6%

profile of v4, /device:TPU:0, one launch (start us, length us, event | category | flops | bytes accessed | tf_op | source)
XLA Modules:
  0.0 42.9 jit_solution(18170116261784206845)
XLA Ops:
  0.6 0.6 %collective-permute-start = (f32[4,64,256]{2,1,0:T(8,128)}, f32[4,64,256]{2,1,0:T(8,128)S(1)}, u32[]{:S(2)}, u32[]{:S(2)}) collective-permute-start(f32[4,64,256]{2,1,0:T(8,128)} %source.2), channel_id=1, source_target_pairs={{0,1},{1,0},{2,3},{3,2},{4,5},{5,4},{6,7},{7,6},{8,9},{9,8},{10,11... | collective-permute-start | bytes 786440 | tf_op jit(solution)/shard_map/ppermute | solution.py:285
  1.2 0.1 collective-permute-start.1
  1.3 0.9 %copy-done.2 = f32[4,64,256]{2,1,0:T(8,128)S(1)} copy-done((f32[4,64,256]{2,1,0:T(8,128)S(1)}, f32[4,64,256]{2,1,0:T(8,128)}, u32[]{:S(2)}) %copy-start.2) | copy-done | bytes 262168
  2.2 0.0 copy-start.3
  2.2 0.3 collective-permute-done.far
  2.6 0.7 %collective-permute-start.2 = (f32[64,512]{1,0:T(8,128)S(1)}, f32[64,512]{1,0:T(8,128)S(1)}, u32[]{:S(2)}, u32[]{:S(2)}) collective-permute-start(f32[64,512]{1,0:T(8,128)S(1)} %get-tuple-element.10), channel_id=1, source_target_pairs={{1,8},{8,1},{9,16},{16,9},{17,24},{24,17},{3,10},{10,3},{11,18},{1... | collective-permute-start | bytes 393224 | tf_op jit(solution)/shard_map/ppermute | solution.py:285
  3.3 0.0 copy-start
  3.3 0.0 copy-start.1
  3.3 4.9 %collective-permute-start.3 = (f32[4,512]{1,0:T(4,128)S(1)}, f32[4,512]{1,0:T(4,128)S(1)}, u32[]{:S(2)}, u32[]{:S(2)}) collective-permute-start(f32[4,512]{1,0:T(4,128)S(1)} %get-tuple-element.11), channel_id=1, source_target_pairs={{0,2},{2,0},{4,6},{6,4},{3,5},{5,3},{8,10},{10,8},{12,14},{14,12},... | collective-permute-start | bytes 24584 | tf_op jit(solution)/shard_map/ppermute | solution.py:313
  8.2 1.6 %collective-permute-done.3.mine = f32[4,512]{1,0:T(4,128)S(1)} collective-permute-done((f32[4,512]{1,0:T(4,128)S(1)}, f32[4,512]{1,0:T(4,128)S(1)}, u32[]{:S(2)}, u32[]{:S(2)}) %collective-permute-start.3) | collective-permute-done | bytes 8224 | tf_op jit(solution)/shard_map/ppermute | solution.py:313
  9.8 0.0 collective-permute-start.4
  9.8 1.1 %collective-permute-done.4.theirs = f32[4,512]{1,0:T(4,128)S(1)} collective-permute-done((f32[4,512]{1,0:T(4,128)S(1)}, f32[4,512]{1,0:T(4,128)S(1)}, u32[]{:S(2)}, u32[]{:S(2)}) %collective-permute-start.4) | collective-permute-done | bytes 8224 | tf_op jit(solution)/shard_map/ppermute | solution.py:285
  11.0 1.2 %shard_map.80 = (f32[2,64,256]{2,1,0:T(8,128)S(1)}, f32[2,64,256]{2,1,0:T(8,128)S(1)}, f32[256,128]{1,0:T(8,128)}) custom-call(f32[4,64,256]{2,1,0:T(8,128)S(1)} %shard_map.77.rho, f32[4,64,256]{2,1,0:T(8,128)S(1)} %collective-permute-done.far, f32[4,64,256]{2,1,0:T(8,128)S(1)} %shard_map.78.kappa, f32[4,64,256]{2,1,0:T(8,128)S(1)} %collective-permute-done.1.far_kappa, ...), custom_call_target="tpu_custom_call" | custom-call | bytes 1048576 | tf_op jit(solution)/shard_map/pallas_call | solution.py:327
  12.2 7.8 %all-to-all-start = ((f32[32,8,128]{2,1,0:T(8,128)}), f32[32,8,128]{2,1,0:T(8,128)S(1)}, u32[]{:S(2)}, u32[]{:S(2)}) async-start(f32[32,8,128]{2,1,0:T(8,128)} %bitcast), calls=%async_computation | async-start | bytes 262144 | tf_op jit(solution)/shard_map/all_to_all | solution.py:338
  20.0 1.9 %shard_map.82 = (bf16[512,256]{1,0:T(8,128)(2,1)S(1)}, bf16[512,256]{1,0:T(8,128)(2,1)S(1)}, f32[2,256]{1,0:T(2,128)S(1)}) custom-call(f32[384,128]{1,0:T(8,128)S(1)} %copy-done.4, f32[4,256]{1,0:T(4,128)S(1)} %copy-done.5), custom_call_target="tpu_custom_call" | custom-call | flops 10000000 | bytes 1048576 | tf_op jit(solution)/shard_map/pallas_call | solution.py:318
  22.0 6.2 %all-to-all-done.spec_ref = f32[32,8,128]{2,1,0:T(8,128)S(1)} async-done(((f32[32,8,128]{2,1,0:T(8,128)}), f32[32,8,128]{2,1,0:T(8,128)S(1)}, u32[]{:S(2)}, u32[]{:S(2)}) %all-to-all-start) | async-done | bytes 131104 | tf_op jit(solution)/shard_map/all_to_all | solution.py:338
  28.2 1.5 %shard_map.83 = f32[32,8,128]{2,1,0:T(8,128)} custom-call(f32[32,8,128]{2,1,0:T(8,128)S(1)} %all-to-all-done.spec_ref, bf16[512,256]{1,0:T(8,128)(2,1)S(1)} %get-tuple-element.15.high_ref, bf16[512,256]{1,0:T(8,128)(2,1)S(1)} %get-tuple-element.16.low_ref, f32[2,256]{1,0:T(2,128)S(1)} %get-tuple-element.17.extra_ref), custom_call_target="tpu_custom_call" | custom-call | bytes 1048576 | tf_op jit(solution)/shard_map/pallas_call | solution.py:340
  29.8 2.6 %all-to-all-start.1 = ((f32[32,8,128]{2,1,0:T(8,128)}), f32[32,8,128]{2,1,0:T(8,128)S(1)}, u32[]{:S(2)}, u32[]{:S(2)}) async-start(f32[32,8,128]{2,1,0:T(8,128)} %shard_map.83), calls=%async_computation.1 | async-start | bytes 262144 | tf_op jit(solution)/shard_map/all_to_all | solution.py:346
  32.3 0.2 collective-permute-start.5
  32.5 8.0 %all-to-all-done.1 = f32[32,8,128]{2,1,0:T(8,128)S(1)} async-done(((f32[32,8,128]{2,1,0:T(8,128)}), f32[32,8,128]{2,1,0:T(8,128)S(1)}, u32[]{:S(2)}, u32[]{:S(2)}) %all-to-all-start.1) | async-done | bytes 131104 | tf_op jit(solution)/shard_map/all_to_all | solution.py:346
  40.6 0.2 collective-permute-start.6
  40.8 0.7 %shard_map.81 = f32[4,64,256]{2,1,0:T(8,128)} custom-call(f32[2,64,256]{2,1,0:T(8,128)S(1)} %get-tuple-element.12.keep, f32[2,64,256]{2,1,0:T(8,128)S(1)} %collective-permute-done.5.back), custom_call_target="tpu_custom_call" | custom-call | bytes 1048576 | tf_op jit(solution)/shard_map/pallas_call | solution.py:348
  41.5 0.4 collective-permute-done.6.far
  41.9 1.0 %shard_map.84 = f32[4,64,256]{2,1,0:T(8,128)} custom-call(f32[256,128]{1,0:T(8,128)S(1)} %bitcast.3, f32[256,128]{1,0:T(8,128)S(1)} %collective-permute-done.6.far, bf16[256,512]{1,0:T(8,128)(2,1)S(1)} %copy-done.1, bf16[256,512]{1,0:T(8,128)(2,1)S(1)} %copy-done), custom_call_target="tpu_custom_call" | custom-call | bytes 1048576 | tf_op jit(solution)/shard_map/pallas_call | solution.py:349
  (14 shorter events, 0.1 us)
Async XLA Ops:
  0.6 1.9 %collective-permute-start = (f32[4,64,256]{2,1,0:T(8,128)}, f32[4,64,256]{2,1,0:T(8,128)S(1)}, u32[]{:S(2)}, u32[]{:S(2)}) collective-permute-start(f32[4,64,256]{2,1,0:T(8,128)} %source.2), channel_id=1, source_target_pairs={{0,1},{1,0},{2,3},{3,2},{4,5},{5,4},{6,7},{7,6},{8,9},{9,8},{10,11... | collective-permute-start | bytes 786440 | tf_op jit(solution)/shard_map/ppermute | solution.py:285
  1.2 8.6 %collective-permute-start.1 = (f32[4,64,256]{2,1,0:T(8,128)}, f32[4,64,256]{2,1,0:T(8,128)S(1)}, u32[]{:S(2)}, u32[]{:S(2)}) collective-permute-start(f32[4,64,256]{2,1,0:T(8,128)} %source.3), channel_id=1, source_target_pairs={{0,1},{1,0},{2,3},{3,2},{4,5},{5,4},{6,7},{7,6},{8,9},{9,8},{10,11... | collective-permute-start | bytes 786440 | tf_op jit(solution)/shard_map/ppermute | solution.py:285
  1.3 0.9 %copy-start.2 = (f32[4,64,256]{2,1,0:T(8,128)S(1)}, f32[4,64,256]{2,1,0:T(8,128)}, u32[]{:S(2)}) copy-start(f32[4,64,256]{2,1,0:T(8,128)} %source.2) | copy-start | bytes 786436
  2.2 7.6 %copy-start.3 = (f32[4,64,256]{2,1,0:T(8,128)S(1)}, f32[4,64,256]{2,1,0:T(8,128)}, u32[]{:S(2)}) copy-start(f32[4,64,256]{2,1,0:T(8,128)} %source.3) | copy-start | bytes 786436
  2.6 8.4 %collective-permute-start.2 = (f32[64,512]{1,0:T(8,128)S(1)}, f32[64,512]{1,0:T(8,128)S(1)}, u32[]{:S(2)}, u32[]{:S(2)}) collective-permute-start(f32[64,512]{1,0:T(8,128)S(1)} %get-tuple-element.10), channel_id=1, source_target_pairs={{1,8},{8,1},{9,16},{16,9},{17,24},{24,17},{3,10},{10,3},{11,18},{1... | collective-permute-start | bytes 393224 | tf_op jit(solution)/shard_map/ppermute | solution.py:285
  3.3 7.7 %copy-start = (bf16[256,512]{1,0:T(8,128)(2,1)S(1)}, bf16[256,512]{1,0:T(8,128)(2,1)}, u32[]{:S(2)}) copy-start(bf16[256,512]{1,0:T(8,128)(2,1)} %constant.11.clone.w_low) | copy-start | bytes 786436
  3.3 7.7 %copy-start.1 = (bf16[256,512]{1,0:T(8,128)(2,1)S(1)}, bf16[256,512]{1,0:T(8,128)(2,1)}, u32[]{:S(2)}) copy-start(bf16[256,512]{1,0:T(8,128)(2,1)} %constant.10.clone.w_high) | copy-start | bytes 786436
  3.3 6.5 %collective-permute-start.3 = (f32[4,512]{1,0:T(4,128)S(1)}, f32[4,512]{1,0:T(4,128)S(1)}, u32[]{:S(2)}, u32[]{:S(2)}) collective-permute-start(f32[4,512]{1,0:T(4,128)S(1)} %get-tuple-element.11), channel_id=1, source_target_pairs={{0,2},{2,0},{4,6},{6,4},{3,5},{5,3},{8,10},{10,8},{12,14},{14,12},... | collective-permute-start | bytes 24584 | tf_op jit(solution)/shard_map/ppermute | solution.py:313
  9.8 1.2 %collective-permute-start.4 = (f32[4,512]{1,0:T(4,128)S(1)}, f32[4,512]{1,0:T(4,128)S(1)}, u32[]{:S(2)}, u32[]{:S(2)}) collective-permute-start(f32[4,512]{1,0:T(4,128)S(1)} %collective-permute-done.3.mine), channel_id=1, source_target_pairs={{0,1},{1,0},{2,3},{3,2},{4,5},{5,4},{6,7},{7,6},{8,9},{9,8},{10,11... | collective-permute-start | bytes 24584 | tf_op jit(solution)/shard_map/ppermute | solution.py:285
  12.2 7.8 %copy-start.4 = (f32[384,128]{1,0:T(8,128)S(1)}, f32[384,128]{1,0:T(8,128)}, u32[]{:S(2)}) copy-start(f32[384,128]{1,0:T(8,128)} %constant.9.clone.coef_ref) | copy-start | bytes 589828
  12.2 7.8 %copy-start.5 = (f32[4,256]{1,0:T(4,128)S(1)}, f32[4,256]{1,0:T(4,128)}, u32[]{:S(2)}) copy-start(f32[4,256]{1,0:T(4,128)} %constant.8.clone.trig_ref) | copy-start | bytes 12292
  12.2 16.0 %all-to-all-start = ((f32[32,8,128]{2,1,0:T(8,128)}), f32[32,8,128]{2,1,0:T(8,128)S(1)}, u32[]{:S(2)}, u32[]{:S(2)}) async-start(f32[32,8,128]{2,1,0:T(8,128)} %bitcast), calls=%async_computation | async-start | bytes 262144 | tf_op jit(solution)/shard_map/all_to_all | solution.py:338
  29.8 10.8 %all-to-all-start.1 = ((f32[32,8,128]{2,1,0:T(8,128)}), f32[32,8,128]{2,1,0:T(8,128)S(1)}, u32[]{:S(2)}, u32[]{:S(2)}) async-start(f32[32,8,128]{2,1,0:T(8,128)} %shard_map.83), calls=%async_computation.1 | async-start | bytes 262144 | tf_op jit(solution)/shard_map/all_to_all | solution.py:346
  32.3 8.4 %collective-permute-start.5 = (f32[2,64,256]{2,1,0:T(8,128)S(1)}, f32[2,64,256]{2,1,0:T(8,128)S(1)}, u32[]{:S(2)}, u32[]{:S(2)}) collective-permute-start(f32[2,64,256]{2,1,0:T(8,128)S(1)} %get-tuple-element.13), channel_id=1, source_target_pairs={{0,1},{1,0},{2,3},{3,2},{4,5},{5,4},{6,7},{7,6},{8,9},{9,8},{10,11... | collective-permute-start | bytes 393224 | tf_op jit(solution)/shard_map/ppermute | solution.py:285
  40.6 1.3 %collective-permute-start.6 = (f32[256,128]{1,0:T(8,128)S(1)}, f32[256,128]{1,0:T(8,128)S(1)}, u32[]{:S(2)}, u32[]{:S(2)}) collective-permute-start(f32[256,128]{1,0:T(8,128)S(1)} %bitcast.2), channel_id=1, source_target_pairs={{0,1},{1,0},{2,3},{3,2},{4,5},{5,4},{6,7},{7,6},{8,9},{9,8},{10,11... | collective-permute-start | bytes 393224 | tf_op jit(solution)/shard_map/ppermute | solution.py:285

commit v5 on v4

--- a/solution.py
+++ b/solution.py
@@ -285,13 +285,26 @@
     return lax.ppermute(value, axes, pairs)
 
 
-def polar_pairs(n_ta, n_pa):
+def halo_pairs(sizes, partner, spare):
+    _, n_ta, n_pa = sizes
+    number = lambda place: (place[0] * n_ta + place[1]) * n_pa + place[2]
+    inside = lambda place: all(0 <= x < n for x, n in zip(place, sizes))
     pairs = []
-    for core in range(2):
-        for t in range(core, n_ta - 1, 2):
-            here, there = t * n_pa + core, (t + 1) * n_pa + core
-            pairs += [(here, there), (there, here)]
+    for place in np.ndindex(*sizes):
+        other = partner(*place)
+        if not inside(other):
+            other = spare(*place)
+        if inside(other):
+            pairs.append((number(place), number(other)))
     return pairs
+
+
+def radial_partner(row, ta, pa):
+    return (row + 1, ta, 0) if pa == 1 else (row - 1, ta, 1)
+
+
+def polar_partner(row, ta, pa):
+    return (row, ta + 1 if ta % 2 == pa else ta - 1, pa)
 
 
 def shards(sizes, density, kappa):
@@ -310,8 +323,10 @@
     shell, ends = call(
         pack_kernel, (((polar, azim_total), F32), ((rows, azim_total), F32)), [VMEM] * 2
     )(density, far)
-    mine = lax.ppermute(ends, ("ta", "pa"), polar_pairs(n_ta, n_pa))
-    shell = pair_swap(shell, ("row", "pa"), n_row * n_pa, 1)
+    pairs = halo_pairs(sizes, polar_partner, lambda row, ta, pa: (row ^ 1, ta, pa))
+    mine = lax.ppermute(ends, AXES, pairs)
+    pairs = halo_pairs(sizes, radial_partner, lambda row, ta, pa: (row, ta ^ 1, pa))
+    shell = lax.ppermute(shell, AXES, pairs)
     theirs = swap(mine)
 
     small = small_table(polar_total, azim_total)

time: 43.2 us -> 39.6 us (0.917)
  starting transfers between devices: 17 us -> 11.5 us
  waiting for transfers between devices: 17.7 us -> 19.7 us
    all_to_all x1, starting transfers between devices: 7.8 us -> 4.86 us  [shards(): spec = spread(spec.reshape(owners, 2 * per, cells))]
    ppermute x1 -> x2, waiting for transfers between devices: 1.61 us -> 3.55 us  [the longest x1 3.55 us: shards(): mine = lax.ppermute(ends, AXES, pairs)]
    ppermute x1 -> x2, starting transfers between devices: 4.89 us -> 3.01 us  [the longest x1 2.91 us: shards(): shell = lax.ppermute(shell, AXES, pairs)]
    ppermute x6 -> x5, starting transfers between devices: 1.7 us -> 1.03 us  [pair_swap(): return lax.ppermute(value, axes, pairs)]
    ppermute x6 -> x5, waiting for transfers between devices: 1.85 us -> 1.85 us  [pair_swap(): return lax.ppermute(value, axes, pairs)]
  transfers between devices with their start and end apart: 9 -> 9, of which waited for: 6 -> 6; matrix products, arithmetic and copies ran while one was open for 0% -> 0% of each run, Pallas kernels for 6% -> 7%
where the time goes in v5:
time: 39.6 us; the launch traced here: 39.3 us
  waiting for transfers between devices  19.7 us (50%)
  starting transfers between devices  11.5 us (29%)
  Pallas kernels  6.51 us (16%)
  local copies, waits for them, and re-layouts  0.97 us (2%)
  between operations  0.71 us (2%)
    all_to_all x1, waiting for transfers between devices, shards(): spec = spread(spec).reshape(2 * DEGREES, cells)  8.03 us
    all_to_all x1, waiting for transfers between devices, shards(): spec = spread(spec.reshape(owners, 2 * per, cells))  6.23 us
    all_to_all x1, starting transfers between devices, shards(): spec = spread(spec.reshape(owners, 2 * per, cells))  4.86 us
    ppermute x1, waiting for transfers between devices, shards(): mine = lax.ppermute(ends, AXES, pairs)  3.55 us
    ppermute x1, starting transfers between devices, shards(): shell = lax.ppermute(shell, AXES, pairs)  2.91 us
    all_to_all x1, starting transfers between devices, shards(): spec = spread(spec).reshape(2 * DEGREES, cells)  2.58 us
    pallas_call x1, Pallas kernels, shards(): call(functools.partial(table_kernel, sizes), (((per * DEGREES, polar_tota...  1.95 us
    ppermute x5, waiting for transfers between devices, pair_swap(): return lax.ppermute(value, axes, pairs)  1.85 us
  transfers between devices with their start and end apart: 9, of which 6 were waited for; matrix products, arithmetic and copies ran while one was open for 0% of the time, Pallas kernels for 7%

profile of v5, /device:TPU:0, one launch (start us, length us, event | category | flops | bytes accessed | tf_op | source)
XLA Modules:
  0.0 39.3 jit_solution(4564995695287913286)
XLA Ops:
  0.6 0.6 %collective-permute-start = (f32[4,64,256]{2,1,0:T(8,128)}, f32[4,64,256]{2,1,0:T(8,128)S(1)}, u32[]{:S(2)}, u32[]{:S(2)}) collective-permute-start(f32[4,64,256]{2,1,0:T(8,128)} %source.2), channel_id=1, source_target_pairs={{0,1},{1,0},{2,3},{3,2},{4,5},{5,4},{6,7},{7,6},{8,9},{9,8},{10,11... | collective-permute-start | bytes 786440 | tf_op jit(solution)/shard_map/ppermute | solution.py:285
  1.2 0.1 collective-permute-start.1
  1.3 0.9 %copy-done.2 = f32[4,64,256]{2,1,0:T(8,128)S(1)} copy-done((f32[4,64,256]{2,1,0:T(8,128)S(1)}, f32[4,64,256]{2,1,0:T(8,128)}, u32[]{:S(2)}) %copy-start.2) | copy-done | bytes 262168
  2.2 0.0 copy-start.3
  2.2 0.3 collective-permute-done.far
  2.6 2.9 %collective-permute-start.2 = (f32[64,512]{1,0:T(8,128)S(1)}, f32[64,512]{1,0:T(8,128)S(1)}, u32[]{:S(2)}, u32[]{:S(2)}) collective-permute-start(f32[64,512]{1,0:T(8,128)S(1)} %get-tuple-element.10), channel_id=1, source_target_pairs={{0,2},{1,8},{2,0},{3,10},{4,6},{5,12},{6,4},{7,14},{8,1},{9,16},{1... | collective-permute-start | bytes 393224 | tf_op jit(solution)/shard_map/ppermute | solution.py:329
  5.5 0.1 collective-permute-start.3
  5.6 3.6 %collective-permute-done.3.mine = f32[4,512]{1,0:T(4,128)S(1)} collective-permute-done((f32[4,512]{1,0:T(4,128)S(1)}, f32[4,512]{1,0:T(4,128)S(1)}, u32[]{:S(2)}, u32[]{:S(2)}) %collective-permute-start.3) | collective-permute-done | bytes 8224 | tf_op jit(solution)/shard_map/ppermute | solution.py:327
  9.2 0.0 collective-permute-start.4
  9.2 1.1 %collective-permute-done.4.theirs = f32[4,512]{1,0:T(4,128)S(1)} collective-permute-done((f32[4,512]{1,0:T(4,128)S(1)}, f32[4,512]{1,0:T(4,128)S(1)}, u32[]{:S(2)}, u32[]{:S(2)}) %collective-permute-start.4) | collective-permute-done | bytes 8224 | tf_op jit(solution)/shard_map/ppermute | solution.py:285
  10.3 0.0 collective-permute-done.2.shell
  10.3 1.2 %shard_map.80 = (f32[2,64,256]{2,1,0:T(8,128)S(1)}, f32[2,64,256]{2,1,0:T(8,128)S(1)}, f32[256,128]{1,0:T(8,128)}) custom-call(f32[4,64,256]{2,1,0:T(8,128)S(1)} %shard_map.77.rho, f32[4,64,256]{2,1,0:T(8,128)S(1)} %collective-permute-done.far, f32[4,64,256]{2,1,0:T(8,128)S(1)} %shard_map.78.kappa, f32[4,64,256]{2,1,0:T(8,128)S(1)} %collective-permute-done.1.far_kappa, ...), custom_call_target="tpu_custom_call" | custom-call | bytes 1048576 | tf_op jit(solution)/shard_map/pallas_call | solution.py:342
  11.6 4.9 %all-to-all-start = ((f32[32,8,128]{2,1,0:T(8,128)}), f32[32,8,128]{2,1,0:T(8,128)S(1)}, u32[]{:S(2)}, u32[]{:S(2)}) async-start(f32[32,8,128]{2,1,0:T(8,128)} %bitcast), calls=%async_computation | async-start | bytes 262144 | tf_op jit(solution)/shard_map/all_to_all | solution.py:353
  16.5 1.9 %shard_map.82 = (bf16[512,256]{1,0:T(8,128)(2,1)S(1)}, bf16[512,256]{1,0:T(8,128)(2,1)S(1)}, f32[2,256]{1,0:T(2,128)S(1)}) custom-call(f32[384,128]{1,0:T(8,128)S(1)} %copy-done.4, f32[4,256]{1,0:T(4,128)S(1)} %copy-done.5), custom_call_target="tpu_custom_call" | custom-call | flops 10000000 | bytes 1048576 | tf_op jit(solution)/shard_map/pallas_call | solution.py:333
  18.4 6.2 %all-to-all-done.spec_ref = f32[32,8,128]{2,1,0:T(8,128)S(1)} async-done(((f32[32,8,128]{2,1,0:T(8,128)}), f32[32,8,128]{2,1,0:T(8,128)S(1)}, u32[]{:S(2)}, u32[]{:S(2)}) %all-to-all-start) | async-done | bytes 131104 | tf_op jit(solution)/shard_map/all_to_all | solution.py:353
  24.6 1.5 %shard_map.83 = f32[32,8,128]{2,1,0:T(8,128)} custom-call(f32[32,8,128]{2,1,0:T(8,128)S(1)} %all-to-all-done.spec_ref, bf16[512,256]{1,0:T(8,128)(2,1)S(1)} %get-tuple-element.15.high_ref, bf16[512,256]{1,0:T(8,128)(2,1)S(1)} %get-tuple-element.16.low_ref, f32[2,256]{1,0:T(2,128)S(1)} %get-tuple-element.17.extra_ref), custom_call_target="tpu_custom_call" | custom-call | bytes 1048576 | tf_op jit(solution)/shard_map/pallas_call | solution.py:355
  26.2 2.6 %all-to-all-start.1 = ((f32[32,8,128]{2,1,0:T(8,128)}), f32[32,8,128]{2,1,0:T(8,128)S(1)}, u32[]{:S(2)}, u32[]{:S(2)}) async-start(f32[32,8,128]{2,1,0:T(8,128)} %shard_map.83), calls=%async_computation.1 | async-start | bytes 262144 | tf_op jit(solution)/shard_map/all_to_all | solution.py:361
  28.8 0.2 collective-permute-start.5
  28.9 8.0 %all-to-all-done.1 = f32[32,8,128]{2,1,0:T(8,128)S(1)} async-done(((f32[32,8,128]{2,1,0:T(8,128)}), f32[32,8,128]{2,1,0:T(8,128)S(1)}, u32[]{:S(2)}, u32[]{:S(2)}) %all-to-all-start.1) | async-done | bytes 131104 | tf_op jit(solution)/shard_map/all_to_all | solution.py:361
  37.0 0.2 collective-permute-start.6
  37.2 0.0 collective-permute-done.5.back
  37.2 0.7 %shard_map.81 = f32[4,64,256]{2,1,0:T(8,128)} custom-call(f32[2,64,256]{2,1,0:T(8,128)S(1)} %get-tuple-element.12.keep, f32[2,64,256]{2,1,0:T(8,128)S(1)} %collective-permute-done.5.back), custom_call_target="tpu_custom_call" | custom-call | bytes 1048576 | tf_op jit(solution)/shard_map/pallas_call | solution.py:363
  37.9 0.4 %collective-permute-done.6.far = f32[256,128]{1,0:T(8,128)S(1)} collective-permute-done((f32[256,128]{1,0:T(8,128)S(1)}, f32[256,128]{1,0:T(8,128)S(1)}, u32[]{:S(2)}, u32[]{:S(2)}) %collective-permute-start.6) | collective-permute-done | bytes 131104 | tf_op jit(solution)/shard_map/ppermute | solution.py:285
  38.3 1.0 %shard_map.84 = f32[4,64,256]{2,1,0:T(8,128)} custom-call(f32[256,128]{1,0:T(8,128)S(1)} %bitcast.3, f32[256,128]{1,0:T(8,128)S(1)} %collective-permute-done.6.far, bf16[256,512]{1,0:T(8,128)(2,1)S(1)} %copy-done.1, bf16[256,512]{1,0:T(8,128)(2,1)S(1)} %copy-done), custom_call_target="tpu_custom_call" | custom-call | bytes 1048576 | tf_op jit(solution)/shard_map/pallas_call | solution.py:364
  (14 shorter events, 0.1 us)
Async XLA Ops:
  0.6 1.9 %collective-permute-start = (f32[4,64,256]{2,1,0:T(8,128)}, f32[4,64,256]{2,1,0:T(8,128)S(1)}, u32[]{:S(2)}, u32[]{:S(2)}) collective-permute-start(f32[4,64,256]{2,1,0:T(8,128)} %source.2), channel_id=1, source_target_pairs={{0,1},{1,0},{2,3},{3,2},{4,5},{5,4},{6,7},{7,6},{8,9},{9,8},{10,11... | collective-permute-start | bytes 786440 | tf_op jit(solution)/shard_map/ppermute | solution.py:285
  1.2 8.0 %collective-permute-start.1 = (f32[4,64,256]{2,1,0:T(8,128)}, f32[4,64,256]{2,1,0:T(8,128)S(1)}, u32[]{:S(2)}, u32[]{:S(2)}) collective-permute-start(f32[4,64,256]{2,1,0:T(8,128)} %source.3), channel_id=1, source_target_pairs={{0,1},{1,0},{2,3},{3,2},{4,5},{5,4},{6,7},{7,6},{8,9},{9,8},{10,11... | collective-permute-start | bytes 786440 | tf_op jit(solution)/shard_map/ppermute | solution.py:285
  1.3 0.9 %copy-start.2 = (f32[4,64,256]{2,1,0:T(8,128)S(1)}, f32[4,64,256]{2,1,0:T(8,128)}, u32[]{:S(2)}) copy-start(f32[4,64,256]{2,1,0:T(8,128)} %source.2) | copy-start | bytes 786436
  2.2 6.9 %copy-start.3 = (f32[4,64,256]{2,1,0:T(8,128)S(1)}, f32[4,64,256]{2,1,0:T(8,128)}, u32[]{:S(2)}) copy-start(f32[4,64,256]{2,1,0:T(8,128)} %source.3) | copy-start | bytes 786436
  2.6 7.7 %collective-permute-start.2 = (f32[64,512]{1,0:T(8,128)S(1)}, f32[64,512]{1,0:T(8,128)S(1)}, u32[]{:S(2)}, u32[]{:S(2)}) collective-permute-start(f32[64,512]{1,0:T(8,128)S(1)} %get-tuple-element.10), channel_id=1, source_target_pairs={{0,2},{1,8},{2,0},{3,10},{4,6},{5,12},{6,4},{7,14},{8,1},{9,16},{1... | collective-permute-start | bytes 393224 | tf_op jit(solution)/shard_map/ppermute | solution.py:329
  5.5 4.8 %copy-start = (bf16[256,512]{1,0:T(8,128)(2,1)S(1)}, bf16[256,512]{1,0:T(8,128)(2,1)}, u32[]{:S(2)}) copy-start(bf16[256,512]{1,0:T(8,128)(2,1)} %constant.11.clone.w_low) | copy-start | bytes 786436
  5.5 4.8 %copy-start.1 = (bf16[256,512]{1,0:T(8,128)(2,1)S(1)}, bf16[256,512]{1,0:T(8,128)(2,1)}, u32[]{:S(2)}) copy-start(bf16[256,512]{1,0:T(8,128)(2,1)} %constant.10.clone.w_high) | copy-start | bytes 786436
  5.5 3.7 %collective-permute-start.3 = (f32[4,512]{1,0:T(4,128)S(1)}, f32[4,512]{1,0:T(4,128)S(1)}, u32[]{:S(2)}, u32[]{:S(2)}) collective-permute-start(f32[4,512]{1,0:T(4,128)S(1)} %get-tuple-element.11), channel_id=1, source_target_pairs={{0,2},{1,9},{2,0},{3,5},{4,6},{5,3},{6,4},{7,15},{8,10},{9,1},{10,... | collective-permute-start | bytes 24584 | tf_op jit(solution)/shard_map/ppermute | solution.py:327
  9.2 1.2 %collective-permute-start.4 = (f32[4,512]{1,0:T(4,128)S(1)}, f32[4,512]{1,0:T(4,128)S(1)}, u32[]{:S(2)}, u32[]{:S(2)}) collective-permute-start(f32[4,512]{1,0:T(4,128)S(1)} %collective-permute-done.3.mine), channel_id=1, source_target_pairs={{0,1},{1,0},{2,3},{3,2},{4,5},{5,4},{6,7},{7,6},{8,9},{9,8},{10,11... | collective-permute-start | bytes 24584 | tf_op jit(solution)/shard_map/ppermute | solution.py:285
  11.6 4.9 %copy-start.4 = (f32[384,128]{1,0:T(8,128)S(1)}, f32[384,128]{1,0:T(8,128)}, u32[]{:S(2)}) copy-start(f32[384,128]{1,0:T(8,128)} %constant.9.clone.coef_ref) | copy-start | bytes 589828
  11.6 4.9 %copy-start.5 = (f32[4,256]{1,0:T(4,128)S(1)}, f32[4,256]{1,0:T(4,128)}, u32[]{:S(2)}) copy-start(f32[4,256]{1,0:T(4,128)} %constant.8.clone.trig_ref) | copy-start | bytes 12292
  11.6 13.1 %all-to-all-start = ((f32[32,8,128]{2,1,0:T(8,128)}), f32[32,8,128]{2,1,0:T(8,128)S(1)}, u32[]{:S(2)}, u32[]{:S(2)}) async-start(f32[32,8,128]{2,1,0:T(8,128)} %bitcast), calls=%async_computation | async-start | bytes 262144 | tf_op jit(solution)/shard_map/all_to_all | solution.py:353
  26.2 10.8 %all-to-all-start.1 = ((f32[32,8,128]{2,1,0:T(8,128)}), f32[32,8,128]{2,1,0:T(8,128)S(1)}, u32[]{:S(2)}, u32[]{:S(2)}) async-start(f32[32,8,128]{2,1,0:T(8,128)} %shard_map.83), calls=%async_computation.1 | async-start | bytes 262144 | tf_op jit(solution)/shard_map/all_to_all | solution.py:361
  28.8 8.4 %collective-permute-start.5 = (f32[2,64,256]{2,1,0:T(8,128)S(1)}, f32[2,64,256]{2,1,0:T(8,128)S(1)}, u32[]{:S(2)}, u32[]{:S(2)}) collective-permute-start(f32[2,64,256]{2,1,0:T(8,128)S(1)} %get-tuple-element.13), channel_id=1, source_target_pairs={{0,1},{1,0},{2,3},{3,2},{4,5},{5,4},{6,7},{7,6},{8,9},{9,8},{10,11... | collective-permute-start | bytes 393224 | tf_op jit(solution)/shard_map/ppermute | solution.py:285
  37.0 1.3 %collective-permute-start.6 = (f32[256,128]{1,0:T(8,128)S(1)}, f32[256,128]{1,0:T(8,128)S(1)}, u32[]{:S(2)}, u32[]{:S(2)}) collective-permute-start(f32[256,128]{1,0:T(8,128)S(1)} %bitcast.2), channel_id=1, source_target_pairs={{0,1},{1,0},{2,3},{3,2},{4,5},{5,4},{6,7},{7,6},{8,9},{9,8},{10,11... | collective-permute-start | bytes 393224 | tf_op jit(solution)/shard_map/ppermute | solution.py:285

commit v6 on v5

--- a/solution.py
+++ b/solution.py
@@ -144,20 +144,14 @@
 
 
 def table_kernel(sizes, coef_ref, trig_ref, high_ref, low_ref, extra_ref, spread_ref, work):
-    per, degrees, polar = work.shape
+    per, degrees, north = work.shape
     extra_ref[...] = trig_ref[2:4, :]
     start = owner_of(sizes) * per
     lanes = 128
-    order = lax.broadcasted_iota(jnp.int32, (degrees, per * lanes), 0)
-    slot = lax.broadcasted_iota(jnp.int32, (degrees, per * lanes), 1) // lanes
-    pick = jnp.where(order == slot + start, 1.0, 0.0).astype(F32)
-    wide = lax.dot_general(
-        coef_ref[: 2 * degrees, :], pick, NN,
-        precision=lax.Precision.HIGHEST, preferred_element_type=F32,
-    )
+    near = pltpu.roll(coef_ref[: 2 * degrees, :], lanes - start, 1)
     for q in range(per):
-        spread_ref[q] = wide[:, q * lanes : (q + 1) * lanes]
-    parts = polar // lanes
+        spread_ref[q] = jnp.broadcast_to(near[:, q : q + 1], (2 * degrees, lanes))
+    parts = north // lanes
     cut = lambda row, k: jnp.broadcast_to(trig_ref[row : row + 1, k * lanes : (k + 1) * lanes], (8, lanes))
     cos_t = [cut(0, k) for k in range(parts)]
     sin_t = [cut(1, k) for k in range(parts)]
@@ -181,8 +175,8 @@
                 seed = l == start + q
                 line = []
                 for k in range(parts):
-                    new = (a * cos_t[k]) * prev[q][k] - ab * older[q][k]
-                    new = jnp.where(seed, sect[k], new)
+                    rest = jnp.where(seed, sect[k], 0.0) - ab * older[q][k]
+                    new = (a * cos_t[k]) * prev[q][k] + rest
                     tiles[q][k] = jnp.where(sub == inner, new, tiles[q][k])
                     line.append(new)
                 fresh.append(line)
@@ -194,9 +188,14 @@
 
     zero = [[jnp.zeros((8, lanes), F32)] * parts for _ in range(per)]
     lax.fori_loop(0, degrees // 8, block, ([jnp.ones((8, lanes), F32)] * parts, zero, zero))
-    for q in range(per):
-        at = pl.ds(q * degrees, degrees)
-        high_ref[at, :], low_ref[at, :] = split(work[q])
+    square = lambda d: lax.broadcasted_iota(jnp.int32, (north, north), d)
+    mirror = jnp.where(square(0) + square(1) == north - 1, 1.0, 0.0).astype(BF16)
+    line = lax.broadcasted_iota(jnp.int32, (per * degrees, north), 0)
+    sign = jnp.where((line + line // degrees + start) % 2 == 0, 1.0, -1.0)
+    for piece, ref in zip(split(work[...].reshape(per * degrees, north)), (high_ref, low_ref)):
+        ref[:, :north] = piece
+        flipped = lax.dot_general(piece, mirror, NN, preferred_element_type=F32)
+        ref[:, north:] = (sign * flipped).astype(BF16)
 
 
 def solve_kernel(sizes, rows, polar, spec_ref, high_ref, low_ref, extra_ref, out_ref, work_ref):
@@ -334,7 +333,7 @@
         functools.partial(table_kernel, sizes),
         (((per * DEGREES, polar_total), BF16),) * 2 + (((2, polar_total), F32),),
         [VMEM] * 2,
-        [pltpu.VMEM((per, 2 * DEGREES, 128), F32), pltpu.VMEM((per, DEGREES, polar_total), F32)],
+        [pltpu.VMEM((per, 2 * DEGREES, 128), F32), pltpu.VMEM((per, DEGREES, polar_total // 2), F32)],
         flops=10**7,
     )(recursion_table(), small)
 

time: 39.6 us -> 39.6 us (level)
  waiting for transfers between devices: 19.7 us -> 20.3 us
  Pallas kernels: 6.51 us -> 5.91 us
    all_to_all x1, waiting for transfers between devices: 6.23 us -> 6.83 us  [shards(): spec = spread(spec.reshape(owners, 2 * per, cells))]
    pallas_call x1, Pallas kernels: 1.95 us -> 1.35 us  [shards(): call(functools.partial(table_kernel, sizes), (((per * DEGREES, polar_tota...]
  transfers between devices with their start and end apart: 9 -> 9, of which waited for: 6 -> 6; matrix products, arithmetic and copies ran while one was open for 0% -> 0% of each run, Pallas kernels for 7% -> 5%
where the time goes in v6:
time: 39.6 us; the launch traced here: 39.3 us
  waiting for transfers between devices  20.3 us (51%)
  starting transfers between devices  11.5 us (29%)
  Pallas kernels  5.91 us (15%)
  local copies, waits for them, and re-layouts  0.97 us (2%)
  between operations  0.71 us (2%)
    all_to_all x1, waiting for transfers between devices, shards(): spec = spread(spec).reshape(2 * DEGREES, cells)  8.03 us
    all_to_all x1, waiting for transfers between devices, shards(): spec = spread(spec.reshape(owners, 2 * per, cells))  6.83 us
    all_to_all x1, starting transfers between devices, shards(): spec = spread(spec.reshape(owners, 2 * per, cells))  4.86 us
    ppermute x1, waiting for transfers between devices, shards(): mine = lax.ppermute(ends, AXES, pairs)  3.55 us
    ppermute x1, starting transfers between devices, shards(): shell = lax.ppermute(shell, AXES, pairs)  2.91 us
    all_to_all x1, starting transfers between devices, shards(): spec = spread(spec).reshape(2 * DEGREES, cells)  2.58 us
    ppermute x5, waiting for transfers between devices, pair_swap(): return lax.ppermute(value, axes, pairs)  1.85 us
    pallas_call x1, Pallas kernels, shards(): call(functools.partial(solve_kernel, sizes, rows, polar), ((spec.shape, F...  1.53 us
  transfers between devices with their start and end apart: 9, of which 6 were waited for; matrix products, arithmetic and copies ran while one was open for 0% of the time, Pallas kernels for 5%

profile of v6, /device:TPU:0, one launch (start us, length us, event | category | flops | bytes accessed | tf_op | source)
XLA Modules:
  0.0 39.3 jit_solution(3417433465436383566)
XLA Ops:
  0.6 0.6 %collective-permute-start = (f32[4,64,256]{2,1,0:T(8,128)}, f32[4,64,256]{2,1,0:T(8,128)S(1)}, u32[]{:S(2)}, u32[]{:S(2)}) collective-permute-start(f32[4,64,256]{2,1,0:T(8,128)} %source.2), channel_id=1, source_target_pairs={{0,1},{1,0},{2,3},{3,2},{4,5},{5,4},{6,7},{7,6},{8,9},{9,8},{10,11... | collective-permute-start | bytes 786440 | tf_op jit(solution)/shard_map/ppermute | solution.py:284
  1.2 0.1 collective-permute-start.1
  1.3 0.9 %copy-done.2 = f32[4,64,256]{2,1,0:T(8,128)S(1)} copy-done((f32[4,64,256]{2,1,0:T(8,128)S(1)}, f32[4,64,256]{2,1,0:T(8,128)}, u32[]{:S(2)}) %copy-start.2) | copy-done | bytes 262168
  2.2 0.0 copy-start.3
  2.2 0.3 collective-permute-done.far
  2.6 2.9 %collective-permute-start.2 = (f32[64,512]{1,0:T(8,128)S(1)}, f32[64,512]{1,0:T(8,128)S(1)}, u32[]{:S(2)}, u32[]{:S(2)}) collective-permute-start(f32[64,512]{1,0:T(8,128)S(1)} %get-tuple-element.10), channel_id=1, source_target_pairs={{0,2},{1,8},{2,0},{3,10},{4,6},{5,12},{6,4},{7,14},{8,1},{9,16},{1... | collective-permute-start | bytes 393224 | tf_op jit(solution)/shard_map/ppermute | solution.py:328
  5.5 0.1 collective-permute-start.3
  5.6 3.6 %collective-permute-done.3.mine = f32[4,512]{1,0:T(4,128)S(1)} collective-permute-done((f32[4,512]{1,0:T(4,128)S(1)}, f32[4,512]{1,0:T(4,128)S(1)}, u32[]{:S(2)}, u32[]{:S(2)}) %collective-permute-start.3) | collective-permute-done | bytes 8224 | tf_op jit(solution)/shard_map/ppermute | solution.py:326
  9.2 0.0 collective-permute-start.4
  9.2 1.1 %collective-permute-done.4.theirs = f32[4,512]{1,0:T(4,128)S(1)} collective-permute-done((f32[4,512]{1,0:T(4,128)S(1)}, f32[4,512]{1,0:T(4,128)S(1)}, u32[]{:S(2)}, u32[]{:S(2)}) %collective-permute-start.4) | collective-permute-done | bytes 8224 | tf_op jit(solution)/shard_map/ppermute | solution.py:284
  10.3 0.0 collective-permute-done.2.shell
  10.3 1.2 %shard_map.80 = (f32[2,64,256]{2,1,0:T(8,128)S(1)}, f32[2,64,256]{2,1,0:T(8,128)S(1)}, f32[256,128]{1,0:T(8,128)}) custom-call(f32[4,64,256]{2,1,0:T(8,128)S(1)} %shard_map.77.rho, f32[4,64,256]{2,1,0:T(8,128)S(1)} %collective-permute-done.far, f32[4,64,256]{2,1,0:T(8,128)S(1)} %shard_map.78.kappa, f32[4,64,256]{2,1,0:T(8,128)S(1)} %collective-permute-done.1.far_kappa, ...), custom_call_target="tpu_custom_call" | custom-call | bytes 1048576 | tf_op jit(solution)/shard_map/pallas_call | solution.py:341
  11.6 4.9 %all-to-all-start = ((f32[32,8,128]{2,1,0:T(8,128)}), f32[32,8,128]{2,1,0:T(8,128)S(1)}, u32[]{:S(2)}, u32[]{:S(2)}) async-start(f32[32,8,128]{2,1,0:T(8,128)} %bitcast), calls=%async_computation | async-start | bytes 262144 | tf_op jit(solution)/shard_map/all_to_all | solution.py:352
  16.5 1.3 %shard_map.82 = (bf16[512,256]{1,0:T(8,128)(2,1)S(1)}, bf16[512,256]{1,0:T(8,128)(2,1)S(1)}, f32[2,256]{1,0:T(2,128)S(1)}) custom-call(f32[384,128]{1,0:T(8,128)S(1)} %copy-done.4, f32[4,256]{1,0:T(4,128)S(1)} %copy-done.5), custom_call_target="tpu_custom_call" | custom-call | flops 10000000 | bytes 1048576 | tf_op jit(solution)/shard_map/pallas_call | solution.py:332
  17.8 6.8 %all-to-all-done.spec_ref = f32[32,8,128]{2,1,0:T(8,128)S(1)} async-done(((f32[32,8,128]{2,1,0:T(8,128)}), f32[32,8,128]{2,1,0:T(8,128)S(1)}, u32[]{:S(2)}, u32[]{:S(2)}) %all-to-all-start) | async-done | bytes 131104 | tf_op jit(solution)/shard_map/all_to_all | solution.py:352
  24.6 1.5 %shard_map.83 = f32[32,8,128]{2,1,0:T(8,128)} custom-call(f32[32,8,128]{2,1,0:T(8,128)S(1)} %all-to-all-done.spec_ref, bf16[512,256]{1,0:T(8,128)(2,1)S(1)} %get-tuple-element.15.high_ref, bf16[512,256]{1,0:T(8,128)(2,1)S(1)} %get-tuple-element.16.low_ref, f32[2,256]{1,0:T(2,128)S(1)} %get-tuple-element.17.extra_ref), custom_call_target="tpu_custom_call" | custom-call | bytes 1048576 | tf_op jit(solution)/shard_map/pallas_call | solution.py:354
  26.2 2.6 %all-to-all-start.1 = ((f32[32,8,128]{2,1,0:T(8,128)}), f32[32,8,128]{2,1,0:T(8,128)S(1)}, u32[]{:S(2)}, u32[]{:S(2)}) async-start(f32[32,8,128]{2,1,0:T(8,128)} %shard_map.83), calls=%async_computation.1 | async-start | bytes 262144 | tf_op jit(solution)/shard_map/all_to_all | solution.py:360
  28.8 0.2 collective-permute-start.5
  28.9 8.0 %all-to-all-done.1 = f32[32,8,128]{2,1,0:T(8,128)S(1)} async-done(((f32[32,8,128]{2,1,0:T(8,128)}), f32[32,8,128]{2,1,0:T(8,128)S(1)}, u32[]{:S(2)}, u32[]{:S(2)}) %all-to-all-start.1) | async-done | bytes 131104 | tf_op jit(solution)/shard_map/all_to_all | solution.py:360
  37.0 0.2 collective-permute-start.6
  37.2 0.0 collective-permute-done.5.back
  37.2 0.7 %shard_map.81 = f32[4,64,256]{2,1,0:T(8,128)} custom-call(f32[2,64,256]{2,1,0:T(8,128)S(1)} %get-tuple-element.12.keep, f32[2,64,256]{2,1,0:T(8,128)S(1)} %collective-permute-done.5.back), custom_call_target="tpu_custom_call" | custom-call | bytes 1048576 | tf_op jit(solution)/shard_map/pallas_call | solution.py:362
  37.9 0.4 %collective-permute-done.6.far = f32[256,128]{1,0:T(8,128)S(1)} collective-permute-done((f32[256,128]{1,0:T(8,128)S(1)}, f32[256,128]{1,0:T(8,128)S(1)}, u32[]{:S(2)}, u32[]{:S(2)}) %collective-permute-start.6) | collective-permute-done | bytes 131104 | tf_op jit(solution)/shard_map/ppermute | solution.py:284
  38.3 1.0 %shard_map.84 = f32[4,64,256]{2,1,0:T(8,128)} custom-call(f32[256,128]{1,0:T(8,128)S(1)} %bitcast.3, f32[256,128]{1,0:T(8,128)S(1)} %collective-permute-done.6.far, bf16[256,512]{1,0:T(8,128)(2,1)S(1)} %copy-done.1, bf16[256,512]{1,0:T(8,128)(2,1)S(1)} %copy-done), custom_call_target="tpu_custom_call" | custom-call | bytes 1048576 | tf_op jit(solution)/shard_map/pallas_call | solution.py:363
  (14 shorter events, 0.1 us)
Async XLA Ops:
  0.6 1.9 %collective-permute-start = (f32[4,64,256]{2,1,0:T(8,128)}, f32[4,64,256]{2,1,0:T(8,128)S(1)}, u32[]{:S(2)}, u32[]{:S(2)}) collective-permute-start(f32[4,64,256]{2,1,0:T(8,128)} %source.2), channel_id=1, source_target_pairs={{0,1},{1,0},{2,3},{3,2},{4,5},{5,4},{6,7},{7,6},{8,9},{9,8},{10,11... | collective-permute-start | bytes 786440 | tf_op jit(solution)/shard_map/ppermute | solution.py:284
  1.2 8.0 %collective-permute-start.1 = (f32[4,64,256]{2,1,0:T(8,128)}, f32[4,64,256]{2,1,0:T(8,128)S(1)}, u32[]{:S(2)}, u32[]{:S(2)}) collective-permute-start(f32[4,64,256]{2,1,0:T(8,128)} %source.3), channel_id=1, source_target_pairs={{0,1},{1,0},{2,3},{3,2},{4,5},{5,4},{6,7},{7,6},{8,9},{9,8},{10,11... | collective-permute-start | bytes 786440 | tf_op jit(solution)/shard_map/ppermute | solution.py:284
  1.3 0.9 %copy-start.2 = (f32[4,64,256]{2,1,0:T(8,128)S(1)}, f32[4,64,256]{2,1,0:T(8,128)}, u32[]{:S(2)}) copy-start(f32[4,64,256]{2,1,0:T(8,128)} %source.2) | copy-start | bytes 786436
  2.2 6.9 %copy-start.3 = (f32[4,64,256]{2,1,0:T(8,128)S(1)}, f32[4,64,256]{2,1,0:T(8,128)}, u32[]{:S(2)}) copy-start(f32[4,64,256]{2,1,0:T(8,128)} %source.3) | copy-start | bytes 786436
  2.6 7.7 %collective-permute-start.2 = (f32[64,512]{1,0:T(8,128)S(1)}, f32[64,512]{1,0:T(8,128)S(1)}, u32[]{:S(2)}, u32[]{:S(2)}) collective-permute-start(f32[64,512]{1,0:T(8,128)S(1)} %get-tuple-element.10), channel_id=1, source_target_pairs={{0,2},{1,8},{2,0},{3,10},{4,6},{5,12},{6,4},{7,14},{8,1},{9,16},{1... | collective-permute-start | bytes 393224 | tf_op jit(solution)/shard_map/ppermute | solution.py:328
  5.5 4.8 %copy-start = (bf16[256,512]{1,0:T(8,128)(2,1)S(1)}, bf16[256,512]{1,0:T(8,128)(2,1)}, u32[]{:S(2)}) copy-start(bf16[256,512]{1,0:T(8,128)(2,1)} %constant.11.clone.w_low) | copy-start | bytes 786436
  5.5 4.8 %copy-start.1 = (bf16[256,512]{1,0:T(8,128)(2,1)S(1)}, bf16[256,512]{1,0:T(8,128)(2,1)}, u32[]{:S(2)}) copy-start(bf16[256,512]{1,0:T(8,128)(2,1)} %constant.10.clone.w_high) | copy-start | bytes 786436
  5.5 3.7 %collective-permute-start.3 = (f32[4,512]{1,0:T(4,128)S(1)}, f32[4,512]{1,0:T(4,128)S(1)}, u32[]{:S(2)}, u32[]{:S(2)}) collective-permute-start(f32[4,512]{1,0:T(4,128)S(1)} %get-tuple-element.11), channel_id=1, source_target_pairs={{0,2},{1,9},{2,0},{3,5},{4,6},{5,3},{6,4},{7,15},{8,10},{9,1},{10,... | collective-permute-start | bytes 24584 | tf_op jit(solution)/shard_map/ppermute | solution.py:326
  9.2 1.2 %collective-permute-start.4 = (f32[4,512]{1,0:T(4,128)S(1)}, f32[4,512]{1,0:T(4,128)S(1)}, u32[]{:S(2)}, u32[]{:S(2)}) collective-permute-start(f32[4,512]{1,0:T(4,128)S(1)} %collective-permute-done.3.mine), channel_id=1, source_target_pairs={{0,1},{1,0},{2,3},{3,2},{4,5},{5,4},{6,7},{7,6},{8,9},{9,8},{10,11... | collective-permute-start | bytes 24584 | tf_op jit(solution)/shard_map/ppermute | solution.py:284
  11.6 4.9 %copy-start.4 = (f32[384,128]{1,0:T(8,128)S(1)}, f32[384,128]{1,0:T(8,128)}, u32[]{:S(2)}) copy-start(f32[384,128]{1,0:T(8,128)} %constant.9.clone.coef_ref) | copy-start | bytes 589828
  11.6 4.9 %copy-start.5 = (f32[4,256]{1,0:T(4,128)S(1)}, f32[4,256]{1,0:T(4,128)}, u32[]{:S(2)}) copy-start(f32[4,256]{1,0:T(4,128)} %constant.8.clone.trig_ref) | copy-start | bytes 12292
  11.6 13.1 %all-to-all-start = ((f32[32,8,128]{2,1,0:T(8,128)}), f32[32,8,128]{2,1,0:T(8,128)S(1)}, u32[]{:S(2)}, u32[]{:S(2)}) async-start(f32[32,8,128]{2,1,0:T(8,128)} %bitcast), calls=%async_computation | async-start | bytes 262144 | tf_op jit(solution)/shard_map/all_to_all | solution.py:352
  26.2 10.8 %all-to-all-start.1 = ((f32[32,8,128]{2,1,0:T(8,128)}), f32[32,8,128]{2,1,0:T(8,128)S(1)}, u32[]{:S(2)}, u32[]{:S(2)}) async-start(f32[32,8,128]{2,1,0:T(8,128)} %shard_map.83), calls=%async_computation.1 | async-start | bytes 262144 | tf_op jit(solution)/shard_map/all_to_all | solution.py:360
  28.8 8.4 %collective-permute-start.5 = (f32[2,64,256]{2,1,0:T(8,128)S(1)}, f32[2,64,256]{2,1,0:T(8,128)S(1)}, u32[]{:S(2)}, u32[]{:S(2)}) collective-permute-start(f32[2,64,256]{2,1,0:T(8,128)S(1)} %get-tuple-element.13), channel_id=1, source_target_pairs={{0,1},{1,0},{2,3},{3,2},{4,5},{5,4},{6,7},{7,6},{8,9},{9,8},{10,11... | collective-permute-start | bytes 393224 | tf_op jit(solution)/shard_map/ppermute | solution.py:284
  37.0 1.3 %collective-permute-start.6 = (f32[256,128]{1,0:T(8,128)S(1)}, f32[256,128]{1,0:T(8,128)S(1)}, u32[]{:S(2)}, u32[]{:S(2)}) collective-permute-start(f32[256,128]{1,0:T(8,128)S(1)} %bitcast.2), channel_id=1, source_target_pairs={{0,1},{1,0},{2,3},{3,2},{4,5},{5,4},{6,7},{7,6},{8,9},{9,8},{10,11... | collective-permute-start | bytes 393224 | tf_op jit(solution)/shard_map/ppermute | solution.py:284

commit v7 on v6

--- a/solution.py
+++ b/solution.py
@@ -28,7 +28,10 @@
 
 def dot3(a, b, dims):
     one = functools.partial(lax.dot_general, dimension_numbers=dims, preferred_element_type=F32)
-    return one(a[0], b[0]) + (one(a[0], b[1]) + one(a[1], b[0]))
+    axis = 1 - dims[0][0][0]
+    rows = a[0].shape[axis]
+    wide = one(jnp.concatenate(a, axis=axis), b[0])
+    return wide[:rows] + (wide[rows:] + one(a[0], b[1]))
 
 
 def wave_table(azim_total, owners):
@@ -190,12 +193,15 @@
     lax.fori_loop(0, degrees // 8, block, ([jnp.ones((8, lanes), F32)] * parts, zero, zero))
     square = lambda d: lax.broadcasted_iota(jnp.int32, (north, north), d)
     mirror = jnp.where(square(0) + square(1) == north - 1, 1.0, 0.0).astype(BF16)
-    line = lax.broadcasted_iota(jnp.int32, (per * degrees, north), 0)
-    sign = jnp.where((line + line // degrees + start) % 2 == 0, 1.0, -1.0)
-    for piece, ref in zip(split(work[...].reshape(per * degrees, north)), (high_ref, low_ref)):
-        ref[:, :north] = piece
-        flipped = lax.dot_general(piece, mirror, NN, preferred_element_type=F32)
-        ref[:, north:] = (sign * flipped).astype(BF16)
+    row = lax.broadcasted_iota(jnp.int32, (8, north), 0)
+    for q in range(per):
+        even = ((row + (start + q)) & 1) == 0
+        sign = jnp.concatenate([jnp.where(even, 1.0, -1.0)] * (degrees // 8), axis=0)
+        at = pl.ds(q * degrees, degrees)
+        for piece, ref in zip(split(work[q]), (high_ref, low_ref)):
+            ref[at, :north] = piece
+            flipped = lax.dot_general(piece, mirror, NN, preferred_element_type=F32)
+            ref[at, north:] = (sign * flipped).astype(BF16)
 
 
 def solve_kernel(sizes, rows, polar, spec_ref, high_ref, low_ref, extra_ref, out_ref, work_ref):
@@ -214,7 +220,7 @@
                 work_ref[pl.ds((g * rows + h * half + r) * pair, pair), :] = piece * band
     table = high_ref[...], low_ref[...]
     wide = dot3(split(work_ref[...]), table, NT)
-    slot = lax.broadcasted_iota(jnp.int32, (shells * pair, degrees), 0) % per
+    slot = lax.broadcasted_iota(jnp.int32, (shells * pair, degrees), 0) & (per - 1)
     picked = wide[:, :degrees]
     for q in range(1, per):
         picked = jnp.where(slot == q, wide[:, q * degrees : (q + 1) * degrees], picked)

time: 39.6 us -> 39.5 us (level)
  no operation moved by 1% of the time
where the time goes in v7:
time: 39.5 us; the launch traced here: 39.2 us
  waiting for transfers between devices  20.3 us (51%)
  starting transfers between devices  11.5 us (29%)
  Pallas kernels  5.77 us (15%)
  local copies, waits for them, and re-layouts  0.97 us (2%)
  between operations  0.71 us (2%)
    all_to_all x1, waiting for transfers between devices, shards(): spec = spread(spec).reshape(2 * DEGREES, cells)  8.03 us
    all_to_all x1, waiting for transfers between devices, shards(): spec = spread(spec.reshape(owners, 2 * per, cells))  6.86 us
    all_to_all x1, starting transfers between devices, shards(): spec = spread(spec.reshape(owners, 2 * per, cells))  4.86 us
    ppermute x1, waiting for transfers between devices, shards(): mine = lax.ppermute(ends, AXES, pairs)  3.55 us
    ppermute x1, starting transfers between devices, shards(): shell = lax.ppermute(shell, AXES, pairs)  2.91 us
    all_to_all x1, starting transfers between devices, shards(): spec = spread(spec).reshape(2 * DEGREES, cells)  2.58 us
    ppermute x5, waiting for transfers between devices, pair_swap(): return lax.ppermute(value, axes, pairs)  1.85 us
    pallas_call x1, Pallas kernels, shards(): call(functools.partial(solve_kernel, sizes, rows, polar), ((spec.shape, F...  1.44 us
  transfers between devices with their start and end apart: 9, of which 6 were waited for; matrix products, arithmetic and copies ran while one was open for 0% of the time, Pallas kernels for 5%

profile of v7, /device:TPU:0, one launch (start us, length us, event | category | flops | bytes accessed | tf_op | source)
XLA Modules:
  0.0 39.2 jit_solution(10363449386843381467)
XLA Ops:
  0.6 0.6 %collective-permute-start = (f32[4,64,256]{2,1,0:T(8,128)}, f32[4,64,256]{2,1,0:T(8,128)S(1)}, u32[]{:S(2)}, u32[]{:S(2)}) collective-permute-start(f32[4,64,256]{2,1,0:T(8,128)} %source.2), channel_id=1, source_target_pairs={{0,1},{1,0},{2,3},{3,2},{4,5},{5,4},{6,7},{7,6},{8,9},{9,8},{10,11... | collective-permute-start | bytes 786440 | tf_op jit(solution)/shard_map/ppermute | solution.py:290
  1.2 0.1 collective-permute-start.1
  1.3 0.9 %copy-done.2 = f32[4,64,256]{2,1,0:T(8,128)S(1)} copy-done((f32[4,64,256]{2,1,0:T(8,128)S(1)}, f32[4,64,256]{2,1,0:T(8,128)}, u32[]{:S(2)}) %copy-start.2) | copy-done | bytes 262168
  2.2 0.0 copy-start.3
  2.2 0.3 collective-permute-done.far
  2.6 2.9 %collective-permute-start.2 = (f32[64,512]{1,0:T(8,128)S(1)}, f32[64,512]{1,0:T(8,128)S(1)}, u32[]{:S(2)}, u32[]{:S(2)}) collective-permute-start(f32[64,512]{1,0:T(8,128)S(1)} %get-tuple-element.10), channel_id=1, source_target_pairs={{0,2},{1,8},{2,0},{3,10},{4,6},{5,12},{6,4},{7,14},{8,1},{9,16},{1... | collective-permute-start | bytes 393224 | tf_op jit(solution)/shard_map/ppermute | solution.py:334
  5.5 0.1 collective-permute-start.3
  5.6 3.6 %collective-permute-done.3.mine = f32[4,512]{1,0:T(4,128)S(1)} collective-permute-done((f32[4,512]{1,0:T(4,128)S(1)}, f32[4,512]{1,0:T(4,128)S(1)}, u32[]{:S(2)}, u32[]{:S(2)}) %collective-permute-start.3) | collective-permute-done | bytes 8224 | tf_op jit(solution)/shard_map/ppermute | solution.py:332
  9.2 0.0 collective-permute-start.4
  9.2 1.1 %collective-permute-done.4.theirs = f32[4,512]{1,0:T(4,128)S(1)} collective-permute-done((f32[4,512]{1,0:T(4,128)S(1)}, f32[4,512]{1,0:T(4,128)S(1)}, u32[]{:S(2)}, u32[]{:S(2)}) %collective-permute-start.4) | collective-permute-done | bytes 8224 | tf_op jit(solution)/shard_map/ppermute | solution.py:290
  10.3 0.0 collective-permute-done.2.shell
  10.3 1.2 %shard_map.80 = (f32[2,64,256]{2,1,0:T(8,128)S(1)}, f32[2,64,256]{2,1,0:T(8,128)S(1)}, f32[256,128]{1,0:T(8,128)}) custom-call(f32[4,64,256]{2,1,0:T(8,128)S(1)} %shard_map.77.rho, f32[4,64,256]{2,1,0:T(8,128)S(1)} %collective-permute-done.far, f32[4,64,256]{2,1,0:T(8,128)S(1)} %shard_map.78.kappa, f32[4,64,256]{2,1,0:T(8,128)S(1)} %collective-permute-done.1.far_kappa, ...), custom_call_target="tpu_custom_call" | custom-call | bytes 1048576 | tf_op jit(solution)/shard_map/pallas_call | solution.py:347
  11.6 4.9 %all-to-all-start = ((f32[32,8,128]{2,1,0:T(8,128)}), f32[32,8,128]{2,1,0:T(8,128)S(1)}, u32[]{:S(2)}, u32[]{:S(2)}) async-start(f32[32,8,128]{2,1,0:T(8,128)} %bitcast), calls=%async_computation | async-start | bytes 262144 | tf_op jit(solution)/shard_map/all_to_all | solution.py:358
  16.5 1.3 %shard_map.82 = (bf16[512,256]{1,0:T(8,128)(2,1)S(1)}, bf16[512,256]{1,0:T(8,128)(2,1)S(1)}, f32[2,256]{1,0:T(2,128)S(1)}) custom-call(f32[384,128]{1,0:T(8,128)S(1)} %copy-done.4, f32[4,256]{1,0:T(4,128)S(1)} %copy-done.5), custom_call_target="tpu_custom_call" | custom-call | flops 10000000 | bytes 1048576 | tf_op jit(solution)/shard_map/pallas_call | solution.py:338
  17.8 6.9 %all-to-all-done.spec_ref = f32[32,8,128]{2,1,0:T(8,128)S(1)} async-done(((f32[32,8,128]{2,1,0:T(8,128)}), f32[32,8,128]{2,1,0:T(8,128)S(1)}, u32[]{:S(2)}, u32[]{:S(2)}) %all-to-all-start) | async-done | bytes 131104 | tf_op jit(solution)/shard_map/all_to_all | solution.py:358
  24.6 1.4 %shard_map.83 = f32[32,8,128]{2,1,0:T(8,128)} custom-call(f32[32,8,128]{2,1,0:T(8,128)S(1)} %all-to-all-done.spec_ref, bf16[512,256]{1,0:T(8,128)(2,1)S(1)} %get-tuple-element.15.high_ref, bf16[512,256]{1,0:T(8,128)(2,1)S(1)} %get-tuple-element.16.low_ref, f32[2,256]{1,0:T(2,128)S(1)} %get-tuple-element.17.extra_ref), custom_call_target="tpu_custom_call" | custom-call | bytes 1048576 | tf_op jit(solution)/shard_map/pallas_call | solution.py:360
  26.1 2.6 %all-to-all-start.1 = ((f32[32,8,128]{2,1,0:T(8,128)}), f32[32,8,128]{2,1,0:T(8,128)S(1)}, u32[]{:S(2)}, u32[]{:S(2)}) async-start(f32[32,8,128]{2,1,0:T(8,128)} %shard_map.83), calls=%async_computation.1 | async-start | bytes 262144 | tf_op jit(solution)/shard_map/all_to_all | solution.py:366
  28.7 0.2 collective-permute-start.5
  28.8 8.0 %all-to-all-done.1 = f32[32,8,128]{2,1,0:T(8,128)S(1)} async-done(((f32[32,8,128]{2,1,0:T(8,128)}), f32[32,8,128]{2,1,0:T(8,128)S(1)}, u32[]{:S(2)}, u32[]{:S(2)}) %all-to-all-start.1) | async-done | bytes 131104 | tf_op jit(solution)/shard_map/all_to_all | solution.py:366
  36.9 0.2 collective-permute-start.6
  37.1 0.0 collective-permute-done.5.back
  37.1 0.7 %shard_map.81 = f32[4,64,256]{2,1,0:T(8,128)} custom-call(f32[2,64,256]{2,1,0:T(8,128)S(1)} %get-tuple-element.12.keep, f32[2,64,256]{2,1,0:T(8,128)S(1)} %collective-permute-done.5.back), custom_call_target="tpu_custom_call" | custom-call | bytes 1048576 | tf_op jit(solution)/shard_map/pallas_call | solution.py:368
  37.8 0.4 %collective-permute-done.6.far = f32[256,128]{1,0:T(8,128)S(1)} collective-permute-done((f32[256,128]{1,0:T(8,128)S(1)}, f32[256,128]{1,0:T(8,128)S(1)}, u32[]{:S(2)}, u32[]{:S(2)}) %collective-permute-start.6) | collective-permute-done | bytes 131104 | tf_op jit(solution)/shard_map/ppermute | solution.py:290
  38.2 1.0 %shard_map.84 = f32[4,64,256]{2,1,0:T(8,128)} custom-call(f32[256,128]{1,0:T(8,128)S(1)} %bitcast.3, f32[256,128]{1,0:T(8,128)S(1)} %collective-permute-done.6.far, bf16[256,512]{1,0:T(8,128)(2,1)S(1)} %copy-done.1, bf16[256,512]{1,0:T(8,128)(2,1)S(1)} %copy-done), custom_call_target="tpu_custom_call" | custom-call | bytes 1048576 | tf_op jit(solution)/shard_map/pallas_call | solution.py:369
  (14 shorter events, 0.1 us)
Async XLA Ops:
  0.6 1.9 %collective-permute-start = (f32[4,64,256]{2,1,0:T(8,128)}, f32[4,64,256]{2,1,0:T(8,128)S(1)}, u32[]{:S(2)}, u32[]{:S(2)}) collective-permute-start(f32[4,64,256]{2,1,0:T(8,128)} %source.2), channel_id=1, source_target_pairs={{0,1},{1,0},{2,3},{3,2},{4,5},{5,4},{6,7},{7,6},{8,9},{9,8},{10,11... | collective-permute-start | bytes 786440 | tf_op jit(solution)/shard_map/ppermute | solution.py:290
  1.2 8.0 %collective-permute-start.1 = (f32[4,64,256]{2,1,0:T(8,128)}, f32[4,64,256]{2,1,0:T(8,128)S(1)}, u32[]{:S(2)}, u32[]{:S(2)}) collective-permute-start(f32[4,64,256]{2,1,0:T(8,128)} %source.3), channel_id=1, source_target_pairs={{0,1},{1,0},{2,3},{3,2},{4,5},{5,4},{6,7},{7,6},{8,9},{9,8},{10,11... | collective-permute-start | bytes 786440 | tf_op jit(solution)/shard_map/ppermute | solution.py:290
  1.3 0.9 %copy-start.2 = (f32[4,64,256]{2,1,0:T(8,128)S(1)}, f32[4,64,256]{2,1,0:T(8,128)}, u32[]{:S(2)}) copy-start(f32[4,64,256]{2,1,0:T(8,128)} %source.2) | copy-start | bytes 786436
  2.2 6.9 %copy-start.3 = (f32[4,64,256]{2,1,0:T(8,128)S(1)}, f32[4,64,256]{2,1,0:T(8,128)}, u32[]{:S(2)}) copy-start(f32[4,64,256]{2,1,0:T(8,128)} %source.3) | copy-start | bytes 786436
  2.6 7.7 %collective-permute-start.2 = (f32[64,512]{1,0:T(8,128)S(1)}, f32[64,512]{1,0:T(8,128)S(1)}, u32[]{:S(2)}, u32[]{:S(2)}) collective-permute-start(f32[64,512]{1,0:T(8,128)S(1)} %get-tuple-element.10), channel_id=1, source_target_pairs={{0,2},{1,8},{2,0},{3,10},{4,6},{5,12},{6,4},{7,14},{8,1},{9,16},{1... | collective-permute-start | bytes 393224 | tf_op jit(solution)/shard_map/ppermute | solution.py:334
  5.5 4.8 %copy-start = (bf16[256,512]{1,0:T(8,128)(2,1)S(1)}, bf16[256,512]{1,0:T(8,128)(2,1)}, u32[]{:S(2)}) copy-start(bf16[256,512]{1,0:T(8,128)(2,1)} %constant.11.clone.w_low) | copy-start | bytes 786436
  5.5 4.8 %copy-start.1 = (bf16[256,512]{1,0:T(8,128)(2,1)S(1)}, bf16[256,512]{1,0:T(8,128)(2,1)}, u32[]{:S(2)}) copy-start(bf16[256,512]{1,0:T(8,128)(2,1)} %constant.10.clone.w_high) | copy-start | bytes 786436
  5.5 3.7 %collective-permute-start.3 = (f32[4,512]{1,0:T(4,128)S(1)}, f32[4,512]{1,0:T(4,128)S(1)}, u32[]{:S(2)}, u32[]{:S(2)}) collective-permute-start(f32[4,512]{1,0:T(4,128)S(1)} %get-tuple-element.11), channel_id=1, source_target_pairs={{0,2},{1,9},{2,0},{3,5},{4,6},{5,3},{6,4},{7,15},{8,10},{9,1},{10,... | collective-permute-start | bytes 24584 | tf_op jit(solution)/shard_map/ppermute | solution.py:332
  9.2 1.2 %collective-permute-start.4 = (f32[4,512]{1,0:T(4,128)S(1)}, f32[4,512]{1,0:T(4,128)S(1)}, u32[]{:S(2)}, u32[]{:S(2)}) collective-permute-start(f32[4,512]{1,0:T(4,128)S(1)} %collective-permute-done.3.mine), channel_id=1, source_target_pairs={{0,1},{1,0},{2,3},{3,2},{4,5},{5,4},{6,7},{7,6},{8,9},{9,8},{10,11... | collective-permute-start | bytes 24584 | tf_op jit(solution)/shard_map/ppermute | solution.py:290
  11.6 4.9 %copy-start.4 = (f32[384,128]{1,0:T(8,128)S(1)}, f32[384,128]{1,0:T(8,128)}, u32[]{:S(2)}) copy-start(f32[384,128]{1,0:T(8,128)} %constant.9.clone.coef_ref) | copy-start | bytes 589828
  11.6 4.9 %copy-start.5 = (f32[4,256]{1,0:T(4,128)S(1)}, f32[4,256]{1,0:T(4,128)}, u32[]{:S(2)}) copy-start(f32[4,256]{1,0:T(4,128)} %constant.8.clone.trig_ref) | copy-start | bytes 12292
  11.6 13.1 %all-to-all-start = ((f32[32,8,128]{2,1,0:T(8,128)}), f32[32,8,128]{2,1,0:T(8,128)S(1)}, u32[]{:S(2)}, u32[]{:S(2)}) async-start(f32[32,8,128]{2,1,0:T(8,128)} %bitcast), calls=%async_computation | async-start | bytes 262144 | tf_op jit(solution)/shard_map/all_to_all | solution.py:358
  26.1 10.8 %all-to-all-start.1 = ((f32[32,8,128]{2,1,0:T(8,128)}), f32[32,8,128]{2,1,0:T(8,128)S(1)}, u32[]{:S(2)}, u32[]{:S(2)}) async-start(f32[32,8,128]{2,1,0:T(8,128)} %shard_map.83), calls=%async_computation.1 | async-start | bytes 262144 | tf_op jit(solution)/shard_map/all_to_all | solution.py:366
  28.7 8.4 %collective-permute-start.5 = (f32[2,64,256]{2,1,0:T(8,128)S(1)}, f32[2,64,256]{2,1,0:T(8,128)S(1)}, u32[]{:S(2)}, u32[]{:S(2)}) collective-permute-start(f32[2,64,256]{2,1,0:T(8,128)S(1)} %get-tuple-element.13), channel_id=1, source_target_pairs={{0,1},{1,0},{2,3},{3,2},{4,5},{5,4},{6,7},{7,6},{8,9},{9,8},{10,11... | collective-permute-start | bytes 393224 | tf_op jit(solution)/shard_map/ppermute | solution.py:290
  36.9 1.3 %collective-permute-start.6 = (f32[256,128]{1,0:T(8,128)S(1)}, f32[256,128]{1,0:T(8,128)S(1)}, u32[]{:S(2)}, u32[]{:S(2)}) collective-permute-start(f32[256,128]{1,0:T(8,128)S(1)} %bitcast.2), channel_id=1, source_target_pairs={{0,1},{1,0},{2,3},{3,2},{4,5},{5,4},{6,7},{7,6},{8,9},{9,8},{10,11... | collective-permute-start | bytes 393224 | tf_op jit(solution)/shard_map/ppermute | solution.py:290

commit v8 on v7

--- a/solution.py
+++ b/solution.py
@@ -81,25 +81,29 @@
     target[...] = source[...]
 
 
-def pack_kernel(rho, far, shell_out, ends_out):
+def pack_kernel(rho, far, shell_out, even_out, odd_out):
     rows, polar, azim = rho.shape
+    half = rows // 2
     ta, pa = lax.axis_index("ta"), lax.axis_index("pa")
     edge = pa * (rows - 1)
-    low = ta % 2 == pa
-    for k, half in enumerate((rho, far)):
+    even = ta % 2 == 0
+    for k, part in enumerate((rho, far)):
         at = pl.ds(k * azim, azim)
-        shell_out[:, at] = half[edge]
-        for r in range(rows):
-            ends_out[r : r + 1, at] = jnp.where(low, half[r, polar - 1 : polar, :], half[r, 0:1, :])
+        shell_out[:, at] = part[edge]
+        for r in range(half):
+            i = pa * half + r
+            first, last = part[i, 0:1, :], part[i, polar - 1 : polar, :]
+            even_out[r : r + 1, at] = jnp.where(even, last, first)
+            odd_out[r : r + 1, at] = jnp.where(even, first, last)
 
 
 def stencil_kernel(
-    sizes, rho, far, kappa, far_kappa, shell, mine, theirs, w_high, w_low, keep, send, spec, cells
+    sizes, rho, far, kappa, far_kappa, shell, even_in, odd_in, w_high, w_low, keep, send, spec, cells
 ):
     rows, polar, azim = rho.shape
     half = rows // 2
     row, ta, pa = (lax.axis_index(a) for a in AXES)
-    low = ta % 2 == pa
+    even = ta % 2 == 0
     sub = lax.broadcasted_iota(jnp.int32, (polar, 2 * azim), 0)
     both = lambda a, b: jnp.concatenate([a, b], axis=1)
     at = lambda i: both(rho[i], far[i])
@@ -118,9 +122,9 @@
             up = jnp.where(pa == 0, at(jnp.minimum(i + 1, rows - 1)), ghost)
         else:
             up = at(i + 1)
-        near, other = mine[pl.ds(i, 1), :], turned(theirs[pl.ds(i, 1), :])
-        north = jnp.where(ta == 0, turned(c[0:1, :]), jnp.where(low, other, near))
-        south = jnp.where(low, near, other)
+        one, two = even_in[r : r + 1, :], odd_in[r : r + 1, :]
+        north = jnp.where(ta == 0, turned(c[0:1, :]), jnp.where(even, two, one))
+        south = jnp.where(even, one, two)
         south = jnp.where(ta == sizes[1] - 1, turned(c[polar - 1 :, :]), south)
         pol_up = jnp.where(sub == 0, north, pltpu.roll(c, 1, 0))
         pol_down = jnp.where(sub == polar - 1, south, pltpu.roll(c, polar - 1, 0))
@@ -308,8 +312,8 @@
     return (row + 1, ta, 0) if pa == 1 else (row - 1, ta, 1)
 
 
-def polar_partner(row, ta, pa):
-    return (row, ta + 1 if ta % 2 == pa else ta - 1, pa)
+def polar_partner(first):
+    return lambda row, ta, pa: (row, ta + 1 if ta % 2 == first else ta - 1, pa)
 
 
 def shards(sizes, density, kappa):
@@ -325,14 +329,15 @@
     far, far_kappa = swap(density), swap(kappa)
     (density,) = call(stage_kernel, ((density.shape, F32),), [VMEM])(density)
     (kappa,) = call(stage_kernel, ((kappa.shape, F32),), [VMEM])(kappa)
-    shell, ends = call(
-        pack_kernel, (((polar, azim_total), F32), ((rows, azim_total), F32)), [VMEM] * 2
+    ends = ((half, azim_total), F32)
+    shell, even, odd = call(
+        pack_kernel, (((polar, azim_total), F32), ends, ends), [VMEM] * 2
     )(density, far)
-    pairs = halo_pairs(sizes, polar_partner, lambda row, ta, pa: (row ^ 1, ta, pa))
-    mine = lax.ppermute(ends, AXES, pairs)
-    pairs = halo_pairs(sizes, radial_partner, lambda row, ta, pa: (row, ta ^ 1, pa))
-    shell = lax.ppermute(shell, AXES, pairs)
-    theirs = swap(mine)
+    sides = lambda row, ta, pa: (row, ta ^ 1, pa)
+    cores = lambda row, ta, pa: (row, ta, pa ^ 1)
+    shell = lax.ppermute(shell, AXES, halo_pairs(sizes, radial_partner, sides))
+    even = lax.ppermute(even, AXES, halo_pairs(sizes, polar_partner(0), cores))
+    odd = lax.ppermute(odd, AXES, halo_pairs(sizes, polar_partner(1), cores))
 
     small = small_table(polar_total, azim_total)
     high, low, extra = call(
@@ -349,7 +354,7 @@
         (((half, polar, azim), F32), ((half, polar, azim), F32), ((2 * DEGREES, cells), F32)),
         [VMEM] * 9,
         [pltpu.VMEM((cells, azim_total), F32)],
-    )(density, far, kappa, far_kappa, shell, mine, theirs, *waves)
+    )(density, far, kappa, far_kappa, shell, even, odd, *waves)
 
     back = swap(send)
     spread = functools.partial(

time: 39.5 us -> 39.4 us (level)
  waiting for transfers between devices: 20.3 us -> 17.8 us
  starting transfers between devices: 11.5 us -> 13.9 us
    ppermute x2 -> x3, waiting for transfers between devices: 3.55 us -> 2.16 us  [the longest x1 2.16 us: shards(): even = lax.ppermute(even, AXES, halo_pairs(sizes, polar_partner(0), cores))]
    ppermute x2 -> x3, starting transfers between devices: 3.01 us -> 4.32 us  [the longest x1 2.91 us: shards(): shell = lax.ppermute(shell, AXES, halo_pairs(sizes, radial_partner, sides))]
    all_to_all x1, starting transfers between devices: 4.86 us -> 6.01 us  [shards(): spec = spread(spec.reshape(owners, 2 * per, cells))]
    ppermute x5 -> x4, waiting for transfers between devices: 1.85 us -> 0.72 us  [pair_swap(): return lax.ppermute(value, axes, pairs)]
    ppermute x5 -> x4, starting transfers between devices: 1.03 us -> 1.03 us  [pair_swap(): return lax.ppermute(value, axes, pairs)]
  transfers between devices with their start and end apart: 9 -> 9, of which waited for: 6 -> 5; matrix products, arithmetic and copies ran while one was open for 0% -> 0% of each run, Pallas kernels for 5% -> 5%
where the time goes in v8:
time: 39.4 us; the launch traced here: 39.2 us
  waiting for transfers between devices  17.8 us (45%)
  starting transfers between devices  13.9 us (35%)
  Pallas kernels  5.78 us (15%)
  local copies, waits for them, and re-layouts  0.97 us (2%)
  between operations  0.72 us (2%)
    all_to_all x1, waiting for transfers between devices, shards(): spec = spread(spec).reshape(2 * DEGREES, cells)  8.03 us
    all_to_all x1, waiting for transfers between devices, shards(): spec = spread(spec.reshape(owners, 2 * per, cells))  6.87 us
    all_to_all x1, starting transfers between devices, shards(): spec = spread(spec.reshape(owners, 2 * per, cells))  6.01 us
    ppermute x1, starting transfers between devices, shards(): shell = lax.ppermute(shell, AXES, halo_pairs(sizes, radial_partner, sides))  2.91 us
    all_to_all x1, starting transfers between devices, shards(): spec = spread(spec).reshape(2 * DEGREES, cells)  2.58 us
    ppermute x1, waiting for transfers between devices, shards(): even = lax.ppermute(even, AXES, halo_pairs(sizes, polar_partner(0), cores))  2.16 us
    pallas_call x1, Pallas kernels, shards(): call(functools.partial(solve_kernel, sizes, rows, polar), ((spec.shape, F...  1.44 us
    ppermute x1, starting transfers between devices, shards(): odd = lax.ppermute(odd, AXES, halo_pairs(sizes, polar_partner(1), cores))  1.33 us
  transfers between devices with their start and end apart: 9, of which 5 were waited for; matrix products, arithmetic and copies ran while one was open for 0% of the time, Pallas kernels for 5%

profile of v8, /device:TPU:0, one launch (start us, length us, event | category | flops | bytes accessed | tf_op | source)
XLA Modules:
  0.0 39.2 jit_solution(426267320946222839)
XLA Ops:
  0.6 0.6 %collective-permute-start = (f32[4,64,256]{2,1,0:T(8,128)}, f32[4,64,256]{2,1,0:T(8,128)S(1)}, u32[]{:S(2)}, u32[]{:S(2)}) collective-permute-start(f32[4,64,256]{2,1,0:T(8,128)} %source.2), channel_id=1, source_target_pairs={{0,1},{1,0},{2,3},{3,2},{4,5},{5,4},{6,7},{7,6},{8,9},{9,8},{10,11... | collective-permute-start | bytes 786440 | tf_op jit(solution)/shard_map/ppermute | solution.py:294
  1.2 0.1 collective-permute-start.1
  1.3 0.9 %copy-done.2 = f32[4,64,256]{2,1,0:T(8,128)S(1)} copy-done((f32[4,64,256]{2,1,0:T(8,128)S(1)}, f32[4,64,256]{2,1,0:T(8,128)}, u32[]{:S(2)}) %copy-start.2) | copy-done | bytes 262168
  2.2 0.0 copy-start.3
  2.2 0.3 collective-permute-done.far
  2.6 2.9 %collective-permute-start.2 = (f32[64,512]{1,0:T(8,128)S(1)}, f32[64,512]{1,0:T(8,128)S(1)}, u32[]{:S(2)}, u32[]{:S(2)}) collective-permute-start(f32[64,512]{1,0:T(8,128)S(1)} %get-tuple-element.11), channel_id=1, source_target_pairs={{0,2},{1,8},{2,0},{3,10},{4,6},{5,12},{6,4},{7,14},{8,1},{9,16},{1... | collective-permute-start | bytes 393224 | tf_op jit(solution)/shard_map/ppermute | solution.py:338
  5.5 0.1 collective-permute-start.3
  5.6 1.3 %collective-permute-start.4 = (f32[2,512]{1,0:T(2,128)S(1)}, f32[2,512]{1,0:T(2,128)S(1)}, u32[]{:S(2)}, u32[]{:S(2)}) collective-permute-start(f32[2,512]{1,0:T(2,128)S(1)} %get-tuple-element.13), channel_id=1, source_target_pairs={{0,1},{1,0},{2,4},{3,5},{4,2},{5,3},{6,7},{7,6},{8,9},{9,8},{10,12... | collective-permute-start | bytes 12296 | tf_op jit(solution)/shard_map/ppermute | solution.py:340
  6.9 0.0 collective-permute-done.1.far_kappa
  6.9 2.2 %collective-permute-done.3.even_in = f32[2,512]{1,0:T(2,128)S(1)} collective-permute-done((f32[2,512]{1,0:T(2,128)S(1)}, f32[2,512]{1,0:T(2,128)S(1)}, u32[]{:S(2)}, u32[]{:S(2)}) %collective-permute-start.3) | collective-permute-done | bytes 4128 | tf_op jit(solution)/shard_map/ppermute | solution.py:339
  9.1 0.0 collective-permute-done.4.odd_in
  9.1 0.0 collective-permute-done.2.shell
  9.1 1.2 %shard_map.80 = (f32[2,64,256]{2,1,0:T(8,128)S(1)}, f32[2,64,256]{2,1,0:T(8,128)S(1)}, f32[256,128]{1,0:T(8,128)}) custom-call(f32[4,64,256]{2,1,0:T(8,128)S(1)} %shard_map.77.rho, f32[4,64,256]{2,1,0:T(8,128)S(1)} %collective-permute-done.far, f32[4,64,256]{2,1,0:T(8,128)S(1)} %shard_map.78.kappa, f32[4,64,256]{2,1,0:T(8,128)S(1)} %collective-permute-done.1.far_kappa, ...), custom_call_target="tpu_custom_call" | custom-call | bytes 1048576 | tf_op jit(solution)/shard_map/pallas_call | solution.py:352
  10.4 6.0 %all-to-all-start = ((f32[32,8,128]{2,1,0:T(8,128)}), f32[32,8,128]{2,1,0:T(8,128)S(1)}, u32[]{:S(2)}, u32[]{:S(2)}) async-start(f32[32,8,128]{2,1,0:T(8,128)} %bitcast), calls=%async_computation | async-start | bytes 262144 | tf_op jit(solution)/shard_map/all_to_all | solution.py:363
  16.4 1.3 %shard_map.82 = (bf16[512,256]{1,0:T(8,128)(2,1)S(1)}, bf16[512,256]{1,0:T(8,128)(2,1)S(1)}, f32[2,256]{1,0:T(2,128)S(1)}) custom-call(f32[384,128]{1,0:T(8,128)S(1)} %copy-done.4, f32[4,256]{1,0:T(4,128)S(1)} %copy-done.5), custom_call_target="tpu_custom_call" | custom-call | flops 10000000 | bytes 1048576 | tf_op jit(solution)/shard_map/pallas_call | solution.py:343
  17.7 6.9 %all-to-all-done.spec_ref = f32[32,8,128]{2,1,0:T(8,128)S(1)} async-done(((f32[32,8,128]{2,1,0:T(8,128)}), f32[32,8,128]{2,1,0:T(8,128)S(1)}, u32[]{:S(2)}, u32[]{:S(2)}) %all-to-all-start) | async-done | bytes 131104 | tf_op jit(solution)/shard_map/all_to_all | solution.py:363
  24.6 1.4 %shard_map.83 = f32[32,8,128]{2,1,0:T(8,128)} custom-call(f32[32,8,128]{2,1,0:T(8,128)S(1)} %all-to-all-done.spec_ref, bf16[512,256]{1,0:T(8,128)(2,1)S(1)} %get-tuple-element.17.high_ref, bf16[512,256]{1,0:T(8,128)(2,1)S(1)} %get-tuple-element.18.low_ref, f32[2,256]{1,0:T(2,128)S(1)} %get-tuple-element.19.extra_ref), custom_call_target="tpu_custom_call" | custom-call | bytes 1048576 | tf_op jit(solution)/shard_map/pallas_call | solution.py:365
  26.0 2.6 %all-to-all-start.1 = ((f32[32,8,128]{2,1,0:T(8,128)}), f32[32,8,128]{2,1,0:T(8,128)S(1)}, u32[]{:S(2)}, u32[]{:S(2)}) async-start(f32[32,8,128]{2,1,0:T(8,128)} %shard_map.83), calls=%async_computation.1 | async-start | bytes 262144 | tf_op jit(solution)/shard_map/all_to_all | solution.py:371
  28.6 0.2 collective-permute-start.5
  28.8 8.0 %all-to-all-done.1 = f32[32,8,128]{2,1,0:T(8,128)S(1)} async-done(((f32[32,8,128]{2,1,0:T(8,128)}), f32[32,8,128]{2,1,0:T(8,128)S(1)}, u32[]{:S(2)}, u32[]{:S(2)}) %all-to-all-start.1) | async-done | bytes 131104 | tf_op jit(solution)/shard_map/all_to_all | solution.py:371
  36.8 0.2 collective-permute-start.6
  37.0 0.7 %shard_map.81 = f32[4,64,256]{2,1,0:T(8,128)} custom-call(f32[2,64,256]{2,1,0:T(8,128)S(1)} %get-tuple-element.14.keep, f32[2,64,256]{2,1,0:T(8,128)S(1)} %collective-permute-done.5.back), custom_call_target="tpu_custom_call" | custom-call | bytes 1048576 | tf_op jit(solution)/shard_map/pallas_call | solution.py:373
  37.8 0.4 %collective-permute-done.6.far = f32[256,128]{1,0:T(8,128)S(1)} collective-permute-done((f32[256,128]{1,0:T(8,128)S(1)}, f32[256,128]{1,0:T(8,128)S(1)}, u32[]{:S(2)}, u32[]{:S(2)}) %collective-permute-start.6) | collective-permute-done | bytes 131104 | tf_op jit(solution)/shard_map/ppermute | solution.py:294
  38.2 1.0 %shard_map.84 = f32[4,64,256]{2,1,0:T(8,128)} custom-call(f32[256,128]{1,0:T(8,128)S(1)} %bitcast.3, f32[256,128]{1,0:T(8,128)S(1)} %collective-permute-done.6.far, bf16[256,512]{1,0:T(8,128)(2,1)S(1)} %copy-done.1, bf16[256,512]{1,0:T(8,128)(2,1)S(1)} %copy-done), custom_call_target="tpu_custom_call" | custom-call | bytes 1048576 | tf_op jit(solution)/shard_map/pallas_call | solution.py:374
  (14 shorter events, 0.1 us)
Async XLA Ops:
  0.6 1.9 %collective-permute-start = (f32[4,64,256]{2,1,0:T(8,128)}, f32[4,64,256]{2,1,0:T(8,128)S(1)}, u32[]{:S(2)}, u32[]{:S(2)}) collective-permute-start(f32[4,64,256]{2,1,0:T(8,128)} %source.2), channel_id=1, source_target_pairs={{0,1},{1,0},{2,3},{3,2},{4,5},{5,4},{6,7},{7,6},{8,9},{9,8},{10,11... | collective-permute-start | bytes 786440 | tf_op jit(solution)/shard_map/ppermute | solution.py:294
  1.2 5.7 %collective-permute-start.1 = (f32[4,64,256]{2,1,0:T(8,128)}, f32[4,64,256]{2,1,0:T(8,128)S(1)}, u32[]{:S(2)}, u32[]{:S(2)}) collective-permute-start(f32[4,64,256]{2,1,0:T(8,128)} %source.3), channel_id=1, source_target_pairs={{0,1},{1,0},{2,3},{3,2},{4,5},{5,4},{6,7},{7,6},{8,9},{9,8},{10,11... | collective-permute-start | bytes 786440 | tf_op jit(solution)/shard_map/ppermute | solution.py:294
  1.3 0.9 %copy-start.2 = (f32[4,64,256]{2,1,0:T(8,128)S(1)}, f32[4,64,256]{2,1,0:T(8,128)}, u32[]{:S(2)}) copy-start(f32[4,64,256]{2,1,0:T(8,128)} %source.2) | copy-start | bytes 786436
  2.2 4.7 %copy-start.3 = (f32[4,64,256]{2,1,0:T(8,128)S(1)}, f32[4,64,256]{2,1,0:T(8,128)}, u32[]{:S(2)}) copy-start(f32[4,64,256]{2,1,0:T(8,128)} %source.3) | copy-start | bytes 786436
  2.6 6.5 %collective-permute-start.2 = (f32[64,512]{1,0:T(8,128)S(1)}, f32[64,512]{1,0:T(8,128)S(1)}, u32[]{:S(2)}, u32[]{:S(2)}) collective-permute-start(f32[64,512]{1,0:T(8,128)S(1)} %get-tuple-element.11), channel_id=1, source_target_pairs={{0,2},{1,8},{2,0},{3,10},{4,6},{5,12},{6,4},{7,14},{8,1},{9,16},{1... | collective-permute-start | bytes 393224 | tf_op jit(solution)/shard_map/ppermute | solution.py:338
  5.5 3.6 %collective-permute-start.3 = (f32[2,512]{1,0:T(2,128)S(1)}, f32[2,512]{1,0:T(2,128)S(1)}, u32[]{:S(2)}, u32[]{:S(2)}) collective-permute-start(f32[2,512]{1,0:T(2,128)S(1)} %get-tuple-element.12), channel_id=1, source_target_pairs={{0,2},{1,3},{2,0},{3,1},{4,6},{5,7},{6,4},{7,5},{8,10},{9,11},{10,... | collective-permute-start | bytes 12296 | tf_op jit(solution)/shard_map/ppermute | solution.py:339
  5.6 3.5 %copy-start = (bf16[256,512]{1,0:T(8,128)(2,1)S(1)}, bf16[256,512]{1,0:T(8,128)(2,1)}, u32[]{:S(2)}) copy-start(bf16[256,512]{1,0:T(8,128)(2,1)} %constant.11.clone.w_low) | copy-start | bytes 786436
  5.6 3.5 %copy-start.1 = (bf16[256,512]{1,0:T(8,128)(2,1)S(1)}, bf16[256,512]{1,0:T(8,128)(2,1)}, u32[]{:S(2)}) copy-start(bf16[256,512]{1,0:T(8,128)(2,1)} %constant.10.clone.w_high) | copy-start | bytes 786436
  5.6 3.5 %collective-permute-start.4 = (f32[2,512]{1,0:T(2,128)S(1)}, f32[2,512]{1,0:T(2,128)S(1)}, u32[]{:S(2)}, u32[]{:S(2)}) collective-permute-start(f32[2,512]{1,0:T(2,128)S(1)} %get-tuple-element.13), channel_id=1, source_target_pairs={{0,1},{1,0},{2,4},{3,5},{4,2},{5,3},{6,7},{7,6},{8,9},{9,8},{10,12... | collective-permute-start | bytes 12296 | tf_op jit(solution)/shard_map/ppermute | solution.py:340
  10.4 6.0 %copy-start.4 = (f32[384,128]{1,0:T(8,128)S(1)}, f32[384,128]{1,0:T(8,128)}, u32[]{:S(2)}) copy-start(f32[384,128]{1,0:T(8,128)} %constant.9.clone.coef_ref) | copy-start | bytes 589828
  10.4 6.0 %copy-start.5 = (f32[4,256]{1,0:T(4,128)S(1)}, f32[4,256]{1,0:T(4,128)}, u32[]{:S(2)}) copy-start(f32[4,256]{1,0:T(4,128)} %constant.8.clone.trig_ref) | copy-start | bytes 12292
  10.4 14.2 %all-to-all-start = ((f32[32,8,128]{2,1,0:T(8,128)}), f32[32,8,128]{2,1,0:T(8,128)S(1)}, u32[]{:S(2)}, u32[]{:S(2)}) async-start(f32[32,8,128]{2,1,0:T(8,128)} %bitcast), calls=%async_computation | async-start | bytes 262144 | tf_op jit(solution)/shard_map/all_to_all | solution.py:363
  26.0 10.8 %all-to-all-start.1 = ((f32[32,8,128]{2,1,0:T(8,128)}), f32[32,8,128]{2,1,0:T(8,128)S(1)}, u32[]{:S(2)}, u32[]{:S(2)}) async-start(f32[32,8,128]{2,1,0:T(8,128)} %shard_map.83), calls=%async_computation.1 | async-start | bytes 262144 | tf_op jit(solution)/shard_map/all_to_all | solution.py:371
  28.6 8.4 %collective-permute-start.5 = (f32[2,64,256]{2,1,0:T(8,128)S(1)}, f32[2,64,256]{2,1,0:T(8,128)S(1)}, u32[]{:S(2)}, u32[]{:S(2)}) collective-permute-start(f32[2,64,256]{2,1,0:T(8,128)S(1)} %get-tuple-element.15), channel_id=1, source_target_pairs={{0,1},{1,0},{2,3},{3,2},{4,5},{5,4},{6,7},{7,6},{8,9},{9,8},{10,11... | collective-permute-start | bytes 393224 | tf_op jit(solution)/shard_map/ppermute | solution.py:294
  36.8 1.3 %collective-permute-start.6 = (f32[256,128]{1,0:T(8,128)S(1)}, f32[256,128]{1,0:T(8,128)S(1)}, u32[]{:S(2)}, u32[]{:S(2)}) collective-permute-start(f32[256,128]{1,0:T(8,128)S(1)} %bitcast.2), channel_id=1, source_target_pairs={{0,1},{1,0},{2,3},{3,2},{4,5},{5,4},{6,7},{7,6},{8,9},{9,8},{10,11... | collective-permute-start | bytes 393224 | tf_op jit(solution)/shard_map/ppermute | solution.py:294

commit v9 on v8

--- a/solution.py
+++ b/solution.py
@@ -97,41 +97,64 @@
             odd_out[r : r + 1, at] = jnp.where(even, first, last)
 
 
-def stencil_kernel(
-    sizes, rho, far, kappa, far_kappa, shell, even_in, odd_in, w_high, w_low, keep, send, spec, cells
-):
+def both(a, b):
+    return jnp.concatenate([a, b], axis=1)
+
+
+def early_kernel(sizes, rho, far, kappa, far_kappa, w_high, w_low, base):
     rows, polar, azim = rho.shape
     half = rows // 2
     row, ta, pa = (lax.axis_index(a) for a in AXES)
-    even = ta % 2 == 0
     sub = lax.broadcasted_iota(jnp.int32, (polar, 2 * azim), 0)
-    both = lambda a, b: jnp.concatenate([a, b], axis=1)
     at = lambda i: both(rho[i], far[i])
     turned = lambda x: both(x[:, azim:], x[:, :azim])
-    outer = turned(shell[...])
     for r in range(half):
         i = pa * half + r
         c = at(i)
         if r == 0:
-            ghost = jnp.where(row == 0, c, outer)
-            down = jnp.where(pa == 0, ghost, at(jnp.maximum(i - 1, 0)))
+            edge = jnp.where(row == 0, c, 0.0)
+            down = jnp.where(pa == 0, edge, at(jnp.maximum(i - 1, 0)))
         else:
             down = at(i - 1)
         if r == half - 1:
-            ghost = jnp.where(row == sizes[0] - 1, c, outer)
-            up = jnp.where(pa == 0, at(jnp.minimum(i + 1, rows - 1)), ghost)
+            edge = jnp.where(row == sizes[0] - 1, c, 0.0)
+            up = jnp.where(pa == 0, at(jnp.minimum(i + 1, rows - 1)), edge)
         else:
             up = at(i + 1)
-        one, two = even_in[r : r + 1, :], odd_in[r : r + 1, :]
-        north = jnp.where(ta == 0, turned(c[0:1, :]), jnp.where(even, two, one))
-        south = jnp.where(even, one, two)
-        south = jnp.where(ta == sizes[1] - 1, turned(c[polar - 1 :, :]), south)
+        north = jnp.where(ta == 0, turned(c[0:1, :]), 0.0)
+        south = jnp.where(ta == sizes[1] - 1, turned(c[polar - 1 :, :]), 0.0)
         pol_up = jnp.where(sub == 0, north, pltpu.roll(c, 1, 0))
         pol_down = jnp.where(sub == polar - 1, south, pltpu.roll(c, polar - 1, 0))
         west = pltpu.roll(c, 1, 1)
         east = pltpu.roll(c, 2 * azim - 1, 1)
         lap = up + down + pol_up + pol_down + west + east - 6.0 * c
-        new = c + both(kappa[i], far_kappa[i]) * lap
+        base[r * polar : (r + 1) * polar, :] = c + both(kappa[i], far_kappa[i]) * lap
+
+
+def stencil_kernel(
+    sizes, base, kappa, far_kappa, shell, even_in, odd_in, w_high, w_low, keep, send, spec, cells
+):
+    rows, polar, azim = kappa.shape
+    half = rows // 2
+    row, ta, pa = (lax.axis_index(a) for a in AXES)
+    even = ta % 2 == 0
+    outer = both(shell[:, azim:], shell[:, :azim])
+    for r in range(half):
+        i = pa * half + r
+        k = both(kappa[i], far_kappa[i])
+        new = base[r * polar : (r + 1) * polar, :]
+        if r == 0:
+            new = new + jnp.where((pa == 0) & (row > 0), k * outer, 0.0)
+        if r == half - 1:
+            new = new + jnp.where((pa == 1) & (row < sizes[0] - 1), k * outer, 0.0)
+        one, two = even_in[r : r + 1, :], odd_in[r : r + 1, :]
+        north = jnp.where(ta == 0, 0.0, jnp.where(even, two, one)) * k[0:1, :]
+        south = jnp.where(ta == sizes[1] - 1, 0.0, jnp.where(even, one, two)) * k[polar - 1 :, :]
+        top, low = new[0:8, :], new[polar - 8 :, :]
+        sub = lax.broadcasted_iota(jnp.int32, top.shape, 0)
+        top = top + jnp.where(sub == 0, north, 0.0)
+        low = low + jnp.where(sub == 7, south, 0.0)
+        new = jnp.concatenate([top, new[8 : polar - 8, :], low], axis=0)
         keep[r] = new[:, :azim]
         send[r] = new[:, azim:]
         cells[r * polar : (r + 1) * polar, :] = new - 1.0
@@ -349,12 +372,15 @@
     )(recursion_table(), small)
 
     waves = wave_table(azim_total, owners)
+    (base,) = call(
+        functools.partial(early_kernel, sizes), (((cells, azim_total), F32),), [VMEM] * 6
+    )(density, far, kappa, far_kappa, *waves)
     keep, send, spec = call(
         functools.partial(stencil_kernel, sizes),
         (((half, polar, azim), F32), ((half, polar, azim), F32), ((2 * DEGREES, cells), F32)),
-        [VMEM] * 9,
+        [VMEM] * 8,
         [pltpu.VMEM((cells, azim_total), F32)],
-    )(density, far, kappa, far_kappa, shell, even, odd, *waves)
+    )(base, kappa, far_kappa, shell, even, odd, *waves)
 
     back = swap(send)
     spread = functools.partial(

time: 39.4 us -> 39.2 us (level)
  transfers between devices with their start and end apart: 9 -> 9, of which waited for: 5 -> 5; matrix products, arithmetic and copies ran while one was open for 0% -> 0% of each run, Pallas kernels for 5% -> 6%
where the time goes in v9:
time: 39.2 us; the launch traced here: 39 us
  waiting for transfers between devices  17.5 us (45%)
  starting transfers between devices  13.9 us (35%)
  Pallas kernels  5.84 us (15%)
  local copies, waits for them, and re-layouts  0.97 us (2%)
  between operations  0.73 us (2%)
    all_to_all x1, waiting for transfers between devices, shards(): spec = spread(spec).reshape(2 * DEGREES, cells)  8.03 us
    all_to_all x1, waiting for transfers between devices, shards(): spec = spread(spec.reshape(owners, 2 * per, cells))  6.86 us
    all_to_all x1, starting transfers between devices, shards(): spec = spread(spec.reshape(owners, 2 * per, cells))  6.01 us
    ppermute x1, starting transfers between devices, shards(): shell = lax.ppermute(shell, AXES, halo_pairs(sizes, radial_partner, sides))  2.91 us
    all_to_all x1, starting transfers between devices, shards(): spec = spread(spec).reshape(2 * DEGREES, cells)  2.58 us
    ppermute x1, waiting for transfers between devices, shards(): even = lax.ppermute(even, AXES, halo_pairs(sizes, polar_partner(0), cores))  1.9 us
    pallas_call x1, Pallas kernels, shards(): call(functools.partial(solve_kernel, sizes, rows, polar), ((spec.shape, F...  1.44 us
    ppermute x1, starting transfers between devices, shards(): odd = lax.ppermute(odd, AXES, halo_pairs(sizes, polar_partner(1), cores))  1.33 us
  transfers between devices with their start and end apart: 9, of which 5 were waited for; matrix products, arithmetic and copies ran while one was open for 0% of the time, Pallas kernels for 6%

profile of v9, /device:TPU:0, one launch (start us, length us, event | category | flops | bytes accessed | tf_op | source)
XLA Modules:
  0.0 39.0 jit_solution(14074076533899860915)
XLA Ops:
  0.6 0.6 %collective-permute-start = (f32[4,64,256]{2,1,0:T(8,128)}, f32[4,64,256]{2,1,0:T(8,128)S(1)}, u32[]{:S(2)}, u32[]{:S(2)}) collective-permute-start(f32[4,64,256]{2,1,0:T(8,128)} %source.2), channel_id=1, source_target_pairs={{0,1},{1,0},{2,3},{3,2},{4,5},{5,4},{6,7},{7,6},{8,9},{9,8},{10,11... | collective-permute-start | bytes 786440 | tf_op jit(solution)/shard_map/ppermute | solution.py:317
  1.2 0.1 collective-permute-start.1
  1.3 0.9 %copy-done.2 = f32[4,64,256]{2,1,0:T(8,128)S(1)} copy-done((f32[4,64,256]{2,1,0:T(8,128)S(1)}, f32[4,64,256]{2,1,0:T(8,128)}, u32[]{:S(2)}) %copy-start.2) | copy-done | bytes 262168
  2.2 0.0 copy-start.3
  2.2 0.3 collective-permute-done.far
  2.6 2.9 %collective-permute-start.2 = (f32[64,512]{1,0:T(8,128)S(1)}, f32[64,512]{1,0:T(8,128)S(1)}, u32[]{:S(2)}, u32[]{:S(2)}) collective-permute-start(f32[64,512]{1,0:T(8,128)S(1)} %get-tuple-element.11), channel_id=1, source_target_pairs={{0,2},{1,8},{2,0},{3,10},{4,6},{5,12},{6,4},{7,14},{8,1},{9,16},{1... | collective-permute-start | bytes 393224 | tf_op jit(solution)/shard_map/ppermute | solution.py:361
  5.5 0.1 collective-permute-start.3
  5.6 1.3 %collective-permute-start.4 = (f32[2,512]{1,0:T(2,128)S(1)}, f32[2,512]{1,0:T(2,128)S(1)}, u32[]{:S(2)}, u32[]{:S(2)}) collective-permute-start(f32[2,512]{1,0:T(2,128)S(1)} %get-tuple-element.13), channel_id=1, source_target_pairs={{0,1},{1,0},{2,4},{3,5},{4,2},{5,3},{6,7},{7,6},{8,9},{9,8},{10,12... | collective-permute-start | bytes 12296 | tf_op jit(solution)/shard_map/ppermute | solution.py:363
  6.9 0.0 collective-permute-done.1.far_kappa
  7.0 0.2 shard_map.79.base
  7.2 1.9 %collective-permute-done.3.even_in = f32[2,512]{1,0:T(2,128)S(1)} collective-permute-done((f32[2,512]{1,0:T(2,128)S(1)}, f32[2,512]{1,0:T(2,128)S(1)}, u32[]{:S(2)}, u32[]{:S(2)}) %collective-permute-start.3) | collective-permute-done | bytes 4128 | tf_op jit(solution)/shard_map/ppermute | solution.py:362
  9.1 0.0 collective-permute-done.4.odd_in
  9.1 1.1 %shard_map.81 = (f32[2,64,256]{2,1,0:T(8,128)S(1)}, f32[2,64,256]{2,1,0:T(8,128)S(1)}, f32[256,128]{1,0:T(8,128)}) custom-call(f32[128,512]{1,0:T(8,128)S(1)} %shard_map.79.base, f32[4,64,256]{2,1,0:T(8,128)S(1)} %shard_map.78.kappa, f32[4,64,256]{2,1,0:T(8,128)S(1)} %collective-permute-done.1.far_kappa, f32[64,512]{1,0:T(8,128)S(1)} %collective-permute-done.2.shell, ...), custom_call_target="tpu_custom_call" | custom-call | bytes 1048576 | tf_op jit(solution)/shard_map/pallas_call | solution.py:378
  10.2 6.0 %all-to-all-start = ((f32[32,8,128]{2,1,0:T(8,128)}), f32[32,8,128]{2,1,0:T(8,128)S(1)}, u32[]{:S(2)}, u32[]{:S(2)}) async-start(f32[32,8,128]{2,1,0:T(8,128)} %bitcast), calls=%async_computation | async-start | bytes 262144 | tf_op jit(solution)/shard_map/all_to_all | solution.py:389
  16.2 1.3 %shard_map.83 = (bf16[512,256]{1,0:T(8,128)(2,1)S(1)}, bf16[512,256]{1,0:T(8,128)(2,1)S(1)}, f32[2,256]{1,0:T(2,128)S(1)}) custom-call(f32[384,128]{1,0:T(8,128)S(1)} %copy-done.4, f32[4,256]{1,0:T(4,128)S(1)} %copy-done.5), custom_call_target="tpu_custom_call" | custom-call | flops 10000000 | bytes 1048576 | tf_op jit(solution)/shard_map/pallas_call | solution.py:366
  17.5 6.9 %all-to-all-done.spec_ref = f32[32,8,128]{2,1,0:T(8,128)S(1)} async-done(((f32[32,8,128]{2,1,0:T(8,128)}), f32[32,8,128]{2,1,0:T(8,128)S(1)}, u32[]{:S(2)}, u32[]{:S(2)}) %all-to-all-start) | async-done | bytes 131104 | tf_op jit(solution)/shard_map/all_to_all | solution.py:389
  24.4 1.4 %shard_map.84 = f32[32,8,128]{2,1,0:T(8,128)} custom-call(f32[32,8,128]{2,1,0:T(8,128)S(1)} %all-to-all-done.spec_ref, bf16[512,256]{1,0:T(8,128)(2,1)S(1)} %get-tuple-element.17.high_ref, bf16[512,256]{1,0:T(8,128)(2,1)S(1)} %get-tuple-element.18.low_ref, f32[2,256]{1,0:T(2,128)S(1)} %get-tuple-element.19.extra_ref), custom_call_target="tpu_custom_call" | custom-call | bytes 1048576 | tf_op jit(solution)/shard_map/pallas_call | solution.py:391
  25.9 2.6 %all-to-all-start.1 = ((f32[32,8,128]{2,1,0:T(8,128)}), f32[32,8,128]{2,1,0:T(8,128)S(1)}, u32[]{:S(2)}, u32[]{:S(2)}) async-start(f32[32,8,128]{2,1,0:T(8,128)} %shard_map.84), calls=%async_computation.1 | async-start | bytes 262144 | tf_op jit(solution)/shard_map/all_to_all | solution.py:397
  28.4 0.2 collective-permute-start.5
  28.6 8.0 %all-to-all-done.1 = f32[32,8,128]{2,1,0:T(8,128)S(1)} async-done(((f32[32,8,128]{2,1,0:T(8,128)}), f32[32,8,128]{2,1,0:T(8,128)S(1)}, u32[]{:S(2)}, u32[]{:S(2)}) %all-to-all-start.1) | async-done | bytes 131104 | tf_op jit(solution)/shard_map/all_to_all | solution.py:397
  36.6 0.2 collective-permute-start.6
  36.9 0.7 %shard_map.82 = f32[4,64,256]{2,1,0:T(8,128)} custom-call(f32[2,64,256]{2,1,0:T(8,128)S(1)} %get-tuple-element.14.keep, f32[2,64,256]{2,1,0:T(8,128)S(1)} %collective-permute-done.5.back), custom_call_target="tpu_custom_call" | custom-call | bytes 1048576 | tf_op jit(solution)/shard_map/pallas_call | solution.py:399
  37.6 0.4 %collective-permute-done.6.far = f32[256,128]{1,0:T(8,128)S(1)} collective-permute-done((f32[256,128]{1,0:T(8,128)S(1)}, f32[256,128]{1,0:T(8,128)S(1)}, u32[]{:S(2)}, u32[]{:S(2)}) %collective-permute-start.6) | collective-permute-done | bytes 131104 | tf_op jit(solution)/shard_map/ppermute | solution.py:317
  38.0 1.0 %shard_map.85 = f32[4,64,256]{2,1,0:T(8,128)} custom-call(f32[256,128]{1,0:T(8,128)S(1)} %bitcast.3, f32[256,128]{1,0:T(8,128)S(1)} %collective-permute-done.6.far, bf16[256,512]{1,0:T(8,128)(2,1)S(1)} %copy-done.1, bf16[256,512]{1,0:T(8,128)(2,1)S(1)} %copy-done), custom_call_target="tpu_custom_call" | custom-call | bytes 1048576 | tf_op jit(solution)/shard_map/pallas_call | solution.py:400
  (15 shorter events, 0.1 us)
Async XLA Ops:
  0.6 1.9 %collective-permute-start = (f32[4,64,256]{2,1,0:T(8,128)}, f32[4,64,256]{2,1,0:T(8,128)S(1)}, u32[]{:S(2)}, u32[]{:S(2)}) collective-permute-start(f32[4,64,256]{2,1,0:T(8,128)} %source.2), channel_id=1, source_target_pairs={{0,1},{1,0},{2,3},{3,2},{4,5},{5,4},{6,7},{7,6},{8,9},{9,8},{10,11... | collective-permute-start | bytes 786440 | tf_op jit(solution)/shard_map/ppermute | solution.py:317
  1.2 5.7 %collective-permute-start.1 = (f32[4,64,256]{2,1,0:T(8,128)}, f32[4,64,256]{2,1,0:T(8,128)S(1)}, u32[]{:S(2)}, u32[]{:S(2)}) collective-permute-start(f32[4,64,256]{2,1,0:T(8,128)} %source.3), channel_id=1, source_target_pairs={{0,1},{1,0},{2,3},{3,2},{4,5},{5,4},{6,7},{7,6},{8,9},{9,8},{10,11... | collective-permute-start | bytes 786440 | tf_op jit(solution)/shard_map/ppermute | solution.py:317
  1.3 0.9 %copy-start.2 = (f32[4,64,256]{2,1,0:T(8,128)S(1)}, f32[4,64,256]{2,1,0:T(8,128)}, u32[]{:S(2)}) copy-start(f32[4,64,256]{2,1,0:T(8,128)} %source.2) | copy-start | bytes 786436
  2.2 4.7 %copy-start.3 = (f32[4,64,256]{2,1,0:T(8,128)S(1)}, f32[4,64,256]{2,1,0:T(8,128)}, u32[]{:S(2)}) copy-start(f32[4,64,256]{2,1,0:T(8,128)} %source.3) | copy-start | bytes 786436
  2.6 6.5 %collective-permute-start.2 = (f32[64,512]{1,0:T(8,128)S(1)}, f32[64,512]{1,0:T(8,128)S(1)}, u32[]{:S(2)}, u32[]{:S(2)}) collective-permute-start(f32[64,512]{1,0:T(8,128)S(1)} %get-tuple-element.11), channel_id=1, source_target_pairs={{0,2},{1,8},{2,0},{3,10},{4,6},{5,12},{6,4},{7,14},{8,1},{9,16},{1... | collective-permute-start | bytes 393224 | tf_op jit(solution)/shard_map/ppermute | solution.py:361
  5.5 3.6 %collective-permute-start.3 = (f32[2,512]{1,0:T(2,128)S(1)}, f32[2,512]{1,0:T(2,128)S(1)}, u32[]{:S(2)}, u32[]{:S(2)}) collective-permute-start(f32[2,512]{1,0:T(2,128)S(1)} %get-tuple-element.12), channel_id=1, source_target_pairs={{0,2},{1,3},{2,0},{3,1},{4,6},{5,7},{6,4},{7,5},{8,10},{9,11},{10,... | collective-permute-start | bytes 12296 | tf_op jit(solution)/shard_map/ppermute | solution.py:362
  5.6 1.4 %copy-start = (bf16[256,512]{1,0:T(8,128)(2,1)S(1)}, bf16[256,512]{1,0:T(8,128)(2,1)}, u32[]{:S(2)}) copy-start(bf16[256,512]{1,0:T(8,128)(2,1)} %constant.11.clone.w_low) | copy-start | bytes 786436
  5.6 1.4 %copy-start.1 = (bf16[256,512]{1,0:T(8,128)(2,1)S(1)}, bf16[256,512]{1,0:T(8,128)(2,1)}, u32[]{:S(2)}) copy-start(bf16[256,512]{1,0:T(8,128)(2,1)} %constant.10.clone.w_high) | copy-start | bytes 786436
  5.6 3.5 %collective-permute-start.4 = (f32[2,512]{1,0:T(2,128)S(1)}, f32[2,512]{1,0:T(2,128)S(1)}, u32[]{:S(2)}, u32[]{:S(2)}) collective-permute-start(f32[2,512]{1,0:T(2,128)S(1)} %get-tuple-element.13), channel_id=1, source_target_pairs={{0,1},{1,0},{2,4},{3,5},{4,2},{5,3},{6,7},{7,6},{8,9},{9,8},{10,12... | collective-permute-start | bytes 12296 | tf_op jit(solution)/shard_map/ppermute | solution.py:363
  10.2 6.0 %copy-start.4 = (f32[384,128]{1,0:T(8,128)S(1)}, f32[384,128]{1,0:T(8,128)}, u32[]{:S(2)}) copy-start(f32[384,128]{1,0:T(8,128)} %constant.9.clone.coef_ref) | copy-start | bytes 589828
  10.2 6.0 %copy-start.5 = (f32[4,256]{1,0:T(4,128)S(1)}, f32[4,256]{1,0:T(4,128)}, u32[]{:S(2)}) copy-start(f32[4,256]{1,0:T(4,128)} %constant.8.clone.trig_ref) | copy-start | bytes 12292
  10.2 14.2 %all-to-all-start = ((f32[32,8,128]{2,1,0:T(8,128)}), f32[32,8,128]{2,1,0:T(8,128)S(1)}, u32[]{:S(2)}, u32[]{:S(2)}) async-start(f32[32,8,128]{2,1,0:T(8,128)} %bitcast), calls=%async_computation | async-start | bytes 262144 | tf_op jit(solution)/shard_map/all_to_all | solution.py:389
  25.9 10.8 %all-to-all-start.1 = ((f32[32,8,128]{2,1,0:T(8,128)}), f32[32,8,128]{2,1,0:T(8,128)S(1)}, u32[]{:S(2)}, u32[]{:S(2)}) async-start(f32[32,8,128]{2,1,0:T(8,128)} %shard_map.84), calls=%async_computation.1 | async-start | bytes 262144 | tf_op jit(solution)/shard_map/all_to_all | solution.py:397
  28.4 8.4 %collective-permute-start.5 = (f32[2,64,256]{2,1,0:T(8,128)S(1)}, f32[2,64,256]{2,1,0:T(8,128)S(1)}, u32[]{:S(2)}, u32[]{:S(2)}) collective-permute-start(f32[2,64,256]{2,1,0:T(8,128)S(1)} %get-tuple-element.15), channel_id=1, source_target_pairs={{0,1},{1,0},{2,3},{3,2},{4,5},{5,4},{6,7},{7,6},{8,9},{9,8},{10,11... | collective-permute-start | bytes 393224 | tf_op jit(solution)/shard_map/ppermute | solution.py:317
  36.6 1.3 %collective-permute-start.6 = (f32[256,128]{1,0:T(8,128)S(1)}, f32[256,128]{1,0:T(8,128)S(1)}, u32[]{:S(2)}, u32[]{:S(2)}) collective-permute-start(f32[256,128]{1,0:T(8,128)S(1)} %bitcast.2), channel_id=1, source_target_pairs={{0,1},{1,0},{2,3},{3,2},{4,5},{5,4},{6,7},{7,6},{8,9},{9,8},{10,11... | collective-permute-start | bytes 393224 | tf_op jit(solution)/shard_map/ppermute | solution.py:317

commit v10 on v9

--- a/solution.py
+++ b/solution.py
@@ -53,7 +53,8 @@
     b = np.sqrt(np.maximum(low * low - m * m, 0) / np.maximum(4 * low * low - 1, 1.0))
     sect = np.where(l == 1, math.sqrt(3.0), np.sqrt((2 * l + 1) / np.maximum(2 * l, 1.0)))
     wide = np.broadcast_to(sect, (DEGREES, 128))
-    return jnp.asarray(np.concatenate([a, a * b, wide]).astype(np.float32))
+    spare = np.zeros((8, 128))
+    return jnp.asarray(np.concatenate([a, a * b, wide, spare]).astype(np.float32))
 
 
 def small_table(polar_total, azim_total):
@@ -180,7 +181,7 @@
     lanes = 128
     near = pltpu.roll(coef_ref[: 2 * degrees, :], lanes - start, 1)
     for q in range(per):
-        spread_ref[q] = jnp.broadcast_to(near[:, q : q + 1], (2 * degrees, lanes))
+        spread_ref[q, : 2 * degrees, :] = jnp.broadcast_to(near[:, q : q + 1], (2 * degrees, lanes))
     parts = north // lanes
     cut = lambda row, k: jnp.broadcast_to(trig_ref[row : row + 1, k * lanes : (k + 1) * lanes], (8, lanes))
     cos_t = [cut(0, k) for k in range(parts)]
@@ -367,7 +368,7 @@
         functools.partial(table_kernel, sizes),
         (((per * DEGREES, polar_total), BF16),) * 2 + (((2, polar_total), F32),),
         [VMEM] * 2,
-        [pltpu.VMEM((per, 2 * DEGREES, 128), F32), pltpu.VMEM((per, DEGREES, polar_total // 2), F32)],
+        [pltpu.VMEM((per, 2 * DEGREES + 8, 128), F32), pltpu.VMEM((per, DEGREES, polar_total // 2), F32)],
         flops=10**7,
     )(recursion_table(), small)
 

time: 39.2 us -> 39.2 us (level)
  no operation moved by 1% of the time
where the time goes in v10:
time: 39.2 us; the launch traced here: 39 us
  waiting for transfers between devices  17.5 us (45%)
  starting transfers between devices  13.9 us (35%)
  Pallas kernels  5.84 us (15%)
  local copies, waits for them, and re-layouts  0.97 us (2%)
  between operations  0.73 us (2%)
    all_to_all x1, waiting for transfers between devices, shards(): spec = spread(spec).reshape(2 * DEGREES, cells)  8.03 us
    all_to_all x1, waiting for transfers between devices, shards(): spec = spread(spec.reshape(owners, 2 * per, cells))  6.86 us
    all_to_all x1, starting transfers between devices, shards(): spec = spread(spec.reshape(owners, 2 * per, cells))  6.01 us
    ppermute x1, starting transfers between devices, shards(): shell = lax.ppermute(shell, AXES, halo_pairs(sizes, radial_partner, sides))  2.91 us
    all_to_all x1, starting transfers between devices, shards(): spec = spread(spec).reshape(2 * DEGREES, cells)  2.58 us
    ppermute x1, waiting for transfers between devices, shards(): even = lax.ppermute(even, AXES, halo_pairs(sizes, polar_partner(0), cores))  1.9 us
    pallas_call x1, Pallas kernels, shards(): call(functools.partial(solve_kernel, sizes, rows, polar), ((spec.shape, F...  1.44 us
    ppermute x1, starting transfers between devices, shards(): odd = lax.ppermute(odd, AXES, halo_pairs(sizes, polar_partner(1), cores))  1.33 us
  transfers between devices with their start and end apart: 9, of which 5 were waited for; matrix products, arithmetic and copies ran while one was open for 0% of the time, Pallas kernels for 6%

profile of v10, /device:TPU:0, one launch (start us, length us, event | category | flops | bytes accessed | tf_op | source)
XLA Modules:
  0.0 39.0 jit_solution(13318398270066495657)
XLA Ops:
  0.6 0.6 %collective-permute-start = (f32[4,64,256]{2,1,0:T(8,128)}, f32[4,64,256]{2,1,0:T(8,128)S(1)}, u32[]{:S(2)}, u32[]{:S(2)}) collective-permute-start(f32[4,64,256]{2,1,0:T(8,128)} %source.2), channel_id=1, source_target_pairs={{0,1},{1,0},{2,3},{3,2},{4,5},{5,4},{6,7},{7,6},{8,9},{9,8},{10,11... | collective-permute-start | bytes 786440 | tf_op jit(solution)/shard_map/ppermute | solution.py:318
  1.2 0.1 collective-permute-start.1
  1.3 0.9 %copy-done.2 = f32[4,64,256]{2,1,0:T(8,128)S(1)} copy-done((f32[4,64,256]{2,1,0:T(8,128)S(1)}, f32[4,64,256]{2,1,0:T(8,128)}, u32[]{:S(2)}) %copy-start.2) | copy-done | bytes 262168
  2.2 0.0 copy-start.3
  2.2 0.3 collective-permute-done.far
  2.6 2.9 %collective-permute-start.2 = (f32[64,512]{1,0:T(8,128)S(1)}, f32[64,512]{1,0:T(8,128)S(1)}, u32[]{:S(2)}, u32[]{:S(2)}) collective-permute-start(f32[64,512]{1,0:T(8,128)S(1)} %get-tuple-element.11), channel_id=1, source_target_pairs={{0,2},{1,8},{2,0},{3,10},{4,6},{5,12},{6,4},{7,14},{8,1},{9,16},{1... | collective-permute-start | bytes 393224 | tf_op jit(solution)/shard_map/ppermute | solution.py:362
  5.5 0.1 collective-permute-start.3
  5.6 1.3 %collective-permute-start.4 = (f32[2,512]{1,0:T(2,128)S(1)}, f32[2,512]{1,0:T(2,128)S(1)}, u32[]{:S(2)}, u32[]{:S(2)}) collective-permute-start(f32[2,512]{1,0:T(2,128)S(1)} %get-tuple-element.13), channel_id=1, source_target_pairs={{0,1},{1,0},{2,4},{3,5},{4,2},{5,3},{6,7},{7,6},{8,9},{9,8},{10,12... | collective-permute-start | bytes 12296 | tf_op jit(solution)/shard_map/ppermute | solution.py:364
  6.9 0.0 collective-permute-done.1.far_kappa
  7.0 0.2 shard_map.79.base
  7.2 1.9 %collective-permute-done.3.even_in = f32[2,512]{1,0:T(2,128)S(1)} collective-permute-done((f32[2,512]{1,0:T(2,128)S(1)}, f32[2,512]{1,0:T(2,128)S(1)}, u32[]{:S(2)}, u32[]{:S(2)}) %collective-permute-start.3) | collective-permute-done | bytes 4128 | tf_op jit(solution)/shard_map/ppermute | solution.py:363
  9.1 0.0 collective-permute-done.4.odd_in
  9.1 1.1 %shard_map.81 = (f32[2,64,256]{2,1,0:T(8,128)S(1)}, f32[2,64,256]{2,1,0:T(8,128)S(1)}, f32[256,128]{1,0:T(8,128)}) custom-call(f32[128,512]{1,0:T(8,128)S(1)} %shard_map.79.base, f32[4,64,256]{2,1,0:T(8,128)S(1)} %shard_map.78.kappa, f32[4,64,256]{2,1,0:T(8,128)S(1)} %collective-permute-done.1.far_kappa, f32[64,512]{1,0:T(8,128)S(1)} %collective-permute-done.2.shell, ...), custom_call_target="tpu_custom_call" | custom-call | bytes 1048576 | tf_op jit(solution)/shard_map/pallas_call | solution.py:379
  10.2 6.0 %all-to-all-start = ((f32[32,8,128]{2,1,0:T(8,128)}), f32[32,8,128]{2,1,0:T(8,128)S(1)}, u32[]{:S(2)}, u32[]{:S(2)}) async-start(f32[32,8,128]{2,1,0:T(8,128)} %bitcast), calls=%async_computation | async-start | bytes 262144 | tf_op jit(solution)/shard_map/all_to_all | solution.py:390
  16.2 1.3 %shard_map.83 = (bf16[512,256]{1,0:T(8,128)(2,1)S(1)}, bf16[512,256]{1,0:T(8,128)(2,1)S(1)}, f32[2,256]{1,0:T(2,128)S(1)}) custom-call(f32[392,128]{1,0:T(8,128)S(1)} %copy-done.4, f32[4,256]{1,0:T(4,128)S(1)} %copy-done.5), custom_call_target="tpu_custom_call" | custom-call | flops 10000000 | bytes 1048576 | tf_op jit(solution)/shard_map/pallas_call | solution.py:367
  17.5 6.9 %all-to-all-done.spec_ref = f32[32,8,128]{2,1,0:T(8,128)S(1)} async-done(((f32[32,8,128]{2,1,0:T(8,128)}), f32[32,8,128]{2,1,0:T(8,128)S(1)}, u32[]{:S(2)}, u32[]{:S(2)}) %all-to-all-start) | async-done | bytes 131104 | tf_op jit(solution)/shard_map/all_to_all | solution.py:390
  24.4 1.4 %shard_map.84 = f32[32,8,128]{2,1,0:T(8,128)} custom-call(f32[32,8,128]{2,1,0:T(8,128)S(1)} %all-to-all-done.spec_ref, bf16[512,256]{1,0:T(8,128)(2,1)S(1)} %get-tuple-element.17.high_ref, bf16[512,256]{1,0:T(8,128)(2,1)S(1)} %get-tuple-element.18.low_ref, f32[2,256]{1,0:T(2,128)S(1)} %get-tuple-element.19.extra_ref), custom_call_target="tpu_custom_call" | custom-call | bytes 1048576 | tf_op jit(solution)/shard_map/pallas_call | solution.py:392
  25.9 2.6 %all-to-all-start.1 = ((f32[32,8,128]{2,1,0:T(8,128)}), f32[32,8,128]{2,1,0:T(8,128)S(1)}, u32[]{:S(2)}, u32[]{:S(2)}) async-start(f32[32,8,128]{2,1,0:T(8,128)} %shard_map.84), calls=%async_computation.1 | async-start | bytes 262144 | tf_op jit(solution)/shard_map/all_to_all | solution.py:398
  28.4 0.2 collective-permute-start.5
  28.6 8.0 %all-to-all-done.1 = f32[32,8,128]{2,1,0:T(8,128)S(1)} async-done(((f32[32,8,128]{2,1,0:T(8,128)}), f32[32,8,128]{2,1,0:T(8,128)S(1)}, u32[]{:S(2)}, u32[]{:S(2)}) %all-to-all-start.1) | async-done | bytes 131104 | tf_op jit(solution)/shard_map/all_to_all | solution.py:398
  36.6 0.2 collective-permute-start.6
  36.9 0.7 %shard_map.82 = f32[4,64,256]{2,1,0:T(8,128)} custom-call(f32[2,64,256]{2,1,0:T(8,128)S(1)} %get-tuple-element.14.keep, f32[2,64,256]{2,1,0:T(8,128)S(1)} %collective-permute-done.5.back), custom_call_target="tpu_custom_call" | custom-call | bytes 1048576 | tf_op jit(solution)/shard_map/pallas_call | solution.py:400
  37.6 0.4 %collective-permute-done.6.far = f32[256,128]{1,0:T(8,128)S(1)} collective-permute-done((f32[256,128]{1,0:T(8,128)S(1)}, f32[256,128]{1,0:T(8,128)S(1)}, u32[]{:S(2)}, u32[]{:S(2)}) %collective-permute-start.6) | collective-permute-done | bytes 131104 | tf_op jit(solution)/shard_map/ppermute | solution.py:318
  38.0 1.0 %shard_map.85 = f32[4,64,256]{2,1,0:T(8,128)} custom-call(f32[256,128]{1,0:T(8,128)S(1)} %bitcast.3, f32[256,128]{1,0:T(8,128)S(1)} %collective-permute-done.6.far, bf16[256,512]{1,0:T(8,128)(2,1)S(1)} %copy-done.1, bf16[256,512]{1,0:T(8,128)(2,1)S(1)} %copy-done), custom_call_target="tpu_custom_call" | custom-call | bytes 1048576 | tf_op jit(solution)/shard_map/pallas_call | solution.py:401
  (15 shorter events, 0.1 us)
Async XLA Ops:
  0.6 1.9 %collective-permute-start = (f32[4,64,256]{2,1,0:T(8,128)}, f32[4,64,256]{2,1,0:T(8,128)S(1)}, u32[]{:S(2)}, u32[]{:S(2)}) collective-permute-start(f32[4,64,256]{2,1,0:T(8,128)} %source.2), channel_id=1, source_target_pairs={{0,1},{1,0},{2,3},{3,2},{4,5},{5,4},{6,7},{7,6},{8,9},{9,8},{10,11... | collective-permute-start | bytes 786440 | tf_op jit(solution)/shard_map/ppermute | solution.py:318
  1.2 5.7 %collective-permute-start.1 = (f32[4,64,256]{2,1,0:T(8,128)}, f32[4,64,256]{2,1,0:T(8,128)S(1)}, u32[]{:S(2)}, u32[]{:S(2)}) collective-permute-start(f32[4,64,256]{2,1,0:T(8,128)} %source.3), channel_id=1, source_target_pairs={{0,1},{1,0},{2,3},{3,2},{4,5},{5,4},{6,7},{7,6},{8,9},{9,8},{10,11... | collective-permute-start | bytes 786440 | tf_op jit(solution)/shard_map/ppermute | solution.py:318
  1.3 0.9 %copy-start.2 = (f32[4,64,256]{2,1,0:T(8,128)S(1)}, f32[4,64,256]{2,1,0:T(8,128)}, u32[]{:S(2)}) copy-start(f32[4,64,256]{2,1,0:T(8,128)} %source.2) | copy-start | bytes 786436
  2.2 4.7 %copy-start.3 = (f32[4,64,256]{2,1,0:T(8,128)S(1)}, f32[4,64,256]{2,1,0:T(8,128)}, u32[]{:S(2)}) copy-start(f32[4,64,256]{2,1,0:T(8,128)} %source.3) | copy-start | bytes 786436
  2.6 6.5 %collective-permute-start.2 = (f32[64,512]{1,0:T(8,128)S(1)}, f32[64,512]{1,0:T(8,128)S(1)}, u32[]{:S(2)}, u32[]{:S(2)}) collective-permute-start(f32[64,512]{1,0:T(8,128)S(1)} %get-tuple-element.11), channel_id=1, source_target_pairs={{0,2},{1,8},{2,0},{3,10},{4,6},{5,12},{6,4},{7,14},{8,1},{9,16},{1... | collective-permute-start | bytes 393224 | tf_op jit(solution)/shard_map/ppermute | solution.py:362
  5.5 3.6 %collective-permute-start.3 = (f32[2,512]{1,0:T(2,128)S(1)}, f32[2,512]{1,0:T(2,128)S(1)}, u32[]{:S(2)}, u32[]{:S(2)}) collective-permute-start(f32[2,512]{1,0:T(2,128)S(1)} %get-tuple-element.12), channel_id=1, source_target_pairs={{0,2},{1,3},{2,0},{3,1},{4,6},{5,7},{6,4},{7,5},{8,10},{9,11},{10,... | collective-permute-start | bytes 12296 | tf_op jit(solution)/shard_map/ppermute | solution.py:363
  5.6 1.4 %copy-start = (bf16[256,512]{1,0:T(8,128)(2,1)S(1)}, bf16[256,512]{1,0:T(8,128)(2,1)}, u32[]{:S(2)}) copy-start(bf16[256,512]{1,0:T(8,128)(2,1)} %constant.11.clone.w_low) | copy-start | bytes 786436
  5.6 1.4 %copy-start.1 = (bf16[256,512]{1,0:T(8,128)(2,1)S(1)}, bf16[256,512]{1,0:T(8,128)(2,1)}, u32[]{:S(2)}) copy-start(bf16[256,512]{1,0:T(8,128)(2,1)} %constant.10.clone.w_high) | copy-start | bytes 786436
  5.6 3.5 %collective-permute-start.4 = (f32[2,512]{1,0:T(2,128)S(1)}, f32[2,512]{1,0:T(2,128)S(1)}, u32[]{:S(2)}, u32[]{:S(2)}) collective-permute-start(f32[2,512]{1,0:T(2,128)S(1)} %get-tuple-element.13), channel_id=1, source_target_pairs={{0,1},{1,0},{2,4},{3,5},{4,2},{5,3},{6,7},{7,6},{8,9},{9,8},{10,12... | collective-permute-start | bytes 12296 | tf_op jit(solution)/shard_map/ppermute | solution.py:364
  10.2 6.0 %copy-start.4 = (f32[392,128]{1,0:T(8,128)S(1)}, f32[392,128]{1,0:T(8,128)}, u32[]{:S(2)}) copy-start(f32[392,128]{1,0:T(8,128)} %constant.9.clone.coef_ref) | copy-start | bytes 602116
  10.2 6.0 %copy-start.5 = (f32[4,256]{1,0:T(4,128)S(1)}, f32[4,256]{1,0:T(4,128)}, u32[]{:S(2)}) copy-start(f32[4,256]{1,0:T(4,128)} %constant.8.clone.trig_ref) | copy-start | bytes 12292
  10.2 14.2 %all-to-all-start = ((f32[32,8,128]{2,1,0:T(8,128)}), f32[32,8,128]{2,1,0:T(8,128)S(1)}, u32[]{:S(2)}, u32[]{:S(2)}) async-start(f32[32,8,128]{2,1,0:T(8,128)} %bitcast), calls=%async_computation | async-start | bytes 262144 | tf_op jit(solution)/shard_map/all_to_all | solution.py:390
  25.9 10.8 %all-to-all-start.1 = ((f32[32,8,128]{2,1,0:T(8,128)}), f32[32,8,128]{2,1,0:T(8,128)S(1)}, u32[]{:S(2)}, u32[]{:S(2)}) async-start(f32[32,8,128]{2,1,0:T(8,128)} %shard_map.84), calls=%async_computation.1 | async-start | bytes 262144 | tf_op jit(solution)/shard_map/all_to_all | solution.py:398
  28.4 8.4 %collective-permute-start.5 = (f32[2,64,256]{2,1,0:T(8,128)S(1)}, f32[2,64,256]{2,1,0:T(8,128)S(1)}, u32[]{:S(2)}, u32[]{:S(2)}) collective-permute-start(f32[2,64,256]{2,1,0:T(8,128)S(1)} %get-tuple-element.15), channel_id=1, source_target_pairs={{0,1},{1,0},{2,3},{3,2},{4,5},{5,4},{6,7},{7,6},{8,9},{9,8},{10,11... | collective-permute-start | bytes 393224 | tf_op jit(solution)/shard_map/ppermute | solution.py:318
  36.6 1.3 %collective-permute-start.6 = (f32[256,128]{1,0:T(8,128)S(1)}, f32[256,128]{1,0:T(8,128)S(1)}, u32[]{:S(2)}, u32[]{:S(2)}) collective-permute-start(f32[256,128]{1,0:T(8,128)S(1)} %bitcast.2), channel_id=1, source_target_pairs={{0,1},{1,0},{2,3},{3,2},{4,5},{5,4},{6,7},{7,6},{8,9},{9,8},{10,11... | collective-permute-start | bytes 393224 | tf_op jit(solution)/shard_map/ppermute | solution.py:318

commit v11 on v10

--- a/solution.py
+++ b/solution.py
@@ -13,6 +13,7 @@
 DEGREES = 128
 AXES = ("row", "ta", "pa")
 VMEM = pl.BlockSpec(memory_space=pltpu.VMEM)
+ANY = pl.BlockSpec(memory_space=pl.ANY)
 PARAMS = pltpu.CompilerParams(vmem_limit_bytes=16 * 2**20)
 F32 = jnp.float32
 BF16 = jnp.bfloat16
@@ -157,7 +158,10 @@
         low = low + jnp.where(sub == 7, south, 0.0)
         new = jnp.concatenate([top, new[8 : polar - 8, :], low], axis=0)
         keep[r] = new[:, :azim]
-        send[r] = new[:, azim:]
+        side = half * polar
+        for k in range(azim // side):
+            spot = pl.ds(k * side + r * polar, polar)
+            send[spot, :] = new[:, azim + k * side : azim + (k + 1) * side]
         cells[r * polar : (r + 1) * polar, :] = new - 1.0
     total = None
     for k, place in enumerate((pa, 1 - pa)):
@@ -165,13 +169,6 @@
         term = dot3((w_high[:, at], w_low[:, at]), split(cells[:, k * azim : (k + 1) * azim]), NT)
         total = term if total is None else total + term
     spec[...] = total
-
-
-def join_kernel(keep, back, out):
-    half = keep.shape[0]
-    pa = lax.axis_index("pa")
-    out[pl.ds(pa * half, half)] = keep[...]
-    out[pl.ds((1 - pa) * half, half)] = back[...]
 
 
 def table_kernel(sizes, coef_ref, trig_ref, high_ref, low_ref, extra_ref, spread_ref, work):
@@ -287,24 +284,57 @@
                 out_ref[(g * n_ta + t) * n_pa + h] = jnp.concatenate(pieces, axis=1)
 
 
-def potential_kernel(spec, far, w_high, w_low, out):
-    rows, polar, azim = out.shape
-    half = rows // 2
+def half_field(spec, w_high, w_low, place):
+    azim = w_high.shape[1] // 2
+    at = pl.ds(pl.multiple_of(place * azim, azim), azim)
+    return dot3(split(spec), (w_high[:, at], w_low[:, at]), TN)
+
+
+def near_kernel(spec, w_high, w_low, pot, work, sem):
+    half = work.shape[0]
     pa = lax.axis_index("pa")
-    at = pl.ds(pl.multiple_of(pa * azim, azim), azim)
-    table = w_high[:, at], w_low[:, at]
-    for part, place in ((spec, pa), (far, 1 - pa)):
-        flat = dot3(split(part[...]), table, TN)
-        out[pl.ds(place * half, half)] = flat.reshape(half, polar, azim)
-
-
-def call(kernel, outs, specs, scratch=(), flops=0):
+    work[...] = half_field(spec[...], w_high, w_low, pa).reshape(work.shape)
+    copy = pltpu.make_async_copy(work, pot.at[pl.ds(pa * half, half)], sem)
+    copy.start()
+    copy.wait()
+
+
+def merge_kernel(spec, send, out):
+    size = spec.shape[0]
+    out[:size, :] = spec[...]
+    out[size:, :] = send[...]
+
+
+def far_kernel(keep, both, w_high, w_low, _, upd, pot, back, work, sems):
+    half, polar, azim = work.shape
+    size = w_high.shape[0]
+    side = half * polar
+    pa = lax.axis_index("pa")
+    mine, other = pl.ds(pa * half, half), pl.ds((1 - pa) * half, half)
+    copies = [
+        pltpu.make_async_copy(keep, upd.at[mine], sems.at[0]),
+        pltpu.make_async_copy(back, upd.at[other], sems.at[1]),
+        pltpu.make_async_copy(work, pot.at[other], sems.at[2]),
+    ]
+    copies[0].start()
+    for k in range(azim // side):
+        piece = both[size + k * side : size + (k + 1) * side, :]
+        back[:, :, k * side : (k + 1) * side] = piece.reshape(half, polar, side)
+    copies[1].start()
+    work[...] = half_field(both[:size, :], w_high, w_low, pa).reshape(work.shape)
+    copies[2].start()
+    for copy in copies:
+        copy.wait()
+
+
+def call(kernel, outs, specs, scratch=(), flops=0, place=VMEM, aliases={}):
     shapes = tuple(jax.ShapeDtypeStruct(s, d) for s, d in outs)
     return pl.pallas_call(
         kernel,
         out_shape=shapes,
         in_specs=specs,
-        out_specs=(VMEM,) * len(outs),
+        out_specs=(place,) * len(outs),
+        input_output_aliases=aliases,
         scratch_shapes=list(scratch),
         compiler_params=PARAMS,
         cost_estimate=pl.CostEstimate(flops=flops, bytes_accessed=2**20, transcendentals=0),
@@ -378,12 +408,11 @@
     )(density, far, kappa, far_kappa, *waves)
     keep, send, spec = call(
         functools.partial(stencil_kernel, sizes),
-        (((half, polar, azim), F32), ((half, polar, azim), F32), ((2 * DEGREES, cells), F32)),
+        (((half, polar, azim), F32), ((azim, cells), F32), ((2 * DEGREES, cells), F32)),
         [VMEM] * 8,
         [pltpu.VMEM((cells, azim_total), F32)],
     )(base, kappa, far_kappa, shell, even, odd, *waves)
 
-    back = swap(send)
     spread = functools.partial(
         lax.all_to_all, axis_name=AXES, split_axis=0, concat_axis=0, tiled=True
     )
@@ -396,9 +425,17 @@
         [pltpu.VMEM((rows * n_row * 2 * per, polar_total), F32)],
     )(spec, high, low, extra)
     spec = spread(spec).reshape(2 * DEGREES, cells)
-    far = swap(spec)
-    (updated,) = call(join_kernel, ((density.shape, F32),), [VMEM] * 2)(keep, back)
-    (potential,) = call(potential_kernel, ((density.shape, F32),), [VMEM] * 4)(spec, far, *waves)
+    (both,) = call(merge_kernel, (((2 * DEGREES + azim, cells), F32),), [VMEM] * 2)(spec, send)
+    far = swap(both)
+    whole = (density.shape, F32)
+    work = pltpu.VMEM((half, polar, azim), F32)
+    (potential,) = call(
+        near_kernel, (whole,), [VMEM] * 3, [work, pltpu.SemaphoreType.DMA], place=ANY
+    )(spec, *waves)
+    updated, potential = call(
+        far_kernel, (whole, whole), [VMEM] * 4 + [ANY],
+        [work, work, pltpu.SemaphoreType.DMA((3,))], place=ANY, aliases={4: 1},
+    )(keep, far, *waves, potential)
     return (updated, potential)
 
 

time: 39.2 us -> 38 us (0.969)
  blocking collectives: 0 us -> 9.97 us
  waiting for transfers between devices: 17.5 us -> 9.47 us
  starting transfers between devices: 13.9 us -> 11.3 us
  Pallas kernels: 5.84 us -> 5.32 us
    all_to_all x0 -> x1, blocking collectives: none -> 9.97 us  [shards(): spec = spread(spec).reshape(2 * DEGREES, cells)]
    all_to_all x1 -> x0, waiting for transfers between devices: 8.03 us -> none  [shards(): spec = spread(spec).reshape(2 * DEGREES, cells)]
    all_to_all x1 -> x0, starting transfers between devices: 2.58 us -> none  [shards(): spec = spread(spec).reshape(2 * DEGREES, cells)]
    pallas_call x1, Pallas kernels: 1.44 us -> 0.79 us  [shards(): call(functools.partial(solve_kernel, sizes, rows, polar), ((spec.shape, F...]
    pallas_call x2 -> x3, Pallas kernels: 1.73 us -> 1.86 us  [the longest x1 0.93 us: shards(): call(far_kernel, (whole, whole), [VMEM] * 4 + [ANY], [work, work, pltpu.S...]
    ppermute x4 -> x3, starting transfers between devices: 1.03 us -> 0.92 us  [pair_swap(): return lax.ppermute(value, axes, pairs)]
  transfers between devices with their start and end apart: 9 -> 7, of which waited for: 5 -> 4; matrix products, arithmetic and copies ran while one was open for 0% -> 0% of each run, Pallas kernels for 6% -> 7%
where the time goes in v11:
time: 38 us; the launch traced here: 37.7 us
  starting transfers between devices  11.3 us (30%)
  blocking collectives  9.97 us (26%)
  waiting for transfers between devices  9.47 us (25%)
  Pallas kernels  5.32 us (14%)
  local copies, waits for them, and re-layouts  0.97 us (3%)
  between operations  0.74 us (2%)
    all_to_all x1, blocking collectives, shards(): spec = spread(spec).reshape(2 * DEGREES, cells)  9.97 us
    all_to_all x1, waiting for transfers between devices, shards(): spec = spread(spec.reshape(owners, 2 * per, cells))  6.86 us
    all_to_all x1, starting transfers between devices, shards(): spec = spread(spec.reshape(owners, 2 * per, cells))  6.01 us
    ppermute x1, starting transfers between devices, shards(): shell = lax.ppermute(shell, AXES, halo_pairs(sizes, radial_partner, sides))  2.91 us
    ppermute x1, waiting for transfers between devices, shards(): even = lax.ppermute(even, AXES, halo_pairs(sizes, polar_partner(0), cores))  1.89 us
    ppermute x1, starting transfers between devices, shards(): odd = lax.ppermute(odd, AXES, halo_pairs(sizes, polar_partner(1), cores))  1.33 us
    pallas_call x1, Pallas kernels, shards(): call(functools.partial(table_kernel, sizes), (((per * DEGREES, polar_tota...  1.31 us
    pallas_call x1, Pallas kernels, shards(): call(functools.partial(stencil_kernel, sizes), (((half, polar, azim), F32...  1.07 us
  transfers between devices with their start and end apart: 7, of which 4 were waited for; matrix products, arithmetic and copies ran while one was open for 0% of the time, Pallas kernels for 7%

profile of v11, /device:TPU:0, one launch (start us, length us, event | category | flops | bytes accessed | tf_op | source)
XLA Modules:
  0.0 37.7 jit_solution(711686810074378174)
XLA Ops:
  0.6 0.6 %collective-permute-start = (f32[4,64,256]{2,1,0:T(8,128)}, f32[4,64,256]{2,1,0:T(8,128)S(1)}, u32[]{:S(2)}, u32[]{:S(2)}) collective-permute-start(f32[4,64,256]{2,1,0:T(8,128)} %source.2), channel_id=1, source_target_pairs={{0,1},{1,0},{2,3},{3,2},{4,5},{5,4},{6,7},{7,6},{8,9},{9,8},{10,11... | collective-permute-start | bytes 786440 | tf_op jit(solution)/shard_map/ppermute | solution.py:348
  1.2 0.1 collective-permute-start.1
  1.3 0.9 %copy-done.2 = f32[4,64,256]{2,1,0:T(8,128)S(1)} copy-done((f32[4,64,256]{2,1,0:T(8,128)S(1)}, f32[4,64,256]{2,1,0:T(8,128)}, u32[]{:S(2)}) %copy-start.2) | copy-done | bytes 262168
  2.2 0.0 copy-start.3
  2.2 0.3 collective-permute-done.far
  2.6 2.9 %collective-permute-start.2 = (f32[64,512]{1,0:T(8,128)S(1)}, f32[64,512]{1,0:T(8,128)S(1)}, u32[]{:S(2)}, u32[]{:S(2)}) collective-permute-start(f32[64,512]{1,0:T(8,128)S(1)} %get-tuple-element.11), channel_id=1, source_target_pairs={{0,2},{1,8},{2,0},{3,10},{4,6},{5,12},{6,4},{7,14},{8,1},{9,16},{1... | collective-permute-start | bytes 393224 | tf_op jit(solution)/shard_map/ppermute | solution.py:392
  5.5 0.1 collective-permute-start.3
  5.6 1.3 %collective-permute-start.4 = (f32[2,512]{1,0:T(2,128)S(1)}, f32[2,512]{1,0:T(2,128)S(1)}, u32[]{:S(2)}, u32[]{:S(2)}) collective-permute-start(f32[2,512]{1,0:T(2,128)S(1)} %get-tuple-element.13), channel_id=1, source_target_pairs={{0,1},{1,0},{2,4},{3,5},{4,2},{5,3},{6,7},{7,6},{8,9},{9,8},{10,12... | collective-permute-start | bytes 12296 | tf_op jit(solution)/shard_map/ppermute | solution.py:394
  6.9 0.0 collective-permute-done.1.far_kappa
  6.9 0.0 copy-done
  7.0 0.2 shard_map.79.base
  7.2 1.9 %collective-permute-done.3.even_in = f32[2,512]{1,0:T(2,128)S(1)} collective-permute-done((f32[2,512]{1,0:T(2,128)S(1)}, f32[2,512]{1,0:T(2,128)S(1)}, u32[]{:S(2)}, u32[]{:S(2)}) %collective-permute-start.3) | collective-permute-done | bytes 4128 | tf_op jit(solution)/shard_map/ppermute | solution.py:393
  9.1 0.0 collective-permute-done.4.odd_in
  9.1 0.0 collective-permute-done.2.shell
  9.1 1.1 %shard_map.81 = (f32[2,64,256]{2,1,0:T(8,128)S(1)}, f32[256,128]{1,0:T(8,128)S(1)}, f32[256,128]{1,0:T(8,128)}) custom-call(f32[128,512]{1,0:T(8,128)S(1)} %shard_map.79.base, f32[4,64,256]{2,1,0:T(8,128)S(1)} %shard_map.78.kappa, f32[4,64,256]{2,1,0:T(8,128)S(1)} %collective-permute-done.1.far_kappa, f32[64,512]{1,0:T(8,128)S(1)} %collective-permute-done.2.shell, ...), custom_call_target="tpu_custom_call" | custom-call | bytes 1048576 | tf_op jit(solution)/shard_map/pallas_call | solution.py:409
  10.2 6.0 %all-to-all-start = ((f32[32,8,128]{2,1,0:T(8,128)}), f32[32,8,128]{2,1,0:T(8,128)S(1)}, u32[]{:S(2)}, u32[]{:S(2)}) async-start(f32[32,8,128]{2,1,0:T(8,128)} %bitcast), calls=%async_computation | async-start | bytes 262144 | tf_op jit(solution)/shard_map/all_to_all | solution.py:419
  16.2 1.3 %shard_map.82 = (bf16[512,256]{1,0:T(8,128)(2,1)S(1)}, bf16[512,256]{1,0:T(8,128)(2,1)S(1)}, f32[2,256]{1,0:T(2,128)S(1)}) custom-call(f32[392,128]{1,0:T(8,128)S(1)} %copy-done.4, f32[4,256]{1,0:T(4,128)S(1)} %copy-done.5), custom_call_target="tpu_custom_call" | custom-call | flops 10000000 | bytes 1048576 | tf_op jit(solution)/shard_map/pallas_call | solution.py:397
  17.5 6.9 %all-to-all-done.spec_ref = f32[32,8,128]{2,1,0:T(8,128)S(1)} async-done(((f32[32,8,128]{2,1,0:T(8,128)}), f32[32,8,128]{2,1,0:T(8,128)S(1)}, u32[]{:S(2)}, u32[]{:S(2)}) %all-to-all-start) | async-done | bytes 131104 | tf_op jit(solution)/shard_map/all_to_all | solution.py:419
  24.4 0.8 %shard_map.83 = f32[32,8,128]{2,1,0:T(8,128)S(1)} custom-call(f32[32,8,128]{2,1,0:T(8,128)S(1)} %all-to-all-done.spec_ref, bf16[512,256]{1,0:T(8,128)(2,1)S(1)} %get-tuple-element.16.high_ref, bf16[512,256]{1,0:T(8,128)(2,1)S(1)} %get-tuple-element.17.low_ref, f32[2,256]{1,0:T(2,128)S(1)} %get-tuple-element.18.extra_ref), custom_call_target="tpu_custom_call" | custom-call | bytes 1048576 | tf_op jit(solution)/shard_map/pallas_call | solution.py:421
  25.2 10.0 %all_to_all.10 = f32[32,8,128]{2,1,0:T(8,128)S(1)} all-to-all(f32[32,8,128]{2,1,0:T(8,128)S(1)} %shard_map.83), channel_id=1, replica_groups=mesh['row'=4,'ta'=4,'pa'=2] {'row','ta','pa'}, dimensions={0} | all-to-all | bytes 262144 | tf_op jit(solution)/shard_map/all_to_all | solution.py:427
  35.2 0.3 collective-permute-start.5
  35.5 0.9 %shard_map.85._ = f32[4,64,256]{2,1,0:T(8,128)} custom-call(f32[256,128]{1,0:T(8,128)S(1)} %bitcast.3, bf16[256,512]{1,0:T(8,128)(2,1)S(1)} %copy-done.1, bf16[256,512]{1,0:T(8,128)(2,1)S(1)} %copy-done), custom_call_target="tpu_custom_call" | custom-call | bytes 1048576 | tf_op jit(solution)/shard_map/pallas_call | solution.py:432
  36.4 0.4 %collective-permute-done.5.both = f32[512,128]{1,0:T(8,128)S(1)} collective-permute-done((f32[512,128]{1,0:T(8,128)S(1)}, f32[512,128]{1,0:T(8,128)S(1)}, u32[]{:S(2)}, u32[]{:S(2)}) %collective-permute-start.5) | collective-permute-done | bytes 262176 | tf_op jit(solution)/shard_map/ppermute | solution.py:348
  36.8 0.9 %shard_map.86 = (f32[4,64,256]{2,1,0:T(8,128)}, f32[4,64,256]{2,1,0:T(8,128)}) custom-call(f32[2,64,256]{2,1,0:T(8,128)S(1)} %get-tuple-element.14.keep, f32[512,128]{1,0:T(8,128)S(1)} %collective-permute-done.5.both, bf16[256,512]{1,0:T(8,128)(2,1)S(1)} %copy-done.1, bf16[256,512]{1,0:T(8,128)(2,1)S(1)} %copy-done, ...), custom_call_target="tpu_custom_call", output_to_operand_aliasing={{1}: (4, {})} | custom-call | bytes 1048576 | tf_op jit(solution)/shard_map/pallas_call | solution.py:435
  (13 shorter events, 0.1 us)
Async XLA Ops:
  0.6 1.9 %collective-permute-start = (f32[4,64,256]{2,1,0:T(8,128)}, f32[4,64,256]{2,1,0:T(8,128)S(1)}, u32[]{:S(2)}, u32[]{:S(2)}) collective-permute-start(f32[4,64,256]{2,1,0:T(8,128)} %source.2), channel_id=1, source_target_pairs={{0,1},{1,0},{2,3},{3,2},{4,5},{5,4},{6,7},{7,6},{8,9},{9,8},{10,11... | collective-permute-start | bytes 786440 | tf_op jit(solution)/shard_map/ppermute | solution.py:348
  1.2 5.7 %collective-permute-start.1 = (f32[4,64,256]{2,1,0:T(8,128)}, f32[4,64,256]{2,1,0:T(8,128)S(1)}, u32[]{:S(2)}, u32[]{:S(2)}) collective-permute-start(f32[4,64,256]{2,1,0:T(8,128)} %source.3), channel_id=1, source_target_pairs={{0,1},{1,0},{2,3},{3,2},{4,5},{5,4},{6,7},{7,6},{8,9},{9,8},{10,11... | collective-permute-start | bytes 786440 | tf_op jit(solution)/shard_map/ppermute | solution.py:348
  1.3 0.9 %copy-start.2 = (f32[4,64,256]{2,1,0:T(8,128)S(1)}, f32[4,64,256]{2,1,0:T(8,128)}, u32[]{:S(2)}) copy-start(f32[4,64,256]{2,1,0:T(8,128)} %source.2) | copy-start | bytes 786436
  2.2 4.7 %copy-start.3 = (f32[4,64,256]{2,1,0:T(8,128)S(1)}, f32[4,64,256]{2,1,0:T(8,128)}, u32[]{:S(2)}) copy-start(f32[4,64,256]{2,1,0:T(8,128)} %source.3) | copy-start | bytes 786436
  2.6 6.5 %collective-permute-start.2 = (f32[64,512]{1,0:T(8,128)S(1)}, f32[64,512]{1,0:T(8,128)S(1)}, u32[]{:S(2)}, u32[]{:S(2)}) collective-permute-start(f32[64,512]{1,0:T(8,128)S(1)} %get-tuple-element.11), channel_id=1, source_target_pairs={{0,2},{1,8},{2,0},{3,10},{4,6},{5,12},{6,4},{7,14},{8,1},{9,16},{1... | collective-permute-start | bytes 393224 | tf_op jit(solution)/shard_map/ppermute | solution.py:392
  5.5 3.6 %collective-permute-start.3 = (f32[2,512]{1,0:T(2,128)S(1)}, f32[2,512]{1,0:T(2,128)S(1)}, u32[]{:S(2)}, u32[]{:S(2)}) collective-permute-start(f32[2,512]{1,0:T(2,128)S(1)} %get-tuple-element.12), channel_id=1, source_target_pairs={{0,2},{1,3},{2,0},{3,1},{4,6},{5,7},{6,4},{7,5},{8,10},{9,11},{10,... | collective-permute-start | bytes 12296 | tf_op jit(solution)/shard_map/ppermute | solution.py:393
  5.6 1.4 %copy-start = (bf16[256,512]{1,0:T(8,128)(2,1)S(1)}, bf16[256,512]{1,0:T(8,128)(2,1)}, u32[]{:S(2)}) copy-start(bf16[256,512]{1,0:T(8,128)(2,1)} %constant.11.clone.w_low) | copy-start | bytes 786436
  5.6 1.4 %copy-start.1 = (bf16[256,512]{1,0:T(8,128)(2,1)S(1)}, bf16[256,512]{1,0:T(8,128)(2,1)}, u32[]{:S(2)}) copy-start(bf16[256,512]{1,0:T(8,128)(2,1)} %constant.10.clone.w_high) | copy-start | bytes 786436
  5.6 3.5 %collective-permute-start.4 = (f32[2,512]{1,0:T(2,128)S(1)}, f32[2,512]{1,0:T(2,128)S(1)}, u32[]{:S(2)}, u32[]{:S(2)}) collective-permute-start(f32[2,512]{1,0:T(2,128)S(1)} %get-tuple-element.13), channel_id=1, source_target_pairs={{0,1},{1,0},{2,4},{3,5},{4,2},{5,3},{6,7},{7,6},{8,9},{9,8},{10,12... | collective-permute-start | bytes 12296 | tf_op jit(solution)/shard_map/ppermute | solution.py:394
  10.2 6.0 %copy-start.4 = (f32[392,128]{1,0:T(8,128)S(1)}, f32[392,128]{1,0:T(8,128)}, u32[]{:S(2)}) copy-start(f32[392,128]{1,0:T(8,128)} %constant.9.clone.coef_ref) | copy-start | bytes 602116
  10.2 6.0 %copy-start.5 = (f32[4,256]{1,0:T(4,128)S(1)}, f32[4,256]{1,0:T(4,128)}, u32[]{:S(2)}) copy-start(f32[4,256]{1,0:T(4,128)} %constant.8.clone.trig_ref) | copy-start | bytes 12292
  10.2 14.2 %all-to-all-start = ((f32[32,8,128]{2,1,0:T(8,128)}), f32[32,8,128]{2,1,0:T(8,128)S(1)}, u32[]{:S(2)}, u32[]{:S(2)}) async-start(f32[32,8,128]{2,1,0:T(8,128)} %bitcast), calls=%async_computation | async-start | bytes 262144 | tf_op jit(solution)/shard_map/all_to_all | solution.py:419
  35.2 1.6 %collective-permute-start.5 = (f32[512,128]{1,0:T(8,128)S(1)}, f32[512,128]{1,0:T(8,128)S(1)}, u32[]{:S(2)}, u32[]{:S(2)}) collective-permute-start(f32[512,128]{1,0:T(8,128)S(1)} %shard_map.84), channel_id=1, source_target_pairs={{0,1},{1,0},{2,3},{3,2},{4,5},{5,4},{6,7},{7,6},{8,9},{9,8},{10,11... | collective-permute-start | bytes 786440 | tf_op jit(solution)/shard_map/ppermute | solution.py:348
